TPU v7x, 512 devices: a whole 4x8x8 slice. The times are simulated.
512 devices in a mesh: tm: 32 (over z, x_hi, core), gz: 16 (over x_lo, y).
Axes of the slice: x: 4 (x_hi: 2, x_lo: 2; x = x_hi * 2 + x_lo), y: 8, z: 8, core: 2. Of those that a mesh axis runs over, the one named last changes fastest.
Arguments:
- c_states: float32 [32, 3, 64, 16, 256], P('tm', None, 'gz'), may hold values from -6 to 6
- velocity: float32 [3, 64, 16, 256], P(None, 'gz'), may hold values from -0.11 to 0.11
Outputs:
- updated: float32 [32, 3, 64, 16, 256], P('tm', None, 'gz')
All inputs are finite; a program needn't handle non-finite values.
Results may differ from a plain program's by a relative error of at most 0.00002.
Values sent between devices are 32-bit elements; how exact they have to be, the bound alone decides.
No kernel may reach another device: no remote copies, remote signals or barrier semaphores. Data moves between devices by JAX's collectives and lax.ppermute only.
A program may use at most 64 MiB of HBM per device.

v0:
```python
import jax
import jax.numpy as jnp
from jax import lax
from jax.sharding import PartitionSpec as P

STEPS = 4


KAPPA = 0.04


def extended_2(cells, sides, width):
    for axis, dim in sides:
        count = lax.axis_size(axis)
        ends = count - 1
        head = lax.slice_in_dim(cells, 0, width, axis=dim)
        tail = lax.slice_in_dim(cells, cells.shape[dim] - width, cells.shape[dim], axis=dim)
        cells = jnp.concatenate(
            [
                lax.ppermute(tail, axis, [(i, (i + 1) % count) for i in range(ends)]),
                cells,
                lax.ppermute(head, axis, [((i + 1) % count, i) for i in range(ends)]),
            ],
            axis=dim,
        )
    return cells


def from_behind(block, axis, distance):
    devices = range(lax.axis_size(axis))
    route = [(i - distance, i) for i in devices if i - distance in devices]
    return lax.ppermute(block, axis, route)


def neighbours(padded, direction):
    lower_cut = [slice(None), slice(1, -1), slice(1, -1), slice(1, -1)]
    upper_cut = list(lower_cut)
    lower_cut[direction] = slice(0, -2)
    upper_cut[direction] = slice(2, None)
    return (padded[tuple(lower_cut)], padded[tuple(upper_cut)])


def pad_plane(values):
    return jnp.pad(values, ((0, 0), (0, 0), (1, 1), (1, 1)))


def pad_depth(values):
    return jnp.pad(values, ((0, 0), (1, 1), (0, 0), (0, 0)))


def tensor_ext(extended):
    padded = pad_plane(extended)
    columns = []
    for direction in (1, 2, 3):
        lower_side, upper_side = neighbours(padded, direction)
        columns.append((upper_side - lower_side) * 0.5)
    return jnp.stack(columns, axis=1)


def march_ext(extended, courant, tensor):
    padded = pad_plane(extended)
    middle = padded[:, 1:-1, 1:-1, 1:-1]
    advection = jnp.zeros_like(middle)
    laplace = jnp.zeros_like(middle)
    for direction in (1, 2, 3):
        lower_side, upper_side = neighbours(padded, direction)
        speed = courant[direction - 1][None]
        advection = (
            advection
            + jnp.maximum(speed, 0.0) * (middle - lower_side)
            + jnp.minimum(speed, 0.0) * (upper_side - middle)
        )
        laplace = laplace + upper_side + lower_side - 2.0 * middle
    stretch = tensor[:, 0] * middle[0:1] + tensor[:, 1] * middle[1:2] + tensor[:, 2] * middle[2:3]
    return middle - advection + stretch + KAPPA * laplace


def coarsen(values):
    comps, zlen, xlen, ylen = values.shape
    return values.reshape(comps, zlen // 2, 2, xlen // 2, 2, ylen // 2, 2).mean(axis=(2, 4, 6))


def refine(values):
    return jnp.repeat(jnp.repeat(jnp.repeat(values, 2, 1), 2, 2), 2, 3)


def z_rims(values):
    return extended_2(values, (("gz", 1),), 1)


def local(c_states, velocity):
    start_state = c_states[0]
    slab_depth = start_state.shape[1]
    slab_index = lax.axis_index("gz")
    total_depth = slab_depth * lax.axis_size("gz")
    at_anchor = lax.axis_index("tm") == 0
    reach = STEPS - 1
    velocity_wide = extended_2(velocity, (("gz", 1),), STEPS)
    tensor_wide = tensor_ext(velocity_wide)
    courant_wide = velocity_wide[:, 1:-1]
    tensor = tensor_wide[:, :, reach : reach + slab_depth]
    depth_index = (
        lax.broadcasted_iota(jnp.int32, (1, slab_depth + 2 * reach, 1, 1), 1)
        + slab_index * slab_depth
        - reach
    )
    inside = jnp.logical_and(depth_index >= 0, depth_index < total_depth).astype(jnp.float32)

    def single_step(current):
        return march_ext(z_rims(current), velocity, tensor)

    def relax_steps(current):
        extended = extended_2(current, (("gz", 1),), reach)
        for _ in range(reach):
            extended = march_ext(pad_depth(extended), courant_wide, tensor_wide) * inside
        return extended[:, reach : reach + slab_depth]

    forward = single_step(relax_steps(start_state))
    incoming = from_behind(forward, "tm", 1)
    relaxed = jnp.where(at_anchor, start_state, incoming)
    again = single_step(relax_steps(relaxed))
    coarse_speed = 2.0 * coarsen(velocity)
    speed_ext = extended_2(coarse_speed, (("gz", 1),), 1)
    coarse_tensor = tensor_ext(speed_ext)
    coarse_relaxed = coarsen(relaxed)
    relaxed_ext = extended_2(coarse_relaxed, (("gz", 1),), 1)
    coarse_image = march_ext(relaxed_ext, coarse_speed, coarse_tensor)
    forcing = from_behind(coarsen(again) - coarse_image, "tm", 1)

    def sweep_turn(counter, state):
        received = from_behind(state, "tm", 1)
        extended = extended_2(received, (("gz", 1),), 1)
        following = march_ext(extended, coarse_speed, coarse_tensor) + forcing
        return jnp.where(at_anchor, coarse_relaxed, following)

    own_state = lax.fori_loop(0, lax.axis_size("tm") - 1, sweep_turn, coarse_relaxed)
    updated = relaxed + refine(own_state - coarse_relaxed)
    return updated[None]


def solution(mesh):
    return jax.shard_map(
        local,
        mesh=mesh,
        in_specs=(P("tm", None, "gz", None, None), P(None, "gz", None, None)),
        out_specs=P("tm", None, "gz", None, None),
        check_vma=False,
    )
```

profile of v0, /device:TPU:258, one launch (start us, length us, event | category | flops | bytes accessed | tf_op | source)
XLA Modules:
  0.0 752.1 jit_solution(3417969042193871571)
XLA Ops:
  0.0 5.3 collective-permute-start.6
  11.9 6.0 collective-permute-start.4
  21.0 14.0 %reshape.76 = f32[3,2,2,8,2,128,2]{6,5,4,3,2,1,0:T(8,128)} reshape(f32[3,4,16,256]{3,2,1,0:T(8,128)S(1)} %copy-done.14) | data formatting | bytes 393216 | tf_op jit(solution)/shard_map/reshape | solution.py:80
  35.0 5.5 reduce_sum.28
  48.1 6.0 collective-permute-start.8
  58.5 6.4 collective-permute-start.10
  66.9 5.8 collective-permute-done.11
  86.3 3.9 collective-permute-start.12
  90.2 14.8 %reshape.75 = f32[3,2,2,8,2,128,2]{6,5,4,3,2,1,0:T(8,128)} reshape(f32[3,4,16,256]{3,2,1,0:T(8,128)} %copy.36) | data formatting | bytes 393216 | tf_op jit(solution)/shard_map/reshape | solution.py:80
  105.0 6.1 reduce_sum.27
  113.8 6.2 collective-permute-start.17
  129.4 6.1 collective-permute-start.15
  139.0 14.0 %reshape.77 = f32[3,2,2,8,2,128,2]{6,5,4,3,2,1,0:T(8,128)} reshape(f32[3,4,16,256]{3,2,1,0:T(8,128)S(1)} %fusion.37) | data formatting | bytes 393216 | tf_op jit(solution)/shard_map/reshape | solution.py:80
  153.2 5.7 reduce_sum.29
  161.3 6.7 collective-permute-done.18
  168.0 581.9 %while.12 = (s32[]{:T(128)}, f32[3,2,8,128]{3,2,1,0:T(8,128)S(1)}, pred[]{:T(512)}, f32[3,2,8,128]{3,2,1,0:T(8,128)S(1)}, f32[3,2,8,128]{3,2,1,0:T(8,128)S(1)}, ...) while((s32[]{:T(128)}, f32[3,2,8,128]{3,2,1,0:T(8,128)S(1)}, ...), condition=%wide.region_4.5_spmd, body=%wide.region_3.4_spmd.sunk | while | flops 485906 | bytes 849054 | solution.py:136
  169.9 6.8 collective-permute-done
  176.7 6.3 collective-permute-start.1
  185.0 5.7 collective-permute-done.2
  193.0 6.8 collective-permute-done
  201.7 3.9 collective-permute-start.2
  211.6 6.8 collective-permute-done
  220.3 3.9 collective-permute-start.2
  230.2 6.8 collective-permute-done
  239.0 3.9 collective-permute-start.2
  248.9 6.8 collective-permute-done
  257.6 3.9 collective-permute-start.2
  267.5 6.8 collective-permute-done
  276.2 3.9 collective-permute-start.2
  286.1 6.8 collective-permute-done
  294.9 3.9 collective-permute-start.2
  304.8 6.8 collective-permute-done
  313.5 3.9 collective-permute-start.2
  323.4 6.8 collective-permute-done
  332.1 3.9 collective-permute-start.2
  342.0 6.8 collective-permute-done
  350.7 3.9 collective-permute-start.2
  360.6 6.8 collective-permute-done
  369.4 3.9 collective-permute-start.2
  379.3 6.8 collective-permute-done
  397.9 6.8 collective-permute-done
  416.5 6.8 collective-permute-done
  435.1 6.8 collective-permute-done
  453.8 6.8 collective-permute-done
  472.4 6.8 collective-permute-done
  491.0 6.8 collective-permute-done
  499.8 3.9 collective-permute-start.2
  509.7 6.8 collective-permute-done
  518.4 3.9 collective-permute-start.2
  528.3 6.8 collective-permute-done
  537.0 3.9 collective-permute-start.2
  546.9 6.8 collective-permute-done
  555.7 3.9 collective-permute-start.2
  565.5 6.8 collective-permute-done
  574.3 3.9 collective-permute-start.2
  584.2 6.8 collective-permute-done
  602.8 6.8 collective-permute-done
  621.4 6.8 collective-permute-done
  640.1 6.8 collective-permute-done
  658.7 6.8 collective-permute-done
  677.3 6.8 collective-permute-done
  695.9 6.8 collective-permute-done
  714.6 6.8 collective-permute-done
  733.2 6.8 collective-permute-done
  (484 shorter events, 353.7 us)
Async XLA Ops:
  0.0 41.9 %collective-permute-start.6 = (f32[3,4,16,256]{3,2,1,0:T(8,128)}, f32[3,4,16,256]{3,2,1,0:T(8,128)S(1)}, u32[]{:S(2)}, u32[]{:S(2)}) collective-permute-start(f32[3,4,16,256]{3,2,1,0:T(8,128)} %param.5), channel_id=1, source_target_pairs={{1,0},{2,1},{3,2},{4,3},{5,4},{6,5},{7,6},{8,7},{9,8},{10,9},{11,1... | collective-permute-start | bytes 589832 | tf_op jit(solution)/shard_map/ppermute | solution.py:22
  5.3 36.0 %collective-permute-start.5 = (f32[3,4,16,256]{3,2,1,0:T(8,128)}, f32[3,4,16,256]{3,2,1,0:T(8,128)S(1)}, u32[]{:S(2)}, u32[]{:S(2)}) collective-permute-start(f32[3,4,16,256]{3,2,1,0:T(8,128)} %param.5), channel_id=1, source_target_pairs={{0,1},{1,2},{2,3},{3,4},{4,5},{5,6},{6,7},{7,8},{8,9},{9,10},{10,1... | collective-permute-start | bytes 589832 | tf_op jit(solution)/shard_map/ppermute | solution.py:20
  11.9 29.3 %collective-permute-start.4 = (f32[3,3,16,256]{3,2,1,0:T(8,128)S(1)}, f32[3,3,16,256]{3,2,1,0:T(8,128)S(1)}, u32[]{:S(2)}, u32[]{:S(2)}) collective-permute-start(f32[3,3,16,256]{3,2,1,0:T(8,128)S(1)} %copy.33), channel_id=1, source_target_pairs={{1,0},{2,1},{3,2},{4,3},{5,4},{6,5},{7,6},{8,7},{9,8},{10,9},{11,1... | collective-permute-start | bytes 442376 | tf_op jit(solution)/shard_map/ppermute | solution.py:22
  18.2 22.9 %collective-permute-start.3 = (f32[3,3,16,256]{3,2,1,0:T(8,128)S(1)}, f32[3,3,16,256]{3,2,1,0:T(8,128)S(1)}, u32[]{:S(2)}, u32[]{:S(2)}) collective-permute-start(f32[3,3,16,256]{3,2,1,0:T(8,128)S(1)} %copy.32), channel_id=1, source_target_pairs={{0,1},{1,2},{2,3},{3,4},{4,5},{5,6},{6,7},{7,8},{8,9},{9,10},{10,1... | collective-permute-start | bytes 442376 | tf_op jit(solution)/shard_map/ppermute | solution.py:20
  46.1 8.2 %collective-permute-start.7 = (f32[3,1,16,256]{3,2,1,0:T(8,128)S(1)}, f32[3,1,16,256]{3,2,1,0:T(8,128)S(1)}, u32[]{:S(2)}, u32[]{:S(2)}) collective-permute-start(f32[3,1,16,256]{3,2,1,0:T(8,128)S(1)} %get-tuple-element.185), channel_id=1, source_target_pairs={{0,1},{1,2},{2,3},{3,4},{4,5},{5,6},{6,7},{7,8},{8,9},{9,10},{10,1... | collective-permute-start | bytes 147464 | tf_op jit(solution)/shard_map/ppermute | solution.py:20
  48.1 7.8 %collective-permute-start.8 = (f32[3,1,16,256]{3,2,1,0:T(8,128)S(1)}, f32[3,1,16,256]{3,2,1,0:T(8,128)S(1)}, u32[]{:S(2)}, u32[]{:S(2)}) collective-permute-start(f32[3,1,16,256]{3,2,1,0:T(8,128)S(1)} %get-tuple-element.186), channel_id=1, source_target_pairs={{1,0},{2,1},{3,2},{4,3},{5,4},{6,5},{7,6},{8,7},{9,8},{10,9},{11,1... | collective-permute-start | bytes 147464 | tf_op jit(solution)/shard_map/ppermute | solution.py:22
  56.6 16.8 %collective-permute-start.9 = (f32[3,4,16,256]{3,2,1,0:T(8,128)S(1)}, f32[3,4,16,256]{3,2,1,0:T(8,128)S(1)}, u32[]{:S(2)}, u32[]{:S(2)}) collective-permute-start(f32[3,4,16,256]{3,2,1,0:T(8,128)S(1)} %fusion.57), channel_id=1, source_target_pairs={{0,16},{16,32},{32,48},{48,64},{64,80},{80,96},{96,112},{112,128},... | collective-permute-start | bytes 589832 | tf_op jit(solution)/shard_map/ppermute | solution.py:32
  58.5 8.3 %collective-permute-start.10 = (f32[3,1,8,128]{3,2,1,0:T(8,128)S(1)}, f32[3,1,8,128]{3,2,1,0:T(8,128)S(1)}, u32[]{:S(2)}, u32[]{:S(2)}) collective-permute-start(f32[3,1,8,128]{3,2,1,0:T(8,128)S(1)} %get-tuple-element.215), channel_id=1, source_target_pairs={{1,0},{2,1},{3,2},{4,3},{5,4},{6,5},{7,6},{8,7},{9,8},{10,9},{11,1... | collective-permute-start | bytes 36872 | tf_op jit(solution)/shard_map/ppermute | solution.py:22
  64.9 7.7 %collective-permute-start.11 = (f32[3,1,8,128]{3,2,1,0:T(8,128)S(1)}, f32[3,1,8,128]{3,2,1,0:T(8,128)S(1)}, u32[]{:S(2)}, u32[]{:S(2)}) collective-permute-start(f32[3,1,8,128]{3,2,1,0:T(8,128)S(1)} %get-tuple-element.216), channel_id=1, source_target_pairs={{0,1},{1,2},{2,3},{3,4},{4,5},{5,6},{6,7},{7,8},{8,9},{9,10},{10,1... | collective-permute-start | bytes 36872 | tf_op jit(solution)/shard_map/ppermute | solution.py:20
  84.4 37.8 %collective-permute-start.13 = (f32[3,3,16,256]{3,2,1,0:T(8,128)}, f32[3,3,16,256]{3,2,1,0:T(8,128)}, u32[]{:S(2)}, u32[]{:S(2)}) collective-permute-start(f32[3,3,16,256]{3,2,1,0:T(8,128)} %copy.38), channel_id=1, source_target_pairs={{1,0},{2,1},{3,2},{4,3},{5,4},{6,5},{7,6},{8,7},{9,8},{10,9},{11,1... | collective-permute-start | bytes 442376 | tf_op jit(solution)/shard_map/ppermute | solution.py:22
  86.3 36.0 %collective-permute-start.12 = (f32[3,3,16,256]{3,2,1,0:T(8,128)}, f32[3,3,16,256]{3,2,1,0:T(8,128)}, u32[]{:S(2)}, u32[]{:S(2)}) collective-permute-start(f32[3,3,16,256]{3,2,1,0:T(8,128)} %copy.37), channel_id=1, source_target_pairs={{0,1},{1,2},{2,3},{3,4},{4,5},{5,6},{6,7},{7,8},{8,9},{9,10},{10,1... | collective-permute-start | bytes 442376 | tf_op jit(solution)/shard_map/ppermute | solution.py:20
  111.9 9.5 %collective-permute-start.16 = (f32[3,1,8,128]{3,2,1,0:T(8,128)S(1)}, f32[3,1,8,128]{3,2,1,0:T(8,128)S(1)}, u32[]{:S(2)}, u32[]{:S(2)}) collective-permute-start(f32[3,1,8,128]{3,2,1,0:T(8,128)S(1)} %get-tuple-element.213), channel_id=1, source_target_pairs={{0,1},{1,2},{2,3},{3,4},{4,5},{5,6},{6,7},{7,8},{8,9},{9,10},{10,1... | collective-permute-start | bytes 36872 | tf_op jit(solution)/shard_map/ppermute | solution.py:20
  127.3 8.3 %collective-permute-start.14 = (f32[3,1,16,256]{3,2,1,0:T(8,128)S(1)}, f32[3,1,16,256]{3,2,1,0:T(8,128)S(1)}, u32[]{:S(2)}, u32[]{:S(2)}) collective-permute-start(f32[3,1,16,256]{3,2,1,0:T(8,128)S(1)} %get-tuple-element.171), channel_id=1, source_target_pairs={{0,1},{1,2},{2,3},{3,4},{4,5},{5,6},{6,7},{7,8},{8,9},{9,10},{10,1... | collective-permute-start | bytes 147464 | tf_op jit(solution)/shard_map/ppermute | solution.py:20
  129.4 7.8 %collective-permute-start.15 = (f32[3,1,16,256]{3,2,1,0:T(8,128)S(1)}, f32[3,1,16,256]{3,2,1,0:T(8,128)S(1)}, u32[]{:S(2)}, u32[]{:S(2)}) collective-permute-start(f32[3,1,16,256]{3,2,1,0:T(8,128)S(1)} %get-tuple-element.172), channel_id=1, source_target_pairs={{1,0},{2,1},{3,2},{4,3},{5,4},{6,5},{7,6},{8,7},{9,8},{10,9},{11,1... | collective-permute-start | bytes 147464 | tf_op jit(solution)/shard_map/ppermute | solution.py:22
  159.2 8.8 %collective-permute-start.18 = (f32[3,2,8,128]{3,2,1,0:T(8,128)S(1)}, f32[3,2,8,128]{3,2,1,0:T(8,128)S(1)}, u32[]{:S(2)}, u32[]{:S(2)}) collective-permute-start(f32[3,2,8,128]{3,2,1,0:T(8,128)S(1)} %fusion.102), channel_id=1, source_target_pairs={{0,16},{16,32},{32,48},{48,64},{64,80},{80,96},{96,112},{112,128},... | collective-permute-start | bytes 73736 | tf_op jit(solution)/shard_map/ppermute | solution.py:32
  168.0 8.7 %collective-permute-start = (f32[3,2,8,128]{3,2,1,0:T(8,128)S(1)}, f32[3,2,8,128]{3,2,1,0:T(8,128)S(1)}, u32[]{:S(2)}, u32[]{:S(2)}) collective-permute-start(f32[3,2,8,128]{3,2,1,0:T(8,128)S(1)} %get-tuple-element.312), channel_id=1, source_target_pairs={{0,16},{16,32},{32,48},{48,64},{64,80},{80,96},{96,112},{112,128},... | collective-permute-start | bytes 73736 | tf_op jit(solution)/shard_map/while/body/eval_jaxpr/ppermute | solution.py:32
  176.7 8.3 %collective-permute-start.1 = (f32[3,1,8,128]{3,2,1,0:T(8,128)S(1)}, f32[3,1,8,128]{3,2,1,0:T(8,128)S(1)}, u32[]{:S(2)}, u32[]{:S(2)}) collective-permute-start(f32[3,1,8,128]{3,2,1,0:T(8,128)S(1)} %get-tuple-element.290), channel_id=1, source_target_pairs={{1,0},{2,1},{3,2},{4,3},{5,4},{6,5},{7,6},{8,7},{9,8},{10,9},{11,1... | collective-permute-start | bytes 36872 | tf_op jit(solution)/shard_map/while/body/eval_jaxpr/ppermute | solution.py:22
  183.1 7.7 %collective-permute-start.2 = (f32[3,1,8,128]{3,2,1,0:T(8,128)S(1)}, f32[3,1,8,128]{3,2,1,0:T(8,128)S(1)}, u32[]{:S(2)}, u32[]{:S(2)}) collective-permute-start(f32[3,1,8,128]{3,2,1,0:T(8,128)S(1)} %get-tuple-element.291), channel_id=1, source_target_pairs={{0,1},{1,2},{2,3},{3,4},{4,5},{5,6},{6,7},{7,8},{8,9},{9,10},{10,1... | collective-permute-start | bytes 36872 | tf_op jit(solution)/shard_map/while/body/eval_jaxpr/ppermute | solution.py:20
  191.0 8.8 %collective-permute-start = (f32[3,2,8,128]{3,2,1,0:T(8,128)S(1)}, f32[3,2,8,128]{3,2,1,0:T(8,128)S(1)}, u32[]{:S(2)}, u32[]{:S(2)}) collective-permute-start(f32[3,2,8,128]{3,2,1,0:T(8,128)S(1)} %get-tuple-element.312), channel_id=1, source_target_pairs={{0,16},{16,32},{32,48},{48,64},{64,80},{80,96},{96,112},{112,128},... | collective-permute-start | bytes 73736 | tf_op jit(solution)/shard_map/while/body/eval_jaxpr/ppermute | solution.py:32
  201.7 7.7 %collective-permute-start.2 = (f32[3,1,8,128]{3,2,1,0:T(8,128)S(1)}, f32[3,1,8,128]{3,2,1,0:T(8,128)S(1)}, u32[]{:S(2)}, u32[]{:S(2)}) collective-permute-start(f32[3,1,8,128]{3,2,1,0:T(8,128)S(1)} %get-tuple-element.291), channel_id=1, source_target_pairs={{0,1},{1,2},{2,3},{3,4},{4,5},{5,6},{6,7},{7,8},{8,9},{9,10},{10,1... | collective-permute-start | bytes 36872 | tf_op jit(solution)/shard_map/while/body/eval_jaxpr/ppermute | solution.py:20
  209.7 8.8 %collective-permute-start = (f32[3,2,8,128]{3,2,1,0:T(8,128)S(1)}, f32[3,2,8,128]{3,2,1,0:T(8,128)S(1)}, u32[]{:S(2)}, u32[]{:S(2)}) collective-permute-start(f32[3,2,8,128]{3,2,1,0:T(8,128)S(1)} %get-tuple-element.312), channel_id=1, source_target_pairs={{0,16},{16,32},{32,48},{48,64},{64,80},{80,96},{96,112},{112,128},... | collective-permute-start | bytes 73736 | tf_op jit(solution)/shard_map/while/body/eval_jaxpr/ppermute | solution.py:32
  220.3 7.7 %collective-permute-start.2 = (f32[3,1,8,128]{3,2,1,0:T(8,128)S(1)}, f32[3,1,8,128]{3,2,1,0:T(8,128)S(1)}, u32[]{:S(2)}, u32[]{:S(2)}) collective-permute-start(f32[3,1,8,128]{3,2,1,0:T(8,128)S(1)} %get-tuple-element.291), channel_id=1, source_target_pairs={{0,1},{1,2},{2,3},{3,4},{4,5},{5,6},{6,7},{7,8},{8,9},{9,10},{10,1... | collective-permute-start | bytes 36872 | tf_op jit(solution)/shard_map/while/body/eval_jaxpr/ppermute | solution.py:20
  228.3 8.8 %collective-permute-start = (f32[3,2,8,128]{3,2,1,0:T(8,128)S(1)}, f32[3,2,8,128]{3,2,1,0:T(8,128)S(1)}, u32[]{:S(2)}, u32[]{:S(2)}) collective-permute-start(f32[3,2,8,128]{3,2,1,0:T(8,128)S(1)} %get-tuple-element.312), channel_id=1, source_target_pairs={{0,16},{16,32},{32,48},{48,64},{64,80},{80,96},{96,112},{112,128},... | collective-permute-start | bytes 73736 | tf_op jit(solution)/shard_map/while/body/eval_jaxpr/ppermute | solution.py:32
  239.0 7.7 %collective-permute-start.2 = (f32[3,1,8,128]{3,2,1,0:T(8,128)S(1)}, f32[3,1,8,128]{3,2,1,0:T(8,128)S(1)}, u32[]{:S(2)}, u32[]{:S(2)}) collective-permute-start(f32[3,1,8,128]{3,2,1,0:T(8,128)S(1)} %get-tuple-element.291), channel_id=1, source_target_pairs={{0,1},{1,2},{2,3},{3,4},{4,5},{5,6},{6,7},{7,8},{8,9},{9,10},{10,1... | collective-permute-start | bytes 36872 | tf_op jit(solution)/shard_map/while/body/eval_jaxpr/ppermute | solution.py:20
  246.9 8.8 %collective-permute-start = (f32[3,2,8,128]{3,2,1,0:T(8,128)S(1)}, f32[3,2,8,128]{3,2,1,0:T(8,128)S(1)}, u32[]{:S(2)}, u32[]{:S(2)}) collective-permute-start(f32[3,2,8,128]{3,2,1,0:T(8,128)S(1)} %get-tuple-element.312), channel_id=1, source_target_pairs={{0,16},{16,32},{32,48},{48,64},{64,80},{80,96},{96,112},{112,128},... | collective-permute-start | bytes 73736 | tf_op jit(solution)/shard_map/while/body/eval_jaxpr/ppermute | solution.py:32
  257.6 7.7 %collective-permute-start.2 = (f32[3,1,8,128]{3,2,1,0:T(8,128)S(1)}, f32[3,1,8,128]{3,2,1,0:T(8,128)S(1)}, u32[]{:S(2)}, u32[]{:S(2)}) collective-permute-start(f32[3,1,8,128]{3,2,1,0:T(8,128)S(1)} %get-tuple-element.291), channel_id=1, source_target_pairs={{0,1},{1,2},{2,3},{3,4},{4,5},{5,6},{6,7},{7,8},{8,9},{9,10},{10,1... | collective-permute-start | bytes 36872 | tf_op jit(solution)/shard_map/while/body/eval_jaxpr/ppermute | solution.py:20
  265.6 8.8 %collective-permute-start = (f32[3,2,8,128]{3,2,1,0:T(8,128)S(1)}, f32[3,2,8,128]{3,2,1,0:T(8,128)S(1)}, u32[]{:S(2)}, u32[]{:S(2)}) collective-permute-start(f32[3,2,8,128]{3,2,1,0:T(8,128)S(1)} %get-tuple-element.312), channel_id=1, source_target_pairs={{0,16},{16,32},{32,48},{48,64},{64,80},{80,96},{96,112},{112,128},... | collective-permute-start | bytes 73736 | tf_op jit(solution)/shard_map/while/body/eval_jaxpr/ppermute | solution.py:32
  276.2 7.7 %collective-permute-start.2 = (f32[3,1,8,128]{3,2,1,0:T(8,128)S(1)}, f32[3,1,8,128]{3,2,1,0:T(8,128)S(1)}, u32[]{:S(2)}, u32[]{:S(2)}) collective-permute-start(f32[3,1,8,128]{3,2,1,0:T(8,128)S(1)} %get-tuple-element.291), channel_id=1, source_target_pairs={{0,1},{1,2},{2,3},{3,4},{4,5},{5,6},{6,7},{7,8},{8,9},{9,10},{10,1... | collective-permute-start | bytes 36872 | tf_op jit(solution)/shard_map/while/body/eval_jaxpr/ppermute | solution.py:20
  284.2 8.8 %collective-permute-start = (f32[3,2,8,128]{3,2,1,0:T(8,128)S(1)}, f32[3,2,8,128]{3,2,1,0:T(8,128)S(1)}, u32[]{:S(2)}, u32[]{:S(2)}) collective-permute-start(f32[3,2,8,128]{3,2,1,0:T(8,128)S(1)} %get-tuple-element.312), channel_id=1, source_target_pairs={{0,16},{16,32},{32,48},{48,64},{64,80},{80,96},{96,112},{112,128},... | collective-permute-start | bytes 73736 | tf_op jit(solution)/shard_map/while/body/eval_jaxpr/ppermute | solution.py:32
  294.9 7.7 %collective-permute-start.2 = (f32[3,1,8,128]{3,2,1,0:T(8,128)S(1)}, f32[3,1,8,128]{3,2,1,0:T(8,128)S(1)}, u32[]{:S(2)}, u32[]{:S(2)}) collective-permute-start(f32[3,1,8,128]{3,2,1,0:T(8,128)S(1)} %get-tuple-element.291), channel_id=1, source_target_pairs={{0,1},{1,2},{2,3},{3,4},{4,5},{5,6},{6,7},{7,8},{8,9},{9,10},{10,1... | collective-permute-start | bytes 36872 | tf_op jit(solution)/shard_map/while/body/eval_jaxpr/ppermute | solution.py:20
  302.8 8.8 %collective-permute-start = (f32[3,2,8,128]{3,2,1,0:T(8,128)S(1)}, f32[3,2,8,128]{3,2,1,0:T(8,128)S(1)}, u32[]{:S(2)}, u32[]{:S(2)}) collective-permute-start(f32[3,2,8,128]{3,2,1,0:T(8,128)S(1)} %get-tuple-element.312), channel_id=1, source_target_pairs={{0,16},{16,32},{32,48},{48,64},{64,80},{80,96},{96,112},{112,128},... | collective-permute-start | bytes 73736 | tf_op jit(solution)/shard_map/while/body/eval_jaxpr/ppermute | solution.py:32
  313.5 7.7 %collective-permute-start.2 = (f32[3,1,8,128]{3,2,1,0:T(8,128)S(1)}, f32[3,1,8,128]{3,2,1,0:T(8,128)S(1)}, u32[]{:S(2)}, u32[]{:S(2)}) collective-permute-start(f32[3,1,8,128]{3,2,1,0:T(8,128)S(1)} %get-tuple-element.291), channel_id=1, source_target_pairs={{0,1},{1,2},{2,3},{3,4},{4,5},{5,6},{6,7},{7,8},{8,9},{9,10},{10,1... | collective-permute-start | bytes 36872 | tf_op jit(solution)/shard_map/while/body/eval_jaxpr/ppermute | solution.py:20
  321.4 8.8 %collective-permute-start = (f32[3,2,8,128]{3,2,1,0:T(8,128)S(1)}, f32[3,2,8,128]{3,2,1,0:T(8,128)S(1)}, u32[]{:S(2)}, u32[]{:S(2)}) collective-permute-start(f32[3,2,8,128]{3,2,1,0:T(8,128)S(1)} %get-tuple-element.312), channel_id=1, source_target_pairs={{0,16},{16,32},{32,48},{48,64},{64,80},{80,96},{96,112},{112,128},... | collective-permute-start | bytes 73736 | tf_op jit(solution)/shard_map/while/body/eval_jaxpr/ppermute | solution.py:32
  332.1 7.7 %collective-permute-start.2 = (f32[3,1,8,128]{3,2,1,0:T(8,128)S(1)}, f32[3,1,8,128]{3,2,1,0:T(8,128)S(1)}, u32[]{:S(2)}, u32[]{:S(2)}) collective-permute-start(f32[3,1,8,128]{3,2,1,0:T(8,128)S(1)} %get-tuple-element.291), channel_id=1, source_target_pairs={{0,1},{1,2},{2,3},{3,4},{4,5},{5,6},{6,7},{7,8},{8,9},{9,10},{10,1... | collective-permute-start | bytes 36872 | tf_op jit(solution)/shard_map/while/body/eval_jaxpr/ppermute | solution.py:20
  340.1 8.8 %collective-permute-start = (f32[3,2,8,128]{3,2,1,0:T(8,128)S(1)}, f32[3,2,8,128]{3,2,1,0:T(8,128)S(1)}, u32[]{:S(2)}, u32[]{:S(2)}) collective-permute-start(f32[3,2,8,128]{3,2,1,0:T(8,128)S(1)} %get-tuple-element.312), channel_id=1, source_target_pairs={{0,16},{16,32},{32,48},{48,64},{64,80},{80,96},{96,112},{112,128},... | collective-permute-start | bytes 73736 | tf_op jit(solution)/shard_map/while/body/eval_jaxpr/ppermute | solution.py:32
  350.7 7.7 %collective-permute-start.2 = (f32[3,1,8,128]{3,2,1,0:T(8,128)S(1)}, f32[3,1,8,128]{3,2,1,0:T(8,128)S(1)}, u32[]{:S(2)}, u32[]{:S(2)}) collective-permute-start(f32[3,1,8,128]{3,2,1,0:T(8,128)S(1)} %get-tuple-element.291), channel_id=1, source_target_pairs={{0,1},{1,2},{2,3},{3,4},{4,5},{5,6},{6,7},{7,8},{8,9},{9,10},{10,1... | collective-permute-start | bytes 36872 | tf_op jit(solution)/shard_map/while/body/eval_jaxpr/ppermute | solution.py:20
  358.7 8.8 %collective-permute-start = (f32[3,2,8,128]{3,2,1,0:T(8,128)S(1)}, f32[3,2,8,128]{3,2,1,0:T(8,128)S(1)}, u32[]{:S(2)}, u32[]{:S(2)}) collective-permute-start(f32[3,2,8,128]{3,2,1,0:T(8,128)S(1)} %get-tuple-element.312), channel_id=1, source_target_pairs={{0,16},{16,32},{32,48},{48,64},{64,80},{80,96},{96,112},{112,128},... | collective-permute-start | bytes 73736 | tf_op jit(solution)/shard_map/while/body/eval_jaxpr/ppermute | solution.py:32
  369.4 7.7 %collective-permute-start.2 = (f32[3,1,8,128]{3,2,1,0:T(8,128)S(1)}, f32[3,1,8,128]{3,2,1,0:T(8,128)S(1)}, u32[]{:S(2)}, u32[]{:S(2)}) collective-permute-start(f32[3,1,8,128]{3,2,1,0:T(8,128)S(1)} %get-tuple-element.291), channel_id=1, source_target_pairs={{0,1},{1,2},{2,3},{3,4},{4,5},{5,6},{6,7},{7,8},{8,9},{9,10},{10,1... | collective-permute-start | bytes 36872 | tf_op jit(solution)/shard_map/while/body/eval_jaxpr/ppermute | solution.py:20
  377.3 8.8 %collective-permute-start = (f32[3,2,8,128]{3,2,1,0:T(8,128)S(1)}, f32[3,2,8,128]{3,2,1,0:T(8,128)S(1)}, u32[]{:S(2)}, u32[]{:S(2)}) collective-permute-start(f32[3,2,8,128]{3,2,1,0:T(8,128)S(1)} %get-tuple-element.312), channel_id=1, source_target_pairs={{0,16},{16,32},{32,48},{48,64},{64,80},{80,96},{96,112},{112,128},... | collective-permute-start | bytes 73736 | tf_op jit(solution)/shard_map/while/body/eval_jaxpr/ppermute | solution.py:32
  388.0 7.7 %collective-permute-start.2 = (f32[3,1,8,128]{3,2,1,0:T(8,128)S(1)}, f32[3,1,8,128]{3,2,1,0:T(8,128)S(1)}, u32[]{:S(2)}, u32[]{:S(2)}) collective-permute-start(f32[3,1,8,128]{3,2,1,0:T(8,128)S(1)} %get-tuple-element.291), channel_id=1, source_target_pairs={{0,1},{1,2},{2,3},{3,4},{4,5},{5,6},{6,7},{7,8},{8,9},{9,10},{10,1... | collective-permute-start | bytes 36872 | tf_op jit(solution)/shard_map/while/body/eval_jaxpr/ppermute | solution.py:20
  395.9 8.8 %collective-permute-start = (f32[3,2,8,128]{3,2,1,0:T(8,128)S(1)}, f32[3,2,8,128]{3,2,1,0:T(8,128)S(1)}, u32[]{:S(2)}, u32[]{:S(2)}) collective-permute-start(f32[3,2,8,128]{3,2,1,0:T(8,128)S(1)} %get-tuple-element.312), channel_id=1, source_target_pairs={{0,16},{16,32},{32,48},{48,64},{64,80},{80,96},{96,112},{112,128},... | collective-permute-start | bytes 73736 | tf_op jit(solution)/shard_map/while/body/eval_jaxpr/ppermute | solution.py:32
  406.6 7.7 %collective-permute-start.2 = (f32[3,1,8,128]{3,2,1,0:T(8,128)S(1)}, f32[3,1,8,128]{3,2,1,0:T(8,128)S(1)}, u32[]{:S(2)}, u32[]{:S(2)}) collective-permute-start(f32[3,1,8,128]{3,2,1,0:T(8,128)S(1)} %get-tuple-element.291), channel_id=1, source_target_pairs={{0,1},{1,2},{2,3},{3,4},{4,5},{5,6},{6,7},{7,8},{8,9},{9,10},{10,1... | collective-permute-start | bytes 36872 | tf_op jit(solution)/shard_map/while/body/eval_jaxpr/ppermute | solution.py:20
  414.6 8.8 %collective-permute-start = (f32[3,2,8,128]{3,2,1,0:T(8,128)S(1)}, f32[3,2,8,128]{3,2,1,0:T(8,128)S(1)}, u32[]{:S(2)}, u32[]{:S(2)}) collective-permute-start(f32[3,2,8,128]{3,2,1,0:T(8,128)S(1)} %get-tuple-element.312), channel_id=1, source_target_pairs={{0,16},{16,32},{32,48},{48,64},{64,80},{80,96},{96,112},{112,128},... | collective-permute-start | bytes 73736 | tf_op jit(solution)/shard_map/while/body/eval_jaxpr/ppermute | solution.py:32
  425.3 7.7 %collective-permute-start.2 = (f32[3,1,8,128]{3,2,1,0:T(8,128)S(1)}, f32[3,1,8,128]{3,2,1,0:T(8,128)S(1)}, u32[]{:S(2)}, u32[]{:S(2)}) collective-permute-start(f32[3,1,8,128]{3,2,1,0:T(8,128)S(1)} %get-tuple-element.291), channel_id=1, source_target_pairs={{0,1},{1,2},{2,3},{3,4},{4,5},{5,6},{6,7},{7,8},{8,9},{9,10},{10,1... | collective-permute-start | bytes 36872 | tf_op jit(solution)/shard_map/while/body/eval_jaxpr/ppermute | solution.py:20
  433.2 8.8 %collective-permute-start = (f32[3,2,8,128]{3,2,1,0:T(8,128)S(1)}, f32[3,2,8,128]{3,2,1,0:T(8,128)S(1)}, u32[]{:S(2)}, u32[]{:S(2)}) collective-permute-start(f32[3,2,8,128]{3,2,1,0:T(8,128)S(1)} %get-tuple-element.312), channel_id=1, source_target_pairs={{0,16},{16,32},{32,48},{48,64},{64,80},{80,96},{96,112},{112,128},... | collective-permute-start | bytes 73736 | tf_op jit(solution)/shard_map/while/body/eval_jaxpr/ppermute | solution.py:32
  443.9 7.7 %collective-permute-start.2 = (f32[3,1,8,128]{3,2,1,0:T(8,128)S(1)}, f32[3,1,8,128]{3,2,1,0:T(8,128)S(1)}, u32[]{:S(2)}, u32[]{:S(2)}) collective-permute-start(f32[3,1,8,128]{3,2,1,0:T(8,128)S(1)} %get-tuple-element.291), channel_id=1, source_target_pairs={{0,1},{1,2},{2,3},{3,4},{4,5},{5,6},{6,7},{7,8},{8,9},{9,10},{10,1... | collective-permute-start | bytes 36872 | tf_op jit(solution)/shard_map/while/body/eval_jaxpr/ppermute | solution.py:20
  451.8 8.8 %collective-permute-start = (f32[3,2,8,128]{3,2,1,0:T(8,128)S(1)}, f32[3,2,8,128]{3,2,1,0:T(8,128)S(1)}, u32[]{:S(2)}, u32[]{:S(2)}) collective-permute-start(f32[3,2,8,128]{3,2,1,0:T(8,128)S(1)} %get-tuple-element.312), channel_id=1, source_target_pairs={{0,16},{16,32},{32,48},{48,64},{64,80},{80,96},{96,112},{112,128},... | collective-permute-start | bytes 73736 | tf_op jit(solution)/shard_map/while/body/eval_jaxpr/ppermute | solution.py:32
  462.5 7.7 %collective-permute-start.2 = (f32[3,1,8,128]{3,2,1,0:T(8,128)S(1)}, f32[3,1,8,128]{3,2,1,0:T(8,128)S(1)}, u32[]{:S(2)}, u32[]{:S(2)}) collective-permute-start(f32[3,1,8,128]{3,2,1,0:T(8,128)S(1)} %get-tuple-element.291), channel_id=1, source_target_pairs={{0,1},{1,2},{2,3},{3,4},{4,5},{5,6},{6,7},{7,8},{8,9},{9,10},{10,1... | collective-permute-start | bytes 36872 | tf_op jit(solution)/shard_map/while/body/eval_jaxpr/ppermute | solution.py:20
  470.5 8.8 %collective-permute-start = (f32[3,2,8,128]{3,2,1,0:T(8,128)S(1)}, f32[3,2,8,128]{3,2,1,0:T(8,128)S(1)}, u32[]{:S(2)}, u32[]{:S(2)}) collective-permute-start(f32[3,2,8,128]{3,2,1,0:T(8,128)S(1)} %get-tuple-element.312), channel_id=1, source_target_pairs={{0,16},{16,32},{32,48},{48,64},{64,80},{80,96},{96,112},{112,128},... | collective-permute-start | bytes 73736 | tf_op jit(solution)/shard_map/while/body/eval_jaxpr/ppermute | solution.py:32
  489.1 8.8 %collective-permute-start = (f32[3,2,8,128]{3,2,1,0:T(8,128)S(1)}, f32[3,2,8,128]{3,2,1,0:T(8,128)S(1)}, u32[]{:S(2)}, u32[]{:S(2)}) collective-permute-start(f32[3,2,8,128]{3,2,1,0:T(8,128)S(1)} %get-tuple-element.312), channel_id=1, source_target_pairs={{0,16},{16,32},{32,48},{48,64},{64,80},{80,96},{96,112},{112,128},... | collective-permute-start | bytes 73736 | tf_op jit(solution)/shard_map/while/body/eval_jaxpr/ppermute | solution.py:32
  507.7 8.8 %collective-permute-start = (f32[3,2,8,128]{3,2,1,0:T(8,128)S(1)}, f32[3,2,8,128]{3,2,1,0:T(8,128)S(1)}, u32[]{:S(2)}, u32[]{:S(2)}) collective-permute-start(f32[3,2,8,128]{3,2,1,0:T(8,128)S(1)} %get-tuple-element.312), channel_id=1, source_target_pairs={{0,16},{16,32},{32,48},{48,64},{64,80},{80,96},{96,112},{112,128},... | collective-permute-start | bytes 73736 | tf_op jit(solution)/shard_map/while/body/eval_jaxpr/ppermute | solution.py:32
  526.3 8.8 %collective-permute-start = (f32[3,2,8,128]{3,2,1,0:T(8,128)S(1)}, f32[3,2,8,128]{3,2,1,0:T(8,128)S(1)}, u32[]{:S(2)}, u32[]{:S(2)}) collective-permute-start(f32[3,2,8,128]{3,2,1,0:T(8,128)S(1)} %get-tuple-element.312), channel_id=1, source_target_pairs={{0,16},{16,32},{32,48},{48,64},{64,80},{80,96},{96,112},{112,128},... | collective-permute-start | bytes 73736 | tf_op jit(solution)/shard_map/while/body/eval_jaxpr/ppermute | solution.py:32
  545.0 8.8 %collective-permute-start = (f32[3,2,8,128]{3,2,1,0:T(8,128)S(1)}, f32[3,2,8,128]{3,2,1,0:T(8,128)S(1)}, u32[]{:S(2)}, u32[]{:S(2)}) collective-permute-start(f32[3,2,8,128]{3,2,1,0:T(8,128)S(1)} %get-tuple-element.312), channel_id=1, source_target_pairs={{0,16},{16,32},{32,48},{48,64},{64,80},{80,96},{96,112},{112,128},... | collective-permute-start | bytes 73736 | tf_op jit(solution)/shard_map/while/body/eval_jaxpr/ppermute | solution.py:32
  563.6 8.8 %collective-permute-start = (f32[3,2,8,128]{3,2,1,0:T(8,128)S(1)}, f32[3,2,8,128]{3,2,1,0:T(8,128)S(1)}, u32[]{:S(2)}, u32[]{:S(2)}) collective-permute-start(f32[3,2,8,128]{3,2,1,0:T(8,128)S(1)} %get-tuple-element.312), channel_id=1, source_target_pairs={{0,16},{16,32},{32,48},{48,64},{64,80},{80,96},{96,112},{112,128},... | collective-permute-start | bytes 73736 | tf_op jit(solution)/shard_map/while/body/eval_jaxpr/ppermute | solution.py:32
  574.3 7.7 %collective-permute-start.2 = (f32[3,1,8,128]{3,2,1,0:T(8,128)S(1)}, f32[3,1,8,128]{3,2,1,0:T(8,128)S(1)}, u32[]{:S(2)}, u32[]{:S(2)}) collective-permute-start(f32[3,1,8,128]{3,2,1,0:T(8,128)S(1)} %get-tuple-element.291), channel_id=1, source_target_pairs={{0,1},{1,2},{2,3},{3,4},{4,5},{5,6},{6,7},{7,8},{8,9},{9,10},{10,1... | collective-permute-start | bytes 36872 | tf_op jit(solution)/shard_map/while/body/eval_jaxpr/ppermute | solution.py:20
  582.2 8.8 %collective-permute-start = (f32[3,2,8,128]{3,2,1,0:T(8,128)S(1)}, f32[3,2,8,128]{3,2,1,0:T(8,128)S(1)}, u32[]{:S(2)}, u32[]{:S(2)}) collective-permute-start(f32[3,2,8,128]{3,2,1,0:T(8,128)S(1)} %get-tuple-element.312), channel_id=1, source_target_pairs={{0,16},{16,32},{32,48},{48,64},{64,80},{80,96},{96,112},{112,128},... | collective-permute-start | bytes 73736 | tf_op jit(solution)/shard_map/while/body/eval_jaxpr/ppermute | solution.py:32
  600.9 8.8 %collective-permute-start = (f32[3,2,8,128]{3,2,1,0:T(8,128)S(1)}, f32[3,2,8,128]{3,2,1,0:T(8,128)S(1)}, u32[]{:S(2)}, u32[]{:S(2)}) collective-permute-start(f32[3,2,8,128]{3,2,1,0:T(8,128)S(1)} %get-tuple-element.312), channel_id=1, source_target_pairs={{0,16},{16,32},{32,48},{48,64},{64,80},{80,96},{96,112},{112,128},... | collective-permute-start | bytes 73736 | tf_op jit(solution)/shard_map/while/body/eval_jaxpr/ppermute | solution.py:32
  619.5 8.8 %collective-permute-start = (f32[3,2,8,128]{3,2,1,0:T(8,128)S(1)}, f32[3,2,8,128]{3,2,1,0:T(8,128)S(1)}, u32[]{:S(2)}, u32[]{:S(2)}) collective-permute-start(f32[3,2,8,128]{3,2,1,0:T(8,128)S(1)} %get-tuple-element.312), channel_id=1, source_target_pairs={{0,16},{16,32},{32,48},{48,64},{64,80},{80,96},{96,112},{112,128},... | collective-permute-start | bytes 73736 | tf_op jit(solution)/shard_map/while/body/eval_jaxpr/ppermute | solution.py:32
  638.1 8.8 %collective-permute-start = (f32[3,2,8,128]{3,2,1,0:T(8,128)S(1)}, f32[3,2,8,128]{3,2,1,0:T(8,128)S(1)}, u32[]{:S(2)}, u32[]{:S(2)}) collective-permute-start(f32[3,2,8,128]{3,2,1,0:T(8,128)S(1)} %get-tuple-element.312), channel_id=1, source_target_pairs={{0,16},{16,32},{32,48},{48,64},{64,80},{80,96},{96,112},{112,128},... | collective-permute-start | bytes 73736 | tf_op jit(solution)/shard_map/while/body/eval_jaxpr/ppermute | solution.py:32
  656.7 8.8 %collective-permute-start = (f32[3,2,8,128]{3,2,1,0:T(8,128)S(1)}, f32[3,2,8,128]{3,2,1,0:T(8,128)S(1)}, u32[]{:S(2)}, u32[]{:S(2)}) collective-permute-start(f32[3,2,8,128]{3,2,1,0:T(8,128)S(1)} %get-tuple-element.312), channel_id=1, source_target_pairs={{0,16},{16,32},{32,48},{48,64},{64,80},{80,96},{96,112},{112,128},... | collective-permute-start | bytes 73736 | tf_op jit(solution)/shard_map/while/body/eval_jaxpr/ppermute | solution.py:32
  675.4 8.8 %collective-permute-start = (f32[3,2,8,128]{3,2,1,0:T(8,128)S(1)}, f32[3,2,8,128]{3,2,1,0:T(8,128)S(1)}, u32[]{:S(2)}, u32[]{:S(2)}) collective-permute-start(f32[3,2,8,128]{3,2,1,0:T(8,128)S(1)} %get-tuple-element.312), channel_id=1, source_target_pairs={{0,16},{16,32},{32,48},{48,64},{64,80},{80,96},{96,112},{112,128},... | collective-permute-start | bytes 73736 | tf_op jit(solution)/shard_map/while/body/eval_jaxpr/ppermute | solution.py:32
  694.0 8.8 %collective-permute-start = (f32[3,2,8,128]{3,2,1,0:T(8,128)S(1)}, f32[3,2,8,128]{3,2,1,0:T(8,128)S(1)}, u32[]{:S(2)}, u32[]{:S(2)}) collective-permute-start(f32[3,2,8,128]{3,2,1,0:T(8,128)S(1)} %get-tuple-element.312), channel_id=1, source_target_pairs={{0,16},{16,32},{32,48},{48,64},{64,80},{80,96},{96,112},{112,128},... | collective-permute-start | bytes 73736 | tf_op jit(solution)/shard_map/while/body/eval_jaxpr/ppermute | solution.py:32
  712.6 8.8 %collective-permute-start = (f32[3,2,8,128]{3,2,1,0:T(8,128)S(1)}, f32[3,2,8,128]{3,2,1,0:T(8,128)S(1)}, u32[]{:S(2)}, u32[]{:S(2)}) collective-permute-start(f32[3,2,8,128]{3,2,1,0:T(8,128)S(1)} %get-tuple-element.312), channel_id=1, source_target_pairs={{0,16},{16,32},{32,48},{48,64},{64,80},{80,96},{96,112},{112,128},... | collective-permute-start | bytes 73736 | tf_op jit(solution)/shard_map/while/body/eval_jaxpr/ppermute | solution.py:32
  731.3 8.8 %collective-permute-start = (f32[3,2,8,128]{3,2,1,0:T(8,128)S(1)}, f32[3,2,8,128]{3,2,1,0:T(8,128)S(1)}, u32[]{:S(2)}, u32[]{:S(2)}) collective-permute-start(f32[3,2,8,128]{3,2,1,0:T(8,128)S(1)} %get-tuple-element.312), channel_id=1, source_target_pairs={{0,16},{16,32},{32,48},{48,64},{64,80},{80,96},{96,112},{112,128},... | collective-permute-start | bytes 73736 | tf_op jit(solution)/shard_map/while/body/eval_jaxpr/ppermute | solution.py:32
  (97 other events, 609.1 us)
where the time goes:
time: 756 us; the launch traced here: 752 us
  waiting for transfers between devices  345 us (46%)
  starting transfers between devices  300 us (40%)
  local copies, waits for them, and re-layouts  60.7 us (8%)
  other arithmetic  42.2 us (6%)
    ppermute x33, waiting for transfers between devices, from_behind(): return lax.ppermute(block, axis, route)  218 us
    ppermute x38, starting transfers between devices, extended_2(): lax.ppermute(tail, axis, [(i, (i + 1) % count) for i in range(ends)])  135 us
    ppermute x38, waiting for transfers between devices, extended_2(): lax.ppermute(tail, axis, [(i, (i + 1) % count) for i in range(ends)])  124 us
    ppermute x38, starting transfers between devices, extended_2(): lax.ppermute(head, axis, [((i + 1) % count, i) for i in range(ends)])  102 us
    ppermute x33, starting transfers between devices, from_behind(): return lax.ppermute(block, axis, route)  63.4 us
    reshape x3, local copies, waits for them, and re-layouts, coarsen(): values.reshape(comps, zlen // 2, 2, xlen // 2, 2, ylen // 2, 2)  42.9 us
    reduce_sum x3, other arithmetic, coarsen(): values.reshape(comps, zlen // 2, 2, xlen // 2, 2, ylen // 2, 2)  17.3 us
  transfers between devices with their start and end apart: 109, of which 68 were waited for; matrix products, arithmetic and copies ran while one was open for 7% of the time, Pallas kernels for 0%

commit v1 on v0

v1 whole, which is shorter than its diff:
```python
import jax
import jax.numpy as jnp
from jax import lax
from jax.experimental import pallas as pl
from jax.experimental.pallas import tpu as pltpu
from jax.sharding import PartitionSpec as P

STEPS = 4
KAPPA = 0.04
F32 = jnp.float32
HI = lax.Precision.HIGHEST
VM = pltpu.MemorySpace.VMEM


def lane_parity(transpose=False):
    row = lax.broadcasted_iota(jnp.int32, (256, 256), 1 if transpose else 0)
    col = lax.broadcasted_iota(jnp.int32, (256, 256), 0 if transpose else 1)
    want = 2 * (col % 128) + col // 128
    return (row == want).astype(F32)


def shift(v, by, axis, masked_at, index):
    return jnp.where(index == masked_at, 0.0, pltpu.roll(v, by % v.shape[axis], axis))


def stencil_terms(low, high, mid, inside):
    a = [KAPPA + jnp.maximum(mid[d], 0.0) for d in range(3)]
    b = [KAPPA - jnp.minimum(mid[d], 0.0) for d in range(3)]
    centre = 1.0 - (a[0] + b[0] + a[1] + b[1] + a[2] + b[2])
    m = [[(high[e][c] - low[e][c]) * 0.5 for e in range(3)] for c in range(3)]
    for c in range(3):
        m[c][c] = m[c][c] + centre
    a = [x * inside for x in a]
    b = [x * inside for x in b]
    m = [[x * inside for x in row] for row in m]
    return a, b, m


def iotas():
    sub = lax.broadcasted_iota(jnp.int32, (8, 128), 0)
    lane = lax.broadcasted_iota(jnp.int32, (8, 128), 1)
    return sub, lane


def coarse_coefs(below, here, above, inside, store):
    sub, lane = iotas()
    low = [below, [shift(v, 1, 0, 0, sub) for v in here], [shift(v, 1, 1, 0, lane) for v in here]]
    high = [above, [shift(v, -1, 0, 7, sub) for v in here], [shift(v, -1, 1, 127, lane) for v in here]]
    a, b, m = stencil_terms(low, high, here, inside)
    a[1] = jnp.where(sub == 0, 0.0, a[1])
    b[1] = jnp.where(sub == 7, 0.0, b[1])
    a[2] = jnp.where(lane == 0, 0.0, a[2])
    b[2] = jnp.where(lane == 127, 0.0, b[2])
    flat = a + b + m[0] + m[1] + m[2]
    for i, x in enumerate(flat):
        store(i, x)


def psi(coef, below, here, above):
    a = [coef(i) for i in range(3)]
    b = [coef(3 + i) for i in range(3)]
    out = []
    for c in range(3):
        w = here[c]
        acc = a[0] * below[c] + b[0] * above[c]
        acc = acc + (a[1] * pltpu.roll(w, 1, 0) + b[1] * pltpu.roll(w, 7, 0))
        acc = acc + (a[2] * pltpu.roll(w, 1, 1) + b[2] * pltpu.roll(w, 127, 1))
        acc = acc + (coef(6 + 3 * c) * here[0] + coef(7 + 3 * c) * here[1] + coef(8 + 3 * c) * here[2])
        out.append(acc)
    return out


NL = 20


def fine_kernel(pos_ref, m2_ref, m1_ref, own_ref, p1_ref, p2_ref,
                start_ref, relaxed_ref, g_ref, first_ref, state_a, state_b, speed, coefs, ev, od):
    slab = pos_ref[0]
    anchor = pos_ref[1] == 1
    depth = pos_ref[2]
    perm = lane_parity()
    for i, ref in enumerate((m2_ref, m1_ref, own_ref, p1_ref, p2_ref)):
        z0 = 4 * i
        for part, dest in ((0, state_a), (1, speed)):
            rows = ref[3 * part:3 * part + 3].reshape(192, 256)
            both = jnp.dot(rows, perm, precision=HI, preferred_element_type=F32)
            ev[...] = both[:, :128]
            od[...] = both[:, 128:]
            for q in range(2):
                dest[:, z0:z0 + 4, 2 * q] = ev[pl.ds(q, 96, stride=2), :].reshape(3, 4, 8, 128)
                dest[:, z0:z0 + 4, 2 * q + 1] = od[pl.ds(q, 96, stride=2), :].reshape(3, 4, 8, 128)
    sub, lane = iotas()

    def build(l, carry):
        z = slab * 4 + l - 8
        inside = jnp.where(jnp.logical_and(z >= 0, z < depth), 1.0, 0.0).astype(F32)
        mid = [[speed[c, l, k] for c in range(3)] for k in range(4)]
        for q in range(2):
            for p in range(2):
                k = 2 * q + p
                here = mid[k]
                xo = mid[2 * (1 - q) + p]
                yo = mid[2 * q + 1 - p]
                low_z = [speed[c, l - 1, k] for c in range(3)]
                high_z = [speed[c, l + 1, k] for c in range(3)]
                low_x = xo if q else [shift(v, 1, 0, 0, sub) for v in xo]
                high_x = [shift(v, -1, 0, 7, sub) for v in xo] if q else xo
                low_y = yo if p else [shift(v, 1, 1, 0, lane) for v in yo]
                high_y = [shift(v, -1, 1, 127, lane) for v in yo] if p else yo
                a, b, m = stencil_terms([low_z, low_x, low_y], [high_z, high_x, high_y], here, inside)
                if q:
                    b[1] = jnp.where(sub == 7, 0.0, b[1])
                else:
                    a[1] = jnp.where(sub == 0, 0.0, a[1])
                if p:
                    b[2] = jnp.where(lane == 127, 0.0, b[2])
                else:
                    a[2] = jnp.where(lane == 0, 0.0, a[2])
                for i, x in enumerate(a + b + m[0] + m[1] + m[2]):
                    coefs[l, k, i] = x
        return carry

    lax.fori_loop(1, NL - 1, build, 0)

    def march(src, dst, first, last):
        def layer(l, carry):
            w = [[src[c, l, k] for k in range(4)] for c in range(3)]
            for q in range(2):
                for p in range(2):
                    k = 2 * q + p
                    kx = 2 * (1 - q) + p
                    ky = 2 * q + 1 - p
                    cf = [coefs[l, k, i] for i in range(15)]
                    for c in range(3):
                        xo = w[c][kx]
                        xr = pltpu.roll(xo, 7 if q else 1, 0)
                        yo = w[c][ky]
                        yr = pltpu.roll(yo, 127 if p else 1, 1)
                        acc = cf[0] * src[c, l - 1, k] + cf[3] * src[c, l + 1, k]
                        acc = acc + (cf[1] * (xo if q else xr) + cf[4] * (xr if q else xo))
                        acc = acc + (cf[2] * (yo if p else yr) + cf[5] * (yr if p else yo))
                        acc = acc + (cf[6 + 3 * c] * w[0][k] + cf[7 + 3 * c] * w[1][k] + cf[8 + 3 * c] * w[2][k])
                        dst[c, l, k] = acc
            return carry
        lax.fori_loop(first, last, layer, 0)

    def restrict(src, j):
        out = []
        for c in range(3):
            lo = (src[c, 2 * j, 0] + src[c, 2 * j, 1]) + (src[c, 2 * j, 2] + src[c, 2 * j, 3])
            hi = (src[c, 2 * j + 1, 0] + src[c, 2 * j + 1, 1]) + (src[c, 2 * j + 1, 2] + src[c, 2 * j + 1, 3])
            out.append((lo + hi) * 0.125)
        return out

    start_ref[...] = state_a[:, 8:12]
    coarse0 = {j: restrict(state_a, j) for j in range(2, 8)}
    speed_c = {j: [2.0 * v for v in restrict(speed, j)] for j in range(2, 8)}
    src, dst = state_a, state_b
    for k in range(1, 5):
        march(src, dst, k, NL - k)
        src, dst = dst, src
    relaxed_ref[...] = src[:, 8:12]
    coarse_r = {j: restrict(src, j) for j in range(3, 7)}
    for k in range(5, 9):
        march(src, dst, k, NL - k)
        src, dst = dst, src
    cc = {}
    for j in range(3, 7):
        z = slab * 2 + j - 4
        inside = jnp.where(jnp.logical_and(z >= 0, z < depth // 2), 1.0, 0.0).astype(F32)
        vals = {}
        coarse_coefs(speed_c[j - 1], speed_c[j], speed_c[j + 1], inside, vals.__setitem__)
        cc[j] = vals
    coarse1 = {}
    for j in range(3, 7):
        image = psi(cc[j].__getitem__, coarse0[j - 1], coarse0[j], coarse0[j + 1])
        coarse1[j] = [image[c] + (coarse_r[j][c] - image[c]) for c in range(3)]
    flag = jnp.where(anchor, 1.0, 0.0).astype(F32)
    for i, j in enumerate((4, 5)):
        again = restrict(src, j)
        image = psi(cc[j].__getitem__, coarse_r[j - 1], coarse_r[j], coarse_r[j + 1])
        start = psi(cc[j].__getitem__, coarse1[j - 1], coarse1[j], coarse1[j + 1])
        for c in range(3):
            forcing = again[c] - image[c]
            g_ref[c, i] = forcing + flag * start[c]
            first_ref[c, i] = coarse1[j][c]


def fine(pos, m2, m1, own, p1, p2):
    vm = pl.BlockSpec(memory_space=VM)
    return pl.pallas_call(
        fine_kernel,
        out_shape=(
            jax.ShapeDtypeStruct((3, 4, 4, 8, 128), F32),
            jax.ShapeDtypeStruct((3, 4, 4, 8, 128), F32),
            jax.ShapeDtypeStruct((3, 2, 8, 128), F32),
            jax.ShapeDtypeStruct((3, 2, 8, 128), F32),
        ),
        in_specs=[pl.BlockSpec(memory_space=pltpu.MemorySpace.SMEM)] + [vm] * 5,
        out_specs=(vm,) * 4,
        scratch_shapes=[
            pltpu.VMEM((3, NL, 4, 8, 128), F32),
            pltpu.VMEM((3, NL, 4, 8, 128), F32),
            pltpu.VMEM((3, NL, 4, 8, 128), F32),
            pltpu.VMEM((NL, 4, 15, 8, 128), F32),
            pltpu.VMEM((192, 128), F32),
            pltpu.VMEM((192, 128), F32),
        ],
        compiler_params=pltpu.CompilerParams(vmem_limit_bytes=40 << 20),
        cost_estimate=pl.CostEstimate(flops=20_000_000, bytes_accessed=3_000_000, transcendentals=0),
        name="fine",
    )(pos, m2, m1, own, p1, p2)


def speed_kernel(own_ref, speed_ref, ev):
    row = lax.broadcasted_iota(jnp.int32, (256, 128), 0)
    col = lax.broadcasted_iota(jnp.int32, (256, 128), 1)
    pool = (row // 2 == col).astype(F32)
    rows = own_ref[...].reshape(192, 256)
    ev[...] = jnp.dot(rows, pool, precision=HI, preferred_element_type=F32)
    x2 = ev[pl.ds(0, 96, stride=2), :] + ev[pl.ds(1, 96, stride=2), :]
    x2 = x2.reshape(3, 2, 2, 8, 128)
    speed_ref[...] = (x2[:, :, 0] + x2[:, :, 1]) * 0.25


def coarse_speed(own):
    vm = pl.BlockSpec(memory_space=VM)
    return pl.pallas_call(
        speed_kernel,
        out_shape=jax.ShapeDtypeStruct((3, 2, 8, 128), F32),
        in_specs=[vm],
        out_specs=vm,
        scratch_shapes=[pltpu.VMEM((192, 128), F32)],
        cost_estimate=pl.CostEstimate(flops=1_000_000, bytes_accessed=200_000, transcendentals=0),
        name="speed",
    )(own)


def build_coefs(speed_ref, coefs, layers):
    def one(j, carry):
        def at(i):
            keep = jnp.where(jnp.logical_and(i >= 0, i < layers), 1.0, 0.0).astype(F32)
            k = jnp.clip(i, 0, layers - 1)
            return [speed_ref[k // 2, c, k % 2] * keep for c in range(3)]
        here = at(j)

        def store(i, x):
            coefs[j, i] = x
        coarse_coefs(at(j - 1), here, at(j + 1), jnp.float32(1.0), store)
        return carry
    lax.fori_loop(0, layers, one, 0)


def psi_layer(coefs, src, j):
    return psi(lambda i: coefs[j, i],
               [src[j, c] for c in range(3)],
               [src[j + 1, c] for c in range(3)],
               [src[j + 2, c] for c in range(3)])


def finish(first, start_ref, relaxed_ref, coarse, out_ref, ev, od):
    for c in range(3):
        for zc in range(2):
            w = [[jnp.where(first, start_ref[c, 2 * zc + dz, k], relaxed_ref[c, 2 * zc + dz, k])
                  for k in range(4)] for dz in range(2)]
            lo, hi = [(v[0] + v[1]) + (v[2] + v[3]) for v in w]
            mean = (lo + hi) * 0.125
            diff = jnp.where(first, mean, coarse(c, zc)) - mean
            for dz in range(2):
                row0 = (c * 4 + 2 * zc + dz) * 16
                for q in range(2):
                    ev[pl.ds(row0 + q, 8, stride=2), :] = w[dz][2 * q] + diff
                    od[pl.ds(row0 + q, 8, stride=2), :] = w[dz][2 * q + 1] + diff
    both = jnp.concatenate([ev[...], od[...]], axis=1)
    out = jnp.dot(both, lane_parity(True), precision=HI, preferred_element_type=F32)
    out_ref[...] = out.reshape(3, 4, 16, 256)


def sweep_all_kernel(pos_ref, start_ref, relaxed_ref, coarse1_ref, speed_ref, g_hbm, out_ref,
                     coefs, state_a, state_b, keep, g_buf, ev, od, sems):
    slab, t = pos_ref[0], pos_ref[1]
    layers = 2 * speed_ref.shape[0]
    turns = g_hbm.shape[0] - 2

    def fetch(k, slot):
        return pltpu.make_async_copy(g_hbm.at[k], g_buf.at[slot], sems.at[slot])
    fetch(0, 0).start()
    build_coefs(speed_ref, coefs, layers)
    for ref in (state_a, state_b):
        ref[...] = jnp.zeros_like(ref)
    keep[...] = coarse1_ref[...]

    def step(k, src, dst, slot):
        fetch(k, slot).wait()

        @pl.when(k + 1 < turns)
        def _():
            fetch(k + 1, 1 - slot).start()

        def layer(j, carry):
            new = psi_layer(coefs, src, j)
            for c in range(3):
                dst[j + 1, c] = new[c] + g_buf[slot, j // 2, c, j % 2]
            return carry
        lax.fori_loop(0, layers, layer, 0)

        @pl.when(k + 2 == t)
        def _():
            for i in range(2):
                for c in range(3):
                    keep[c, i] = dst[1 + 2 * slab + i, c]

    def two(i, carry):
        step(2 * i, state_a, state_b, 0)
        step(2 * i + 1, state_b, state_a, 1)
        return carry
    lax.fori_loop(0, turns // 2, two, 0)
    finish(t == 0, start_ref, relaxed_ref, lambda c, zc: keep[c, zc], out_ref, ev, od)


def sweep_all(pos, start, relaxed, coarse1, speed, g):
    vm = pl.BlockSpec(memory_space=VM)
    layers = 2 * speed.shape[0]
    return pl.pallas_call(
        sweep_all_kernel,
        out_shape=jax.ShapeDtypeStruct((3, 4, 16, 256), F32),
        in_specs=[pl.BlockSpec(memory_space=pltpu.MemorySpace.SMEM)] + [vm] * 4 + [pl.BlockSpec(memory_space=pl.ANY)],
        out_specs=vm,
        scratch_shapes=[
            pltpu.VMEM((layers, 15, 8, 128), F32),
            pltpu.VMEM((layers + 2, 3, 8, 128), F32),
            pltpu.VMEM((layers + 2, 3, 8, 128), F32),
            pltpu.VMEM((3, 2, 8, 128), F32),
            pltpu.VMEM((2,) + g.shape[1:], F32),
            pltpu.VMEM((192, 128), F32),
            pltpu.VMEM((192, 128), F32),
            pltpu.SemaphoreType.DMA((2,)),
        ],
        compiler_params=pltpu.CompilerParams(vmem_limit_bytes=16 << 20),
        cost_estimate=pl.CostEstimate(flops=50_000_000, bytes_accessed=13_000_000, transcendentals=0),
        name="sweep",
    )(pos, start, relaxed, coarse1, speed, g)


def moved(block, by):
    count = lax.axis_size("gz")
    route = [(i, i + by) for i in range(count) if 0 <= i + by < count]
    return lax.ppermute(block, "gz", route)


def local(c_states, velocity):
    slab = lax.axis_index("gz")
    t = lax.axis_index("tm")
    intervals, slabs = lax.axis_size("tm"), lax.axis_size("gz")
    depth = slabs * velocity.shape[1]
    own = jnp.concatenate([c_states[0], velocity], axis=0)
    m2, m1, p1, p2 = [moved(own, by) for by in (2, 1, -1, -2)]
    speed = lax.all_gather(coarse_speed(velocity), "gz")
    pos = jnp.stack([slab, (t == 0).astype(jnp.int32), jnp.int32(depth)])
    start, after, forcing, coarse1 = fine(pos, m2, m1, own, p1, p2)
    route = [(i, i + 1) for i in range(intervals - 1)]
    relaxed = lax.ppermute(after, "tm", route)
    coarse1 = lax.ppermute(coarse1, "tm", route)
    forcing = lax.all_gather(forcing, ("tm", "gz"))
    forcing = forcing.reshape((intervals, slabs) + forcing.shape[1:])
    out = sweep_all(jnp.stack([slab, t]), start, relaxed, coarse1, speed, forcing)
    return out[None]


def solution(mesh):
    return jax.shard_map(
        local,
        mesh=mesh,
        in_specs=(P("tm", None, "gz", None, None), P(None, "gz", None, None)),
        out_specs=P("tm", None, "gz", None, None),
        check_vma=False,
    )
```

time: 756 us -> 1600 us (2.12)
  the two profiles are of different devices: /device:TPU:258 before, /device:TPU:27 now
where the time goes in v1:
time: 1600 us
  waiting for transfers between devices  1420 us (89%)
  Pallas kernels  99.4 us (6%)
  starting transfers between devices  30.8 us (2%)
  blocking collectives  25.4 us (2%)
    all_gather x1, waiting for transfers between devices, local(): forcing = lax.all_gather(forcing, ('tm', 'gz'))  1410 us
    pallas_call x1, Pallas kernels, sweep_all(): pl.pallas_call(sweep_all_kernel, out_shape=jax.ShapeDtypeStruct((3, 4, 16...  85.3 us
  transfers between devices with their start and end apart: 7, of which 4 were waited for; matrix products, arithmetic and copies ran while one was open for 0% of the time, Pallas kernels for 0%

profile of v1, /device:TPU:27, one launch (start us, length us, event | category | flops | bytes accessed | tf_op | source)
XLA Modules:
  0.0 1599.6 jit_solution(5584510148740678635)
XLA Ops:
  6.5 0.0 all-gather.4.cloned.1.call-start
  6.5 1.0 pad_maximum_fusion.own_ref
  7.6 4.5 collective-permute-start
  12.1 2.3 collective-permute-start.1
  14.4 3.0 collective-permute-start.2
  17.4 2.7 collective-permute-start.3
  20.1 0.1 pad_add_fusion.1.pos_ref
  20.2 9.6 collective-permute-done.m2_ref
  29.8 8.8 collective-permute-done.1.m1_ref
  38.6 0.0 collective-permute-done.2.p1_ref
  38.6 0.0 collective-permute-done.3.p2_ref
  38.6 12.3 fine.1
  50.8 0.0 all-gather.4.cloned.1.call-update
  50.8 1.9 speed.1
  52.7 10.0 collective-permute-start.4
  62.7 25.4 %all-gather = f32[48,2,8,128]{3,2,1,0:T(8,128)S(1)} all-gather(f32[3,2,8,128]{3,2,1,0:T(8,128)} %speed.1), channel_id=2, replica_groups=mesh['tm'=32,'gz'=16] {'gz'}, dimensions={0}, use_global_device_ids=true | all-gather | bytes 417792 | tf_op jit(solution)/shard_map/all_gather | solution.py:358
  88.2 8.3 collective-permute-start.5
  96.4 0.1 pad_add_fusion.pos_ref
  96.5 0.8 collective-permute-done.5.coarse1_ref
  97.4 0.0 collective-permute-done.4.relaxed_ref
  97.4 1405.6 %all-gather.4.cloned.1.call-done = f32[1536,2,8,128]{3,2,1,0:T(8,128)} async-done(((f32[3,2,8,128]{3,2,1,0:T(8,128)}), f32[1536,2,8,128]{3,2,1,0:T(8,128)}) %all-gather.4.cloned.1.call-update) | async-done | bytes 12582928 | tf_op jit(solution)/shard_map/all_gather | solution.py:364
  1502.9 0.0 copy-start
  1502.9 4.6 copy-done
  1507.5 85.3 %sweep.1 = f32[3,4,16,256]{3,2,1,0:T(8,128)} custom-call(s32[2]{0:T(128)S(1)} %pad_add_fusion.pos_ref, f32[3,4,4,8,128]{4,3,2,1,0:T(8,128)S(1)} %get-tuple-element.9.start_ref, f32[3,4,4,8,128]{4,3,2,1,0:T(8,128)S(1)} %collective-permute-done.4.relaxed_ref, f32[3,2,8,128]{3,2,1,0:T(8,128)S(1)} %collective-permute-done.5.coarse1_ref, ...), custom_call_target="tpu_custom_call" | custom-call | flops 50000000 | bytes 13000000 | tf_op jit(solution)/shard_map/sweep/pallas_call | solution.py:324
Async XLA Ops:
  6.5 1496.4 %all-gather.4.cloned.1.call-start = ((), (), s32[]{:S(2)}) async-start(), calls=%async_computation | async-start | bytes 12607488 | tf_op jit(solution)/shard_map/all_gather | solution.py:364
  7.6 22.2 %collective-permute-start = (f32[6,4,16,256]{3,2,1,0:T(8,128)S(1)}, f32[6,4,16,256]{3,2,1,0:T(8,128)S(1)}, u32[]{:S(2)}, u32[]{:S(2)}) collective-permute-start(f32[6,4,16,256]{3,2,1,0:T(8,128)S(1)} %pad_maximum_fusion.own_ref), channel_id=1, source_target_pairs={{0,2},{1,3},{2,4},{3,5},{4,6},{5,7},{6,8},{7,9},{8,10},{9,11},{10,... | collective-permute-start | bytes 1179656 | tf_op jit(solution)/shard_map/ppermute | solution.py:348
  12.1 26.4 %collective-permute-start.1 = (f32[6,4,16,256]{3,2,1,0:T(8,128)S(1)}, f32[6,4,16,256]{3,2,1,0:T(8,128)S(1)}, u32[]{:S(2)}, u32[]{:S(2)}) collective-permute-start(f32[6,4,16,256]{3,2,1,0:T(8,128)S(1)} %pad_maximum_fusion.own_ref), channel_id=1, source_target_pairs={{0,1},{1,2},{2,3},{3,4},{4,5},{5,6},{6,7},{7,8},{8,9},{9,10},{10,1... | collective-permute-start | bytes 1179656 | tf_op jit(solution)/shard_map/ppermute | solution.py:348
  14.4 24.1 %collective-permute-start.2 = (f32[6,4,16,256]{3,2,1,0:T(8,128)S(1)}, f32[6,4,16,256]{3,2,1,0:T(8,128)S(1)}, u32[]{:S(2)}, u32[]{:S(2)}) collective-permute-start(f32[6,4,16,256]{3,2,1,0:T(8,128)S(1)} %pad_maximum_fusion.own_ref), channel_id=1, source_target_pairs={{1,0},{2,1},{3,2},{4,3},{5,4},{6,5},{7,6},{8,7},{9,8},{10,9},{11,1... | collective-permute-start | bytes 1179656 | tf_op jit(solution)/shard_map/ppermute | solution.py:348
  17.4 21.1 %collective-permute-start.3 = (f32[6,4,16,256]{3,2,1,0:T(8,128)S(1)}, f32[6,4,16,256]{3,2,1,0:T(8,128)S(1)}, u32[]{:S(2)}, u32[]{:S(2)}) collective-permute-start(f32[6,4,16,256]{3,2,1,0:T(8,128)S(1)} %pad_maximum_fusion.own_ref), channel_id=1, source_target_pairs={{2,0},{3,1},{4,2},{5,3},{6,4},{7,5},{8,6},{9,7},{10,8},{11,9},{12,... | collective-permute-start | bytes 1179656 | tf_op jit(solution)/shard_map/ppermute | solution.py:348
  52.7 44.6 %collective-permute-start.4 = (f32[3,4,4,8,128]{4,3,2,1,0:T(8,128)S(1)}, f32[3,4,4,8,128]{4,3,2,1,0:T(8,128)S(1)}, u32[]{:S(2)}, u32[]{:S(2)}) collective-permute-start(f32[3,4,4,8,128]{4,3,2,1,0:T(8,128)S(1)} %get-tuple-element.10), channel_id=1, source_target_pairs={{0,16},{16,32},{32,48},{48,64},{64,80},{80,96},{96,112},{112,128},... | collective-permute-start | bytes 589832 | tf_op jit(solution)/shard_map/ppermute | solution.py:362
  88.2 9.2 collective-permute-start.5
  1502.9 4.6 copy-start
Sparse Core Ops, SparseCore 0:
  51.0 1451.9 all-gather.3

commit v2 on v1

v2 whole, which is shorter than its diff:
```python
import functools
import jax
import jax.numpy as jnp
from jax import lax
from jax.experimental import pallas as pl
from jax.experimental.pallas import tpu as pltpu
from jax.sharding import PartitionSpec as P

STEPS = 4
KAPPA = 0.04
FINE_UNROLL = 2
F32 = jnp.float32
HI = lax.Precision.HIGHEST
VM = pltpu.MemorySpace.VMEM


def lane_parity(transpose=False):
    row = lax.broadcasted_iota(jnp.int32, (256, 256), 1 if transpose else 0)
    col = lax.broadcasted_iota(jnp.int32, (256, 256), 0 if transpose else 1)
    want = 2 * (col % 128) + col // 128
    return (row == want).astype(F32)


def shift(v, by, axis, masked_at, index):
    return jnp.where(index == masked_at, 0.0, pltpu.roll(v, by % v.shape[axis], axis))


def stencil_terms(low, high, mid, inside):
    a = [KAPPA + jnp.maximum(mid[d], 0.0) for d in range(3)]
    b = [KAPPA - jnp.minimum(mid[d], 0.0) for d in range(3)]
    centre = 1.0 - (a[0] + b[0] + a[1] + b[1] + a[2] + b[2])
    m = [[(high[e][c] - low[e][c]) * 0.5 for e in range(3)] for c in range(3)]
    for c in range(3):
        m[c][c] = m[c][c] + centre
    a = [x * inside for x in a]
    b = [x * inside for x in b]
    m = [[x * inside for x in row] for row in m]
    return a, b, m


def iotas():
    sub = lax.broadcasted_iota(jnp.int32, (8, 128), 0)
    lane = lax.broadcasted_iota(jnp.int32, (8, 128), 1)
    return sub, lane


def coarse_coefs(below, here, above, inside, store):
    sub, lane = iotas()
    low = [below, [shift(v, 1, 0, 0, sub) for v in here], [shift(v, 1, 1, 0, lane) for v in here]]
    high = [above, [shift(v, -1, 0, 7, sub) for v in here], [shift(v, -1, 1, 127, lane) for v in here]]
    a, b, m = stencil_terms(low, high, here, inside)
    a[1] = jnp.where(sub == 0, 0.0, a[1])
    b[1] = jnp.where(sub == 7, 0.0, b[1])
    a[2] = jnp.where(lane == 0, 0.0, a[2])
    b[2] = jnp.where(lane == 127, 0.0, b[2])
    flat = a + b + m[0] + m[1] + m[2]
    for i, x in enumerate(flat):
        store(i, x)


def psi(coef, below, here, above):
    a = [coef(i) for i in range(3)]
    b = [coef(3 + i) for i in range(3)]
    out = []
    for c in range(3):
        w = here[c]
        acc = a[0] * below[c] + b[0] * above[c]
        acc = acc + (a[1] * pltpu.roll(w, 1, 0) + b[1] * pltpu.roll(w, 7, 0))
        acc = acc + (a[2] * pltpu.roll(w, 1, 1) + b[2] * pltpu.roll(w, 127, 1))
        acc = acc + (coef(6 + 3 * c) * here[0] + coef(7 + 3 * c) * here[1] + coef(8 + 3 * c) * here[2])
        out.append(acc)
    return out


NL = 12
VSPEC = pl.BlockSpec(memory_space=VM)
SSPEC = pl.BlockSpec(memory_space=pltpu.MemorySpace.SMEM)
GRANT = 40 << 20


def shaped(*dims):
    return jax.ShapeDtypeStruct(dims, F32)


def cost(flops, moved):
    return pl.CostEstimate(flops=flops, bytes_accessed=moved, transcendentals=0)


def march4(coefs, first, second, base):
    src, dst = first, second
    for k in range(1, STEPS + 1):
        def layer(l, carry, src=src, dst=dst):
            w = [[src[c, l, k] for k in range(4)] for c in range(3)]
            for q in range(2):
                for p in range(2):
                    k = 2 * q + p
                    kx = 2 * (1 - q) + p
                    ky = 2 * q + 1 - p
                    cf = [coefs[l, k, i] for i in range(15)]
                    for c in range(3):
                        xo = w[c][kx]
                        xr = pltpu.roll(xo, 7 if q else 1, 0)
                        yo = w[c][ky]
                        yr = pltpu.roll(yo, 127 if p else 1, 1)
                        acc = cf[0] * src[c, l - 1, k] + cf[3] * src[c, l + 1, k]
                        acc = acc + (cf[1] * (xo if q else xr) + cf[4] * (xr if q else xo))
                        acc = acc + (cf[2] * (yo if p else yr) + cf[5] * (yr if p else yo))
                        acc = acc + (cf[6 + 3 * c] * w[0][k] + cf[7 + 3 * c] * w[1][k] + cf[8 + 3 * c] * w[2][k])
                        dst[c, l, k] = acc
            return carry
        lax.fori_loop(k, NL - k, layer, 0, unroll=FINE_UNROLL)
        src, dst = dst, src


def restrict(src, j):
    out = []
    for c in range(3):
        lo = (src[c, 2 * j, 0] + src[c, 2 * j, 1]) + (src[c, 2 * j, 2] + src[c, 2 * j, 3])
        hi = (src[c, 2 * j + 1, 0] + src[c, 2 * j + 1, 1]) + (src[c, 2 * j + 1, 2] + src[c, 2 * j + 1, 3])
        out.append((lo + hi) * 0.125)
    return out


def fine1_kernel(pos_ref, m1_ref, own_ref, p1_ref, start_ref, after_ref, coefs, speed_c_ref,
                 state_a, state_b, speed, ev, od):
    slab = pos_ref[0]
    depth = pos_ref[2]
    perm = lane_parity()
    for i, ref in enumerate((m1_ref, own_ref, p1_ref)):
        rows = ref[...].reshape(384, 256)
        both = jnp.dot(rows, perm, precision=HI, preferred_element_type=F32)
        ev[...] = both[:, :128]
        od[...] = both[:, 128:]
        for part, dest in ((0, state_a), (1, speed)):
            for q in range(2):
                for p, half in ((0, ev), (1, od)):
                    got = half[pl.ds(192 * part + q, 96, stride=2), :]
                    dest[:, 4 * i:4 * i + 4, 2 * q + p] = got.reshape(3, 4, 8, 128)
    start_ref[...] = state_a[...]
    sub, lane = iotas()

    def build(l, carry):
        z = slab * 4 + l - 4
        inside = jnp.where(jnp.logical_and(z >= 0, z < depth), 1.0, 0.0).astype(F32)
        mid = [[speed[c, l, k] for c in range(3)] for k in range(4)]
        for q in range(2):
            for p in range(2):
                k = 2 * q + p
                here = mid[k]
                xo = mid[2 * (1 - q) + p]
                yo = mid[2 * q + 1 - p]
                low_z = [speed[c, l - 1, k] for c in range(3)]
                high_z = [speed[c, l + 1, k] for c in range(3)]
                low_x = xo if q else [shift(v, 1, 0, 0, sub) for v in xo]
                high_x = [shift(v, -1, 0, 7, sub) for v in xo] if q else xo
                low_y = yo if p else [shift(v, 1, 1, 0, lane) for v in yo]
                high_y = [shift(v, -1, 1, 127, lane) for v in yo] if p else yo
                a, b, m = stencil_terms([low_z, low_x, low_y], [high_z, high_x, high_y], here, inside)
                if q:
                    b[1] = jnp.where(sub == 7, 0.0, b[1])
                else:
                    a[1] = jnp.where(sub == 0, 0.0, a[1])
                if p:
                    b[2] = jnp.where(lane == 127, 0.0, b[2])
                else:
                    a[2] = jnp.where(lane == 0, 0.0, a[2])
                for i, x in enumerate(a + b + m[0] + m[1] + m[2]):
                    coefs[l, k, i] = x
        return carry

    lax.fori_loop(1, NL - 1, build, 0)
    for j in range(1, 5):
        for c, v in enumerate(restrict(speed, j)):
            speed_c_ref[j - 1, c] = 2.0 * v
    march4(coefs, state_a, state_b, 0)
    after_ref[...] = state_a[:, 4:8]


def fine1(pos, m1, own, p1):
    return pl.pallas_call(
        fine1_kernel,
        out_shape=(shaped(3, NL, 4, 8, 128), shaped(3, 4, 4, 8, 128), shaped(NL, 4, 15, 8, 128), shaped(4, 3, 8, 128)),
        in_specs=[SSPEC] + [VSPEC] * 3,
        out_specs=(VSPEC,) * 4,
        scratch_shapes=[pltpu.VMEM((3, NL, 4, 8, 128), F32)] * 3 + [pltpu.VMEM((384, 128), F32)] * 2,
        compiler_params=pltpu.CompilerParams(vmem_limit_bytes=GRANT),
        cost_estimate=cost(10_000_000, 6_000_000),
        name="fine1",
    )(pos, m1, own, p1)


def fine2_kernel(pos_ref, coefs, speed_c, start_ref, m1_ref, own_ref, p1_ref, relaxed_ref, share_ref, state_a, state_b):
    slab = pos_ref[0]
    first = pos_ref[1] == 1
    depth = pos_ref[2]
    for i, ref in enumerate((m1_ref, own_ref, p1_ref)):
        for dz in range(4):
            l = 4 * i + dz
            for c in range(3):
                for k in range(4):
                    state_a[c, l, k] = jnp.where(first, start_ref[c, l, k], ref[c, dz, k])
    relaxed_ref[...] = state_a[:, 4:8]
    coarse = {j: restrict(state_a, j) for j in range(1, 5)}
    image = {}
    for j in (2, 3):
        cc = {}
        coarse_coefs(*[[speed_c[i, c] for c in range(3)] for i in (j - 2, j - 1, j)], jnp.float32(1.0), cc.__setitem__)
        image[j] = psi(cc.__getitem__, coarse[j - 1], coarse[j], coarse[j + 1])
    march4(coefs, state_a, state_b, 0)
    for i, j in enumerate((2, 3)):
        again = restrict(state_a, j)
        for c in range(3):
            forcing = again[c] - image[j][c]
            forcing = forcing + jnp.where(first, image[j][c], 0.0)
            for s in range(share_ref.shape[0]):
                share_ref[s, 0, i, c] = forcing
                share_ref[s, 1, i, c] = speed_c[j - 1, c]


def fine2(pos, coefs, speed_c, start, m1, own, p1, slabs):
    return pl.pallas_call(
        fine2_kernel,
        out_shape=(shaped(3, 4, 4, 8, 128), shaped(slabs, 2, 2, 3, 8, 128)),
        in_specs=[SSPEC] + [VSPEC] * 6,
        out_specs=(VSPEC,) * 2,
        scratch_shapes=[pltpu.VMEM((3, NL, 4, 8, 128), F32)] * 2,
        compiler_params=pltpu.CompilerParams(vmem_limit_bytes=GRANT),
        cost_estimate=cost(10_000_000, 6_000_000),
        name="fine2",
    )(pos, coefs, speed_c, start, m1, own, p1)


def coefs_kernel(speed_ref, coefs):
    layers = speed_ref.shape[0]

    def one(j, carry):
        def at(i):
            keep = jnp.where(jnp.logical_and(i >= 0, i < layers), 1.0, 0.0).astype(F32)
            k = jnp.clip(i, 0, layers - 1)
            return [speed_ref[k, c] * keep for c in range(3)]

        def store(i, x):
            coefs[j, i] = x
        coarse_coefs(at(j - 1), at(j), at(j + 1), jnp.float32(1.0), store)
        return carry
    lax.fori_loop(0, layers, one, 0, unroll=2)


def sweep_coefs(speed):
    return pl.pallas_call(
        coefs_kernel,
        out_shape=shaped(speed.shape[0], 15, 8, 128),
        in_specs=[VSPEC],
        out_specs=VSPEC,
        compiler_params=pltpu.CompilerParams(vmem_limit_bytes=GRANT),
        cost_estimate=cost(3_000_000, 2_400_000),
        name="coefs",
    )(speed)


CHUNK = 4


def window(slab, halo, layers):
    count = min(layers, 2 + 2 * halo)
    return count, jnp.clip(2 * slab - halo, 0, layers - count)


def psi_steps(coefs, src, dst, slab, halo, steps):
    layers = coefs.shape[0]
    for s in range(steps):
        reach = halo + steps - 1 - s
        low = jnp.maximum(2 * slab - reach, 0) // CHUNK
        high = (jnp.minimum(2 * slab + 2 + reach, layers) + CHUNK - 1) // CHUNK
        src, dst = psi_step(coefs, src, dst, low, high)
    return src


def psi_step(coefs, src, dst, low, high):
    def some(i, carry):
        for dj in range(CHUNK):
            j = i * CHUNK + dj
            new = psi(lambda n: coefs[j, n],
                      [src[j, c] for c in range(3)],
                      [src[j + 1, c] for c in range(3)],
                      [src[j + 2, c] for c in range(3)])
            for c in range(3):
                dst[j + 1, c] = new[c]
        return carry
    lax.fori_loop(low, high, some, 0)
    return dst, src


def round_kernel(distance, halo_own, halo_out, pos_ref, coefs, own_ref, got_ref, out_ref, state_a, state_b):
    slab = pos_ref[0]
    layers = coefs.shape[0]
    n_got, at_got = window(slab, halo_out + distance, layers)
    n_own, at_own = window(slab, halo_own, layers)
    n_out, at_out = window(slab, halo_out, layers)
    for ref in (state_a, state_b):
        ref[0] = jnp.zeros((3, 8, 128), F32)
        ref[layers + 1] = jnp.zeros((3, 8, 128), F32)
    state_a[pl.ds(at_got + 1, n_got)] = got_ref[...]
    if distance >= 4:
        def pair(i, carry):
            reach = halo_out + distance - 1 - 2 * i

            def span(r):
                low = jnp.maximum(2 * slab - r, 0) // CHUNK
                return low, (jnp.minimum(2 * slab + 2 + r, layers) + CHUNK - 1) // CHUNK
            psi_step(coefs, state_a, state_b, *span(reach))
            psi_step(coefs, state_b, state_a, *span(reach - 1))
            return carry
        lax.fori_loop(0, distance // 2, pair, 0)
        last = state_a
    else:
        last = psi_steps(coefs, state_a, state_b, slab, halo_out, distance)
    out_ref[...] = last[pl.ds(at_out + 1, n_out)] + own_ref[pl.ds(at_out - at_own, n_out)]


def sweep_round(distance, halo_own, halo_out, pos, coefs, own, got):
    layers = coefs.shape[0]
    count = min(layers, 2 + 2 * halo_out)
    return pl.pallas_call(
        functools.partial(round_kernel, distance, halo_own, halo_out),
        out_shape=shaped(count, 3, 8, 128),
        in_specs=[SSPEC] + [VSPEC] * 3,
        out_specs=VSPEC,
        scratch_shapes=[pltpu.VMEM((layers + 2, 3, 8, 128), F32)] * 2,
        compiler_params=pltpu.CompilerParams(vmem_limit_bytes=GRANT),
        cost_estimate=cost(distance * 2_000_000, 3_000_000),
        name=f"round{distance}",
    )(pos, coefs, own, got)


def last_kernel(pos_ref, coefs, relaxed_ref, near_ref, far_ref, out_ref, state_a, ev, od):
    slab = pos_ref[0]
    first = pos_ref[1] == 1
    layers = coefs.shape[0]
    n_got, at_got = window(slab, 1, layers)
    state_a[0] = jnp.zeros((3, 8, 128), F32)
    state_a[layers + 1] = jnp.zeros((3, 8, 128), F32)
    state_a[pl.ds(at_got + 1, n_got)] = far_ref[...]
    for zc in range(2):
        j = 2 * slab + zc
        new = psi(lambda n: coefs[j, n], *[[state_a[j + d, c] for c in range(3)] for d in range(3)])
        for c in range(3):
            coarse = new[c] + near_ref[j - at_got, c]
            w = [[relaxed_ref[c, 2 * zc + dz, k] for k in range(4)] for dz in range(2)]
            lo, hi = [(v[0] + v[1]) + (v[2] + v[3]) for v in w]
            mean = (lo + hi) * 0.125
            diff = jnp.where(first, mean, coarse) - mean
            for dz in range(2):
                row0 = (c * 4 + 2 * zc + dz) * 16
                for q in range(2):
                    ev[pl.ds(row0 + q, 8, stride=2), :] = w[dz][2 * q] + diff
                    od[pl.ds(row0 + q, 8, stride=2), :] = w[dz][2 * q + 1] + diff
    both = jnp.concatenate([ev[...], od[...]], axis=1)
    out = jnp.dot(both, lane_parity(True), precision=HI, preferred_element_type=F32)
    out_ref[...] = out.reshape(3, 4, 16, 256)


def sweep_last(pos, coefs, relaxed, near, far):
    layers = coefs.shape[0]
    return pl.pallas_call(
        last_kernel,
        out_shape=shaped(3, 4, 16, 256),
        in_specs=[SSPEC] + [VSPEC] * 4,
        out_specs=VSPEC,
        scratch_shapes=[pltpu.VMEM((layers + 2, 3, 8, 128), F32)] + [pltpu.VMEM((192, 128), F32)] * 2,
        compiler_params=pltpu.CompilerParams(vmem_limit_bytes=GRANT),
        cost_estimate=cost(2_000_000, 3_000_000),
        name="last",
    )(pos, coefs, relaxed, near, far)


def moved(block, by_t, by_z):
    nt, nz = lax.axis_size("tm"), lax.axis_size("gz")
    route = [
        ((t - by_t) * nz + z - by_z, t * nz + z)
        for t in range(nt) for z in range(nz)
        if 0 <= t - by_t < nt and 0 <= z - by_z < nz
    ]
    return lax.ppermute(block, ("tm", "gz"), route)


def local(c_states, velocity):
    slab = lax.axis_index("gz")
    t = lax.axis_index("tm")
    slabs = lax.axis_size("gz")
    depth = slabs * velocity.shape[1]
    pos = jnp.stack([slab, (t == 0).astype(jnp.int32), jnp.int32(depth)])
    own = jnp.concatenate([c_states[0], velocity], axis=0)
    start, after, coefs, speed_c = fine1(pos, moved(own, 0, 1), own, moved(own, 0, -1))
    m1, same, p1 = [moved(after, 1, by) for by in (1, 0, -1)]
    relaxed, share = fine2(pos, coefs, speed_c, start, m1, same, p1, slabs)
    share = lax.all_to_all(share, "gz", 0, 0, tiled=True)
    state = share[:, 0].reshape(2 * slabs, 3, 8, 128)
    coefs = sweep_coefs(share[:, 1].reshape(2 * slabs, 3, 8, 128))
    halo_own = slabs * 2
    for distance in (16, 8, 4, 2):
        state = sweep_round(distance, halo_own, distance - 1, pos, coefs, state, moved(state, distance, 0))
        halo_own = distance - 1
    out = sweep_last(pos, coefs, relaxed, moved(state, 1, 0), moved(state, 2, 0))
    return out[None]


def solution(mesh):
    return jax.shard_map(
        local,
        mesh=mesh,
        in_specs=(P("tm", None, "gz", None, None), P(None, "gz", None, None)),
        out_specs=P("tm", None, "gz", None, None),
        check_vma=False,
    )
```

time: 1600 us -> 168 us (0.10)
  the two profiles are of different devices: /device:TPU:27 before, /device:TPU:206 now
where the time goes in v2:
time: 168 us
  starting transfers between devices  56.4 us (34%)
  waiting for transfers between devices  52.3 us (31%)
  Pallas kernels  31.4 us (19%)
  blocking collectives  26.5 us (16%)
    ppermute x11, starting transfers between devices, moved(): return lax.ppermute(block, ('tm', 'gz'), route)  56.4 us
    ppermute x11, waiting for transfers between devices, moved(): return lax.ppermute(block, ('tm', 'gz'), route)  52.3 us
    all_to_all x1, blocking collectives, local(): share = lax.all_to_all(share, 'gz', 0, 0, tiled=True)  26.5 us
    pallas_call x4, Pallas kernels, sweep_round(): pl.pallas_call(functools.partial(round_kernel, distance, halo_own, halo_o...  22.1 us
    pallas_call x1, Pallas kernels, fine1(): pl.pallas_call(fine1_kernel, out_shape=(shaped(3, NL, 4, 8, 128), shaped(...  4.14 us
  transfers between devices with their start and end apart: 11, of which 9 were waited for; matrix products, arithmetic and copies ran while one was open for 0% of the time, Pallas kernels for 1%

profile of v2, /device:TPU:206, one launch (start us, length us, event | category | flops | bytes accessed | tf_op | source)
XLA Modules:
  0.0 168.0 jit_solution(12206159340732879261)
XLA Ops:
  0.0 1.0 pad_maximum_fusion.own_ref
  1.1 2.4 %collective-permute-start.1 = (f32[6,4,16,256]{3,2,1,0:T(8,128)S(1)}, f32[6,4,16,256]{3,2,1,0:T(8,128)S(1)}, u32[]{:S(2)}, u32[]{:S(2)}) collective-permute-start(f32[6,4,16,256]{3,2,1,0:T(8,128)S(1)} %pad_maximum_fusion.own_ref), channel_id=1, source_target_pairs={{1,0},{2,1},{3,2},{4,3},{5,4},{6,5},{7,6},{8,7},{9,8},{10,9},{11,1... | collective-permute-start | bytes 1179656 | tf_op jit(solution)/shard_map/ppermute | solution.py:384
  3.4 3.5 %collective-permute-start = (f32[6,4,16,256]{3,2,1,0:T(8,128)S(1)}, f32[6,4,16,256]{3,2,1,0:T(8,128)S(1)}, u32[]{:S(2)}, u32[]{:S(2)}) collective-permute-start(f32[6,4,16,256]{3,2,1,0:T(8,128)S(1)} %pad_maximum_fusion.own_ref), channel_id=1, source_target_pairs={{0,1},{1,2},{2,3},{3,4},{4,5},{5,6},{6,7},{7,8},{8,9},{9,10},{10,1... | collective-permute-start | bytes 1179656 | tf_op jit(solution)/shard_map/ppermute | solution.py:384
  6.9 0.1 pad_add_fusion.pos_ref
  7.0 6.8 %collective-permute-done.1.p1_ref = f32[6,4,16,256]{3,2,1,0:T(8,128)S(1)} collective-permute-done((f32[6,4,16,256]{3,2,1,0:T(8,128)S(1)}, f32[6,4,16,256]{3,2,1,0:T(8,128)S(1)}, u32[]{:S(2)}, u32[]{:S(2)}) %collective-permute-start.1) | collective-permute-done | bytes 393248 | tf_op jit(solution)/shard_map/ppermute | solution.py:384
  13.8 4.1 %collective-permute-done.m1_ref = f32[6,4,16,256]{3,2,1,0:T(8,128)S(1)} collective-permute-done((f32[6,4,16,256]{3,2,1,0:T(8,128)S(1)}, f32[6,4,16,256]{3,2,1,0:T(8,128)S(1)}, u32[]{:S(2)}, u32[]{:S(2)}) %collective-permute-start) | collective-permute-done | bytes 393248 | tf_op jit(solution)/shard_map/ppermute | solution.py:384
  17.9 4.1 %fine1.1 = (f32[3,12,4,8,128]{4,3,2,1,0:T(8,128)S(1)}, f32[3,4,4,8,128]{4,3,2,1,0:T(8,128)S(1)}, f32[12,4,15,8,128]{4,3,2,1,0:T(8,128)S(1)}, f32[4,3,8,128]{3,2,1,0:T(8,128)S(1)}) custom-call(s32[3]{0:T(128)S(1)} %pad_add_fusion.pos_ref, f32[6,4,16,256]{3,2,1,0:T(8,128)S(1)} %collective-permute-done.m1_ref, f32[6,4,16,256]{3,2,1,0:T(8,128)S(1)} %pad_maximum_fusion.own_ref, ...), custom_call_target="tpu_custom_call" | custom-call | flops 10000000 | bytes 6000000 | tf_op jit(solution)/shard_map/fine1/pallas_call | solution.py:180
  22.0 4.1 %collective-permute-start.4 = (f32[3,4,4,8,128]{4,3,2,1,0:T(8,128)S(1)}, f32[3,4,4,8,128]{4,3,2,1,0:T(8,128)S(1)}, u32[]{:S(2)}, u32[]{:S(2)}) collective-permute-start(f32[3,4,4,8,128]{4,3,2,1,0:T(8,128)S(1)} %get-tuple-element.14), channel_id=1, source_target_pairs={{1,16},{2,17},{3,18},{4,19},{5,20},{6,21},{7,22},{8,23},{9,24},{10... | collective-permute-start | bytes 589832 | tf_op jit(solution)/shard_map/ppermute | solution.py:384
  26.1 7.3 %collective-permute-start.3 = (f32[3,4,4,8,128]{4,3,2,1,0:T(8,128)S(1)}, f32[3,4,4,8,128]{4,3,2,1,0:T(8,128)S(1)}, u32[]{:S(2)}, u32[]{:S(2)}) collective-permute-start(f32[3,4,4,8,128]{4,3,2,1,0:T(8,128)S(1)} %get-tuple-element.14), channel_id=1, source_target_pairs={{0,16},{1,17},{2,18},{3,19},{4,20},{5,21},{6,22},{7,23},{8,24},{9,... | collective-permute-start | bytes 589832 | tf_op jit(solution)/shard_map/ppermute | solution.py:384
  33.4 1.9 %collective-permute-start.2 = (f32[3,4,4,8,128]{4,3,2,1,0:T(8,128)S(1)}, f32[3,4,4,8,128]{4,3,2,1,0:T(8,128)S(1)}, u32[]{:S(2)}, u32[]{:S(2)}) collective-permute-start(f32[3,4,4,8,128]{4,3,2,1,0:T(8,128)S(1)} %get-tuple-element.14), channel_id=1, source_target_pairs={{0,17},{1,18},{2,19},{3,20},{4,21},{5,22},{6,23},{7,24},{8,25},{9,... | collective-permute-start | bytes 589832 | tf_op jit(solution)/shard_map/ppermute | solution.py:384
  35.3 0.0 collective-permute-done.4.p1_ref
  35.3 0.4 collective-permute-done.3.own_ref
  35.7 7.0 %collective-permute-done.2.m1_ref = f32[3,4,4,8,128]{4,3,2,1,0:T(8,128)S(1)} collective-permute-done((f32[3,4,4,8,128]{4,3,2,1,0:T(8,128)S(1)}, f32[3,4,4,8,128]{4,3,2,1,0:T(8,128)S(1)}, u32[]{:S(2)}, u32[]{:S(2)}) %collective-permute-start.2) | collective-permute-done | bytes 196640 | tf_op jit(solution)/shard_map/ppermute | solution.py:384
  42.8 2.2 %fine2.1 = (f32[3,4,4,8,128]{4,3,2,1,0:T(8,128)S(1)}, f32[16,2,2,3,8,128]{5,4,3,2,1,0:T(8,128)S(1)}) custom-call(s32[3]{0:T(128)S(1)} %pad_add_fusion.pos_ref, f32[12,4,15,8,128]{4,3,2,1,0:T(8,128)S(1)} %get-tuple-element.11.coefs, f32[4,3,8,128]{3,2,1,0:T(8,128)S(1)} %get-tuple-element.12.speed_c, f32[3,12,4,8,128]{4,3,2,1,0:T(8,128)S(1)} %get-tuple-element.13.start_ref, ...), custom_call_target="tpu_custom_call" | custom-call | flops 10000000 | bytes 6000000 | tf_op jit(solution)/shard_map/fine2/pallas_call | solution.py:221
  45.0 26.5 %all_to_all.5 = f32[16,2,2,3,8,128]{5,4,3,2,1,0:T(8,128)S(1)} all-to-all(f32[16,2,2,3,8,128]{5,4,3,2,1,0:T(8,128)S(1)} %get-tuple-element.15), channel_id=1, replica_groups=mesh['tm'=32,'gz'=16] {'gz'}, dimensions={0} | all-to-all | bytes 1572864 | tf_op jit(solution)/shard_map/all_to_all | solution.py:397
  71.5 0.1 fusion
  71.5 1.3 collective-permute-start.5
  72.9 1.4 coefs.1
  74.2 5.8 %collective-permute-done.5.got_ref = f32[32,3,8,128]{3,2,1,0:T(8,128)S(1)} collective-permute-done((f32[32,3,8,128]{3,2,1,0:T(8,128)S(1)}, f32[32,3,8,128]{3,2,1,0:T(8,128)S(1)}, u32[]{:S(2)}, u32[]{:S(2)}) %collective-permute-start.5) | collective-permute-done | bytes 393248 | tf_op jit(solution)/shard_map/ppermute | solution.py:384
  80.1 13.5 %round16.1.own_ref = f32[32,3,8,128]{3,2,1,0:T(8,128)S(1)} custom-call(s32[3]{0:T(128)S(1)} %pad_add_fusion.pos_ref, f32[32,15,8,128]{3,2,1,0:T(8,128)S(1)} %coefs.1, f32[32,3,8,128]{3,2,1,0:T(8,128)S(1)} %bitcast.8, f32[32,3,8,128]{3,2,1,0:T(8,128)S(1)} %collective-permute-done.5.got_ref), custom_call_target="tpu_custom_call" | custom-call | flops 32000000 | bytes 3000000 | tf_op jit(solution)/shard_map/round16/pallas_call | solution.py:324
  93.6 16.7 %collective-permute-start.6 = (f32[32,3,8,128]{3,2,1,0:T(8,128)S(1)}, f32[32,3,8,128]{3,2,1,0:T(8,128)S(1)}, u32[]{:S(2)}, u32[]{:S(2)}) collective-permute-start(f32[32,3,8,128]{3,2,1,0:T(8,128)S(1)} %round16.1.own_ref), channel_id=1, source_target_pairs={{0,128},{1,129},{2,130},{3,131},{4,132},{5,133},{6,134},{7,135},{8... | collective-permute-start | bytes 1179656 | tf_op jit(solution)/shard_map/ppermute | solution.py:384
  110.3 16.9 %collective-permute-done.6.got_ref = f32[32,3,8,128]{3,2,1,0:T(8,128)S(1)} collective-permute-done((f32[32,3,8,128]{3,2,1,0:T(8,128)S(1)}, f32[32,3,8,128]{3,2,1,0:T(8,128)S(1)}, u32[]{:S(2)}, u32[]{:S(2)}) %collective-permute-start.6) | collective-permute-done | bytes 393248 | tf_op jit(solution)/shard_map/ppermute | solution.py:384
  127.2 5.6 %round8.1.own_ref = f32[16,3,8,128]{3,2,1,0:T(8,128)S(1)} custom-call(s32[3]{0:T(128)S(1)} %pad_add_fusion.pos_ref, f32[32,15,8,128]{3,2,1,0:T(8,128)S(1)} %coefs.1, f32[32,3,8,128]{3,2,1,0:T(8,128)S(1)} %round16.1.own_ref, f32[32,3,8,128]{3,2,1,0:T(8,128)S(1)} %collective-permute-done.6.got_ref), custom_call_target="tpu_custom_call" | custom-call | flops 16000000 | bytes 3000000 | tf_op jit(solution)/shard_map/round8/pallas_call | solution.py:324
  132.9 5.4 %collective-permute-start.7 = (f32[16,3,8,128]{3,2,1,0:T(8,128)S(1)}, f32[16,3,8,128]{3,2,1,0:T(8,128)S(1)}, u32[]{:S(2)}, u32[]{:S(2)}) collective-permute-start(f32[16,3,8,128]{3,2,1,0:T(8,128)S(1)} %round8.1.own_ref), channel_id=1, source_target_pairs={{0,64},{1,65},{2,66},{3,67},{4,68},{5,69},{6,70},{7,71},{8,72},{9,... | collective-permute-start | bytes 589832 | tf_op jit(solution)/shard_map/ppermute | solution.py:384
  138.3 3.2 %collective-permute-done.7.got_ref = f32[16,3,8,128]{3,2,1,0:T(8,128)S(1)} collective-permute-done((f32[16,3,8,128]{3,2,1,0:T(8,128)S(1)}, f32[16,3,8,128]{3,2,1,0:T(8,128)S(1)}, u32[]{:S(2)}, u32[]{:S(2)}) %collective-permute-start.7) | collective-permute-done | bytes 196640 | tf_op jit(solution)/shard_map/ppermute | solution.py:384
  141.5 2.0 %round4.1.own_ref = f32[8,3,8,128]{3,2,1,0:T(8,128)S(1)} custom-call(s32[3]{0:T(128)S(1)} %pad_add_fusion.pos_ref, f32[32,15,8,128]{3,2,1,0:T(8,128)S(1)} %coefs.1, f32[16,3,8,128]{3,2,1,0:T(8,128)S(1)} %round8.1.own_ref, f32[16,3,8,128]{3,2,1,0:T(8,128)S(1)} %collective-permute-done.7.got_ref), custom_call_target="tpu_custom_call" | custom-call | flops 8000000 | bytes 3000000 | tf_op jit(solution)/shard_map/round4/pallas_call | solution.py:324
  143.5 4.9 %collective-permute-start.8 = (f32[8,3,8,128]{3,2,1,0:T(8,128)S(1)}, f32[8,3,8,128]{3,2,1,0:T(8,128)S(1)}, u32[]{:S(2)}, u32[]{:S(2)}) collective-permute-start(f32[8,3,8,128]{3,2,1,0:T(8,128)S(1)} %round4.1.own_ref), channel_id=1, source_target_pairs={{0,32},{1,33},{2,34},{3,35},{4,36},{5,37},{6,38},{7,39},{8,40},{9,... | collective-permute-start | bytes 294920 | tf_op jit(solution)/shard_map/ppermute | solution.py:384
  148.4 3.1 %collective-permute-done.8.got_ref = f32[8,3,8,128]{3,2,1,0:T(8,128)S(1)} collective-permute-done((f32[8,3,8,128]{3,2,1,0:T(8,128)S(1)}, f32[8,3,8,128]{3,2,1,0:T(8,128)S(1)}, u32[]{:S(2)}, u32[]{:S(2)}) %collective-permute-start.8) | collective-permute-done | bytes 98336 | tf_op jit(solution)/shard_map/ppermute | solution.py:384
  151.5 1.0 round2.1
  152.5 7.0 %collective-permute-start.10 = (f32[4,3,8,128]{3,2,1,0:T(8,128)S(1)}, f32[4,3,8,128]{3,2,1,0:T(8,128)S(1)}, u32[]{:S(2)}, u32[]{:S(2)}) collective-permute-start(f32[4,3,8,128]{3,2,1,0:T(8,128)S(1)} %round2.1), channel_id=1, source_target_pairs={{0,32},{1,33},{2,34},{3,35},{4,36},{5,37},{6,38},{7,39},{8,40},{9,... | collective-permute-start | bytes 147464 | tf_op jit(solution)/shard_map/ppermute | solution.py:384
  159.5 1.9 %collective-permute-start.9 = (f32[4,3,8,128]{3,2,1,0:T(8,128)S(1)}, f32[4,3,8,128]{3,2,1,0:T(8,128)S(1)}, u32[]{:S(2)}, u32[]{:S(2)}) collective-permute-start(f32[4,3,8,128]{3,2,1,0:T(8,128)S(1)} %round2.1), channel_id=1, source_target_pairs={{0,16},{1,17},{2,18},{3,19},{4,20},{5,21},{6,22},{7,23},{8,24},{9,... | collective-permute-start | bytes 147464 | tf_op jit(solution)/shard_map/ppermute | solution.py:384
  161.4 0.0 collective-permute-done.10.far_ref
  161.4 5.0 %collective-permute-done.9.near_ref = f32[4,3,8,128]{3,2,1,0:T(8,128)S(1)} collective-permute-done((f32[4,3,8,128]{3,2,1,0:T(8,128)S(1)}, f32[4,3,8,128]{3,2,1,0:T(8,128)S(1)}, u32[]{:S(2)}, u32[]{:S(2)}) %collective-permute-start.9) | collective-permute-done | bytes 49184 | tf_op jit(solution)/shard_map/ppermute | solution.py:384
  166.4 1.6 last.1
Async XLA Ops:
  1.1 12.7 %collective-permute-start.1 = (f32[6,4,16,256]{3,2,1,0:T(8,128)S(1)}, f32[6,4,16,256]{3,2,1,0:T(8,128)S(1)}, u32[]{:S(2)}, u32[]{:S(2)}) collective-permute-start(f32[6,4,16,256]{3,2,1,0:T(8,128)S(1)} %pad_maximum_fusion.own_ref), channel_id=1, source_target_pairs={{1,0},{2,1},{3,2},{4,3},{5,4},{6,5},{7,6},{8,7},{9,8},{10,9},{11,1... | collective-permute-start | bytes 1179656 | tf_op jit(solution)/shard_map/ppermute | solution.py:384
  3.4 14.5 %collective-permute-start = (f32[6,4,16,256]{3,2,1,0:T(8,128)S(1)}, f32[6,4,16,256]{3,2,1,0:T(8,128)S(1)}, u32[]{:S(2)}, u32[]{:S(2)}) collective-permute-start(f32[6,4,16,256]{3,2,1,0:T(8,128)S(1)} %pad_maximum_fusion.own_ref), channel_id=1, source_target_pairs={{0,1},{1,2},{2,3},{3,4},{4,5},{5,6},{6,7},{7,8},{8,9},{9,10},{10,1... | collective-permute-start | bytes 1179656 | tf_op jit(solution)/shard_map/ppermute | solution.py:384
  22.0 13.3 %collective-permute-start.4 = (f32[3,4,4,8,128]{4,3,2,1,0:T(8,128)S(1)}, f32[3,4,4,8,128]{4,3,2,1,0:T(8,128)S(1)}, u32[]{:S(2)}, u32[]{:S(2)}) collective-permute-start(f32[3,4,4,8,128]{4,3,2,1,0:T(8,128)S(1)} %get-tuple-element.14), channel_id=1, source_target_pairs={{1,16},{2,17},{3,18},{4,19},{5,20},{6,21},{7,22},{8,23},{9,24},{10... | collective-permute-start | bytes 589832 | tf_op jit(solution)/shard_map/ppermute | solution.py:384
  26.1 9.6 %collective-permute-start.3 = (f32[3,4,4,8,128]{4,3,2,1,0:T(8,128)S(1)}, f32[3,4,4,8,128]{4,3,2,1,0:T(8,128)S(1)}, u32[]{:S(2)}, u32[]{:S(2)}) collective-permute-start(f32[3,4,4,8,128]{4,3,2,1,0:T(8,128)S(1)} %get-tuple-element.14), channel_id=1, source_target_pairs={{0,16},{1,17},{2,18},{3,19},{4,20},{5,21},{6,22},{7,23},{8,24},{9,... | collective-permute-start | bytes 589832 | tf_op jit(solution)/shard_map/ppermute | solution.py:384
  33.4 9.4 %collective-permute-start.2 = (f32[3,4,4,8,128]{4,3,2,1,0:T(8,128)S(1)}, f32[3,4,4,8,128]{4,3,2,1,0:T(8,128)S(1)}, u32[]{:S(2)}, u32[]{:S(2)}) collective-permute-start(f32[3,4,4,8,128]{4,3,2,1,0:T(8,128)S(1)} %get-tuple-element.14), channel_id=1, source_target_pairs={{0,17},{1,18},{2,19},{3,20},{4,21},{5,22},{6,23},{7,24},{8,25},{9,... | collective-permute-start | bytes 589832 | tf_op jit(solution)/shard_map/ppermute | solution.py:384
  71.5 8.5 %collective-permute-start.5 = (f32[32,3,8,128]{3,2,1,0:T(8,128)S(1)}, f32[32,3,8,128]{3,2,1,0:T(8,128)S(1)}, u32[]{:S(2)}, u32[]{:S(2)}) collective-permute-start(f32[32,3,8,128]{3,2,1,0:T(8,128)S(1)} %bitcast.7), channel_id=1, source_target_pairs={{0,256},{1,257},{2,258},{3,259},{4,260},{5,261},{6,262},{7,263},{8... | collective-permute-start | bytes 1179656 | tf_op jit(solution)/shard_map/ppermute | solution.py:384
  93.6 33.6 %collective-permute-start.6 = (f32[32,3,8,128]{3,2,1,0:T(8,128)S(1)}, f32[32,3,8,128]{3,2,1,0:T(8,128)S(1)}, u32[]{:S(2)}, u32[]{:S(2)}) collective-permute-start(f32[32,3,8,128]{3,2,1,0:T(8,128)S(1)} %round16.1.own_ref), channel_id=1, source_target_pairs={{0,128},{1,129},{2,130},{3,131},{4,132},{5,133},{6,134},{7,135},{8... | collective-permute-start | bytes 1179656 | tf_op jit(solution)/shard_map/ppermute | solution.py:384
  132.9 8.6 %collective-permute-start.7 = (f32[16,3,8,128]{3,2,1,0:T(8,128)S(1)}, f32[16,3,8,128]{3,2,1,0:T(8,128)S(1)}, u32[]{:S(2)}, u32[]{:S(2)}) collective-permute-start(f32[16,3,8,128]{3,2,1,0:T(8,128)S(1)} %round8.1.own_ref), channel_id=1, source_target_pairs={{0,64},{1,65},{2,66},{3,67},{4,68},{5,69},{6,70},{7,71},{8,72},{9,... | collective-permute-start | bytes 589832 | tf_op jit(solution)/shard_map/ppermute | solution.py:384
  143.5 8.0 %collective-permute-start.8 = (f32[8,3,8,128]{3,2,1,0:T(8,128)S(1)}, f32[8,3,8,128]{3,2,1,0:T(8,128)S(1)}, u32[]{:S(2)}, u32[]{:S(2)}) collective-permute-start(f32[8,3,8,128]{3,2,1,0:T(8,128)S(1)} %round4.1.own_ref), channel_id=1, source_target_pairs={{0,32},{1,33},{2,34},{3,35},{4,36},{5,37},{6,38},{7,39},{8,40},{9,... | collective-permute-start | bytes 294920 | tf_op jit(solution)/shard_map/ppermute | solution.py:384
  152.5 8.9 %collective-permute-start.10 = (f32[4,3,8,128]{3,2,1,0:T(8,128)S(1)}, f32[4,3,8,128]{3,2,1,0:T(8,128)S(1)}, u32[]{:S(2)}, u32[]{:S(2)}) collective-permute-start(f32[4,3,8,128]{3,2,1,0:T(8,128)S(1)} %round2.1), channel_id=1, source_target_pairs={{0,32},{1,33},{2,34},{3,35},{4,36},{5,37},{6,38},{7,39},{8,40},{9,... | collective-permute-start | bytes 147464 | tf_op jit(solution)/shard_map/ppermute | solution.py:384
  159.5 6.9 %collective-permute-start.9 = (f32[4,3,8,128]{3,2,1,0:T(8,128)S(1)}, f32[4,3,8,128]{3,2,1,0:T(8,128)S(1)}, u32[]{:S(2)}, u32[]{:S(2)}) collective-permute-start(f32[4,3,8,128]{3,2,1,0:T(8,128)S(1)} %round2.1), channel_id=1, source_target_pairs={{0,16},{1,17},{2,18},{3,19},{4,20},{5,21},{6,22},{7,23},{8,24},{9,... | collective-permute-start | bytes 147464 | tf_op jit(solution)/shard_map/ppermute | solution.py:384

commit v3 on v2

--- a/solution.py
+++ b/solution.py
@@ -9,6 +9,7 @@
 STEPS = 4
 KAPPA = 0.04
 FINE_UNROLL = 2
+FULL_CHUNK = 8
 F32 = jnp.float32
 HI = lax.Precision.HIGHEST
 VM = pltpu.MemorySpace.VMEM
@@ -74,8 +75,9 @@
 
 NL = 12
 VSPEC = pl.BlockSpec(memory_space=VM)
+HSPEC = pl.BlockSpec(memory_space=pltpu.MemorySpace.HBM)
 SSPEC = pl.BlockSpec(memory_space=pltpu.MemorySpace.SMEM)
-GRANT = 40 << 20
+GRANT = 16 << 20
 
 
 def shaped(*dims):
@@ -121,8 +123,8 @@
     return out
 
 
-def fine1_kernel(pos_ref, m1_ref, own_ref, p1_ref, start_ref, after_ref, coefs, speed_c_ref,
-                 state_a, state_b, speed, ev, od):
+def fine1_kernel(pos_ref, m1_ref, own_ref, p1_ref, start_ref, after_ref, coefs, speed_c_ref, share_ref,
+                 state_a, state_b, begin, speed, share, ev, od, sems):
     slab = pos_ref[0]
     depth = pos_ref[2]
     perm = lane_parity()
@@ -136,7 +138,9 @@
                 for p, half in ((0, ev), (1, od)):
                     got = half[pl.ds(192 * part + q, 96, stride=2), :]
                     dest[:, 4 * i:4 * i + 4, 2 * q + p] = got.reshape(3, 4, 8, 128)
-    start_ref[...] = state_a[...]
+    begin[...] = state_a[...]
+    keep = pltpu.make_async_copy(begin, start_ref, sems.at[0])
+    keep.start()
     sub, lane = iotas()
 
     def build(l, carry):
@@ -172,33 +176,46 @@
     for j in range(1, 5):
         for c, v in enumerate(restrict(speed, j)):
             speed_c_ref[j - 1, c] = 2.0 * v
+            if j in (2, 3):
+                for to in range(share.shape[0]):
+                    share[to, j - 2, c] = 2.0 * v
+    send = pltpu.make_async_copy(share, share_ref, sems.at[1])
+    send.start()
     march4(coefs, state_a, state_b, 0)
     after_ref[...] = state_a[:, 4:8]
-
-
-def fine1(pos, m1, own, p1):
+    keep.wait()
+    send.wait()
+
+
+def fine1(pos, m1, own, p1, slabs):
     return pl.pallas_call(
         fine1_kernel,
-        out_shape=(shaped(3, NL, 4, 8, 128), shaped(3, 4, 4, 8, 128), shaped(NL, 4, 15, 8, 128), shaped(4, 3, 8, 128)),
+        out_shape=(shaped(3, NL, 4, 8, 128), shaped(3, 4, 4, 8, 128), shaped(NL, 4, 15, 8, 128),
+                   shaped(4, 3, 8, 128), shaped(slabs, 2, 3, 8, 128)),
         in_specs=[SSPEC] + [VSPEC] * 3,
-        out_specs=(VSPEC,) * 4,
-        scratch_shapes=[pltpu.VMEM((3, NL, 4, 8, 128), F32)] * 3 + [pltpu.VMEM((384, 128), F32)] * 2,
+        out_specs=(HSPEC, VSPEC, VSPEC, VSPEC, HSPEC),
+        scratch_shapes=[pltpu.VMEM((3, NL, 4, 8, 128), F32)] * 4 + [pltpu.VMEM((slabs, 2, 3, 8, 128), F32)]
+        + [pltpu.VMEM((384, 128), F32)] * 2 + [pltpu.SemaphoreType.DMA((2,))],
         compiler_params=pltpu.CompilerParams(vmem_limit_bytes=GRANT),
         cost_estimate=cost(10_000_000, 6_000_000),
         name="fine1",
     )(pos, m1, own, p1)
 
 
-def fine2_kernel(pos_ref, coefs, speed_c, start_ref, m1_ref, own_ref, p1_ref, relaxed_ref, share_ref, state_a, state_b):
+def fine2_kernel(pos_ref, coefs, speed_c, start_ref, m1_ref, own_ref, p1_ref, relaxed_ref, forcing_ref, state_a, state_b, sem):
     slab = pos_ref[0]
     first = pos_ref[1] == 1
     depth = pos_ref[2]
-    for i, ref in enumerate((m1_ref, own_ref, p1_ref)):
-        for dz in range(4):
-            l = 4 * i + dz
-            for c in range(3):
-                for k in range(4):
-                    state_a[c, l, k] = jnp.where(first, start_ref[c, l, k], ref[c, dz, k])
+    @pl.when(first)
+    def _():
+        fetch = pltpu.make_async_copy(start_ref, state_a, sem)
+        fetch.start()
+        fetch.wait()
+
+    @pl.when(jnp.logical_not(first))
+    def _():
+        for i, ref in enumerate((m1_ref, own_ref, p1_ref)):
+            state_a[:, 4 * i:4 * i + 4] = ref[...]
     relaxed_ref[...] = state_a[:, 4:8]
     coarse = {j: restrict(state_a, j) for j in range(1, 5)}
     image = {}
@@ -212,18 +229,16 @@
         for c in range(3):
             forcing = again[c] - image[j][c]
             forcing = forcing + jnp.where(first, image[j][c], 0.0)
-            for s in range(share_ref.shape[0]):
-                share_ref[s, 0, i, c] = forcing
-                share_ref[s, 1, i, c] = speed_c[j - 1, c]
-
-
-def fine2(pos, coefs, speed_c, start, m1, own, p1, slabs):
+            forcing_ref[i, c] = forcing
+
+
+def fine2(pos, coefs, speed_c, start, m1, own, p1):
     return pl.pallas_call(
         fine2_kernel,
-        out_shape=(shaped(3, 4, 4, 8, 128), shaped(slabs, 2, 2, 3, 8, 128)),
-        in_specs=[SSPEC] + [VSPEC] * 6,
+        out_shape=(shaped(3, 4, 4, 8, 128), shaped(2, 3, 8, 128)),
+        in_specs=[SSPEC, VSPEC, VSPEC, HSPEC] + [VSPEC] * 3,
         out_specs=(VSPEC,) * 2,
-        scratch_shapes=[pltpu.VMEM((3, NL, 4, 8, 128), F32)] * 2,
+        scratch_shapes=[pltpu.VMEM((3, NL, 4, 8, 128), F32)] * 2 + [pltpu.SemaphoreType.DMA],
         compiler_params=pltpu.CompilerParams(vmem_limit_bytes=GRANT),
         cost_estimate=cost(10_000_000, 6_000_000),
         name="fine2",
@@ -258,28 +273,15 @@
     )(speed)
 
 
-CHUNK = 4
-
-
 def window(slab, halo, layers):
     count = min(layers, 2 + 2 * halo)
     return count, jnp.clip(2 * slab - halo, 0, layers - count)
 
 
-def psi_steps(coefs, src, dst, slab, halo, steps):
-    layers = coefs.shape[0]
-    for s in range(steps):
-        reach = halo + steps - 1 - s
-        low = jnp.maximum(2 * slab - reach, 0) // CHUNK
-        high = (jnp.minimum(2 * slab + 2 + reach, layers) + CHUNK - 1) // CHUNK
-        src, dst = psi_step(coefs, src, dst, low, high)
-    return src
-
-
-def psi_step(coefs, src, dst, low, high):
+def psi_step(coefs, src, dst, chunk, low, high):
     def some(i, carry):
-        for dj in range(CHUNK):
-            j = i * CHUNK + dj
+        for dj in range(chunk):
+            j = i * chunk + dj
             new = psi(lambda n: coefs[j, n],
                       [src[j, c] for c in range(3)],
                       [src[j + 1, c] for c in range(3)],
@@ -288,68 +290,98 @@
                 dst[j + 1, c] = new[c]
         return carry
     lax.fori_loop(low, high, some, 0)
-    return dst, src
-
-
-def round_kernel(distance, halo_own, halo_out, pos_ref, coefs, own_ref, got_ref, out_ref, state_a, state_b):
+
+
+def spread(distance, halo, slab, coefs, got_ref, state_a, state_b):
+    layers = coefs.shape[0]
+    for ref in (state_a, state_b):
+        ref[...] = jnp.zeros_like(ref)
+    n_in, at_in = window(slab, halo, layers)
+    state_a[pl.ds(at_in + 1, n_in)] = got_ref[...]
+    src, dst = state_a, state_b
+    chunk = 2 if distance == 1 else 4
+    for s in range(distance):
+        reach = halo + 1 + s
+        low = jnp.maximum(2 * slab - reach, 0) // chunk
+        high = (jnp.minimum(2 * slab + 2 + reach, layers) + chunk - 1) // chunk
+        psi_step(coefs, src, dst, chunk, low, high)
+        src, dst = dst, src
+    return src, dst
+
+
+def round_kernel(distance, halo, pos_ref, coefs, own_ref, got_ref, out_ref, state_a, state_b):
     slab = pos_ref[0]
     layers = coefs.shape[0]
-    n_got, at_got = window(slab, halo_out + distance, layers)
-    n_own, at_own = window(slab, halo_own, layers)
-    n_out, at_out = window(slab, halo_out, layers)
-    for ref in (state_a, state_b):
-        ref[0] = jnp.zeros((3, 8, 128), F32)
-        ref[layers + 1] = jnp.zeros((3, 8, 128), F32)
-    state_a[pl.ds(at_got + 1, n_got)] = got_ref[...]
-    if distance >= 4:
-        def pair(i, carry):
-            reach = halo_out + distance - 1 - 2 * i
-
-            def span(r):
-                low = jnp.maximum(2 * slab - r, 0) // CHUNK
-                return low, (jnp.minimum(2 * slab + 2 + r, layers) + CHUNK - 1) // CHUNK
-            psi_step(coefs, state_a, state_b, *span(reach))
-            psi_step(coefs, state_b, state_a, *span(reach - 1))
-            return carry
-        lax.fori_loop(0, distance // 2, pair, 0)
-        last = state_a
-    else:
-        last = psi_steps(coefs, state_a, state_b, slab, halo_out, distance)
-    out_ref[...] = last[pl.ds(at_out + 1, n_out)] + own_ref[pl.ds(at_out - at_own, n_out)]
-
-
-def sweep_round(distance, halo_own, halo_out, pos, coefs, own, got):
+    n_in, at_in = window(slab, halo, layers)
+    n_out, at_out = window(slab, halo + distance, layers)
+    last, _ = spread(distance, halo, slab, coefs, got_ref, state_a, state_b)
+    out_ref[...] = last[pl.ds(at_out + 1, n_out)]
+    inner = pl.ds(at_in - at_out, n_in)
+    out_ref[inner] = out_ref[inner] + own_ref[...]
+
+
+def final_kernel(distance, halo, pos_ref, coefs, own_ref, got_ref, share_ref, state_a, state_b):
+    slab = pos_ref[0]
     layers = coefs.shape[0]
-    count = min(layers, 2 + 2 * halo_out)
-    return pl.pallas_call(
-        functools.partial(round_kernel, distance, halo_own, halo_out),
-        out_shape=shaped(count, 3, 8, 128),
+    n_in, at_in = window(slab, halo, layers)
+    last, other = spread(distance, halo, slab, coefs, got_ref, state_a, state_b)
+    inner = pl.ds(at_in + 1, n_in)
+    last[inner] = last[inner] + own_ref[...]
+    share_ref[:, 0] = last[1:layers + 1].reshape(layers // 2, 2, 3, 8, 128)
+
+    def pair(i, carry):
+        psi_step(coefs, last, other, FULL_CHUNK, 0, layers // FULL_CHUNK)
+        psi_step(coefs, other, last, FULL_CHUNK, 0, layers // FULL_CHUNK)
+        return carry
+    lax.fori_loop(0, distance, pair, 0)
+    share_ref[:, 1] = last[1:layers + 1].reshape(layers // 2, 2, 3, 8, 128)
+
+
+def sweep_round(distance, halo, final, pos, coefs, own, got):
+    layers = coefs.shape[0]
+    out = shaped(layers // 2, 2, 2, 3, 8, 128) if final else shaped(min(layers, 2 + 2 * (halo + distance)), 3, 8, 128)
+    return pl.pallas_call(
+        functools.partial(final_kernel if final else round_kernel, distance, halo),
+        out_shape=out,
         in_specs=[SSPEC] + [VSPEC] * 3,
         out_specs=VSPEC,
         scratch_shapes=[pltpu.VMEM((layers + 2, 3, 8, 128), F32)] * 2,
         compiler_params=pltpu.CompilerParams(vmem_limit_bytes=GRANT),
-        cost_estimate=cost(distance * 2_000_000, 3_000_000),
+        cost_estimate=cost((3 if final else 1) * distance * 2_000_000, 3_000_000),
         name=f"round{distance}",
     )(pos, coefs, own, got)
 
 
-def last_kernel(pos_ref, coefs, relaxed_ref, near_ref, far_ref, out_ref, state_a, ev, od):
-    slab = pos_ref[0]
+def total_kernel(got_ref, near_ref, far_ref):
+    for i in range(2):
+        for c in range(3):
+            for part, ref in ((0, near_ref), (1, far_ref)):
+                terms = [got_ref[s, part, i, c] for s in range(got_ref.shape[0])]
+                while len(terms) > 1:
+                    terms = [a + b for a, b in zip(terms[::2], terms[1::2])] + terms[len(terms) // 2 * 2:]
+                ref[i, c] = terms[0]
+
+
+def totals(got):
+    return pl.pallas_call(
+        total_kernel,
+        out_shape=(shaped(2, 3, 8, 128),) * 2,
+        in_specs=[VSPEC],
+        out_specs=(VSPEC,) * 2,
+        compiler_params=pltpu.CompilerParams(vmem_limit_bytes=GRANT),
+        cost_estimate=cost(200_000, 850_000),
+        name="totals",
+    )(got)
+
+
+def last_kernel(pos_ref, relaxed_ref, near_ref, far_ref, out_ref, ev, od):
     first = pos_ref[1] == 1
-    layers = coefs.shape[0]
-    n_got, at_got = window(slab, 1, layers)
-    state_a[0] = jnp.zeros((3, 8, 128), F32)
-    state_a[layers + 1] = jnp.zeros((3, 8, 128), F32)
-    state_a[pl.ds(at_got + 1, n_got)] = far_ref[...]
     for zc in range(2):
-        j = 2 * slab + zc
-        new = psi(lambda n: coefs[j, n], *[[state_a[j + d, c] for c in range(3)] for d in range(3)])
         for c in range(3):
-            coarse = new[c] + near_ref[j - at_got, c]
             w = [[relaxed_ref[c, 2 * zc + dz, k] for k in range(4)] for dz in range(2)]
             lo, hi = [(v[0] + v[1]) + (v[2] + v[3]) for v in w]
             mean = (lo + hi) * 0.125
-            diff = jnp.where(first, mean, coarse) - mean
+            diff = jnp.where(first, mean, near_ref[zc, c] + far_ref[zc, c]) - mean
             for dz in range(2):
                 row0 = (c * 4 + 2 * zc + dz) * 16
                 for q in range(2):
@@ -360,18 +392,17 @@
     out_ref[...] = out.reshape(3, 4, 16, 256)
 
 
-def sweep_last(pos, coefs, relaxed, near, far):
-    layers = coefs.shape[0]
+def sweep_last(pos, relaxed, near, far):
     return pl.pallas_call(
         last_kernel,
         out_shape=shaped(3, 4, 16, 256),
-        in_specs=[SSPEC] + [VSPEC] * 4,
+        in_specs=[SSPEC] + [VSPEC] * 3,
         out_specs=VSPEC,
-        scratch_shapes=[pltpu.VMEM((layers + 2, 3, 8, 128), F32)] + [pltpu.VMEM((192, 128), F32)] * 2,
-        compiler_params=pltpu.CompilerParams(vmem_limit_bytes=GRANT),
-        cost_estimate=cost(2_000_000, 3_000_000),
+        scratch_shapes=[pltpu.VMEM((192, 128), F32)] * 2,
+        compiler_params=pltpu.CompilerParams(vmem_limit_bytes=GRANT),
+        cost_estimate=cost(2_000_000, 500_000),
         name="last",
-    )(pos, coefs, relaxed, near, far)
+    )(pos, relaxed, near, far)
 
 
 def moved(block, by_t, by_z):
@@ -391,17 +422,15 @@
     depth = slabs * velocity.shape[1]
     pos = jnp.stack([slab, (t == 0).astype(jnp.int32), jnp.int32(depth)])
     own = jnp.concatenate([c_states[0], velocity], axis=0)
-    start, after, coefs, speed_c = fine1(pos, moved(own, 0, 1), own, moved(own, 0, -1))
+    start, after, coefs, speed_c, share = fine1(pos, moved(own, 0, 1), own, moved(own, 0, -1), slabs)
     m1, same, p1 = [moved(after, 1, by) for by in (1, 0, -1)]
-    relaxed, share = fine2(pos, coefs, speed_c, start, m1, same, p1, slabs)
-    share = lax.all_to_all(share, "gz", 0, 0, tiled=True)
-    state = share[:, 0].reshape(2 * slabs, 3, 8, 128)
-    coefs = sweep_coefs(share[:, 1].reshape(2 * slabs, 3, 8, 128))
-    halo_own = slabs * 2
-    for distance in (16, 8, 4, 2):
-        state = sweep_round(distance, halo_own, distance - 1, pos, coefs, state, moved(state, distance, 0))
-        halo_own = distance - 1
-    out = sweep_last(pos, coefs, relaxed, moved(state, 1, 0), moved(state, 2, 0))
+    speed = lax.all_to_all(share, "gz", 0, 0, tiled=True)
+    relaxed, state = fine2(pos, coefs, speed_c, start, m1, same, p1)
+    coefs = sweep_coefs(speed.reshape(2 * slabs, 3, 8, 128))
+    for distance in (1, 2, 4, 8):
+        state = sweep_round(distance, distance - 1, distance == 8, pos, coefs, state, moved(state, distance, 0))
+    near, far = totals(lax.all_to_all(state, "gz", 0, 0, tiled=True))
+    out = sweep_last(pos, relaxed, moved(near, 1, 0), moved(far, 17, 0))
     return out[None]
 
 

time: 168 us -> 153 us (0.911)
  the two profiles are of different devices: /device:TPU:206 before, /device:TPU:8 now
where the time goes in v3:
time: 153 us; the launch traced here: 152 us
  starting transfers between devices  70.4 us (46%)
  blocking collectives  28.2 us (18%)
  Pallas kernels  25.9 us (17%)
  waiting for transfers between devices  19 us (12%)
  local copies, waits for them, and re-layouts  7.53 us (5%)
    ppermute x11, starting transfers between devices, moved(): return lax.ppermute(block, ('tm', 'gz'), route)  63.3 us
    all_to_all x1, blocking collectives, local(): near, far = totals(lax.all_to_all(state, 'gz', 0, 0, tiled=True))  28.2 us
    ppermute x11, waiting for transfers between devices, moved(): return lax.ppermute(block, ('tm', 'gz'), route)  19 us
    pallas_call x4, Pallas kernels, sweep_round(): pl.pallas_call(functools.partial(final_kernel if final else round_kernel,...  15.8 us
    unnamed x18, local copies, waits for them, and re-layouts  7.53 us
    all_to_all x1, starting transfers between devices, local(): speed = lax.all_to_all(share, 'gz', 0, 0, tiled=True)  7.15 us
    pallas_call x1, Pallas kernels, fine1(): pl.pallas_call(fine1_kernel, out_shape=(shaped(3, NL, 4, 8, 128), shaped(...  4.37 us
  transfers between devices with their start and end apart: 12, of which 8 were waited for; matrix products, arithmetic and copies ran while one was open for 0% of the time, Pallas kernels for 3%

profile of v3, /device:TPU:8, one launch (start us, length us, event | category | flops | bytes accessed | tf_op | source)
XLA Modules:
  0.0 152.3 jit_solution(11468996454913572884)
XLA Ops:
  0.0 1.0 pad_maximum_fusion.own_ref
  1.1 7.7 %collective-permute-start.1 = (f32[6,4,16,256]{3,2,1,0:T(8,128)S(1)}, f32[6,4,16,256]{3,2,1,0:T(8,128)S(1)}, u32[]{:S(2)}, u32[]{:S(2)}) collective-permute-start(f32[6,4,16,256]{3,2,1,0:T(8,128)S(1)} %pad_maximum_fusion.own_ref), channel_id=1, source_target_pairs={{1,0},{2,1},{3,2},{4,3},{5,4},{6,5},{7,6},{8,7},{9,8},{10,9},{11,1... | collective-permute-start | bytes 1179656 | tf_op jit(solution)/shard_map/ppermute | solution.py:415
  8.8 1.9 %collective-permute-start = (f32[6,4,16,256]{3,2,1,0:T(8,128)S(1)}, f32[6,4,16,256]{3,2,1,0:T(8,128)S(1)}, u32[]{:S(2)}, u32[]{:S(2)}) collective-permute-start(f32[6,4,16,256]{3,2,1,0:T(8,128)S(1)} %pad_maximum_fusion.own_ref), channel_id=1, source_target_pairs={{0,1},{1,2},{2,3},{3,4},{4,5},{5,6},{6,7},{7,8},{8,9},{9,10},{10,1... | collective-permute-start | bytes 1179656 | tf_op jit(solution)/shard_map/ppermute | solution.py:415
  10.7 0.1 pad_add_fusion.pos_ref
  10.8 3.3 %collective-permute-done.1.p1_ref = f32[6,4,16,256]{3,2,1,0:T(8,128)S(1)} collective-permute-done((f32[6,4,16,256]{3,2,1,0:T(8,128)S(1)}, f32[6,4,16,256]{3,2,1,0:T(8,128)S(1)}, u32[]{:S(2)}, u32[]{:S(2)}) %collective-permute-start.1) | collective-permute-done | bytes 393248 | tf_op jit(solution)/shard_map/ppermute | solution.py:415
  14.0 0.0 copy-start.3
  14.0 0.7 copy-done.3
  14.8 3.7 %collective-permute-done.m1_ref = f32[6,4,16,256]{3,2,1,0:T(8,128)S(1)} collective-permute-done((f32[6,4,16,256]{3,2,1,0:T(8,128)S(1)}, f32[6,4,16,256]{3,2,1,0:T(8,128)S(1)}, u32[]{:S(2)}, u32[]{:S(2)}) %collective-permute-start) | collective-permute-done | bytes 393248 | tf_op jit(solution)/shard_map/ppermute | solution.py:415
  18.4 0.0 copy-start.5
  18.4 0.7 copy-done.5
  19.2 0.0 copy-start.4
  19.2 1.0 copy-done.4
  20.2 0.0 copy-start.6
  20.2 1.0 copy-done.6
  21.2 4.4 %fine1.1 = (f32[3,12,4,8,128]{4,3,2,1,0:T(8,128)S(1)}, f32[3,4,4,8,128]{4,3,2,1,0:T(8,128)S(1)}, f32[12,4,15,8,128]{4,3,2,1,0:T(8,128)S(1)}, f32[4,3,8,128]{3,2,1,0:T(8,128)S(1)}, f32[16,2,3,8,128]{4,3,2,1,0:T(8,128)S(1)}) custom-call(s32[3]{0:T(128)S(1)} %pad_add_fusion.pos_ref, f32[6,4,16,256]{3,2,1,0:T(8,128)S(1)} %copy-done.6, ...), custom_call_target="tpu_custom_call" | custom-call | flops 10000000 | bytes 6000000 | tf_op jit(solution)/shard_map/fine1/pallas_call | solution.py:191
  25.5 0.0 copy-start
  25.6 0.8 copy-done
  26.4 0.0 copy-start.2
  26.4 0.7 copy-done.2
  27.1 0.0 copy-start.7
  27.1 0.6 copy-done.7
  27.7 7.2 %all-to-all-start = ((f32[16,2,3,8,128]{4,3,2,1,0:T(8,128)}), f32[16,2,3,8,128]{4,3,2,1,0:T(8,128)S(1)}, u32[]{:S(2)}, u32[]{:S(2)}) async-start(f32[16,2,3,8,128]{4,3,2,1,0:T(8,128)} %copy-done.2), calls=%async_computation | async-start | bytes 786432 | tf_op jit(solution)/shard_map/all_to_all | solution.py:427
  34.9 1.3 collective-permute-start.4
  36.2 4.9 %collective-permute-start.3 = (f32[3,4,4,8,128]{4,3,2,1,0:T(8,128)S(1)}, f32[3,4,4,8,128]{4,3,2,1,0:T(8,128)S(1)}, u32[]{:S(2)}, u32[]{:S(2)}) collective-permute-start(f32[3,4,4,8,128]{4,3,2,1,0:T(8,128)S(1)} %get-tuple-element.17), channel_id=1, source_target_pairs={{0,16},{1,17},{2,18},{3,19},{4,20},{5,21},{6,22},{7,23},{8,24},{9,... | collective-permute-start | bytes 589832 | tf_op jit(solution)/shard_map/ppermute | solution.py:415
  41.1 3.4 %collective-permute-start.2 = (f32[3,4,4,8,128]{4,3,2,1,0:T(8,128)S(1)}, f32[3,4,4,8,128]{4,3,2,1,0:T(8,128)S(1)}, u32[]{:S(2)}, u32[]{:S(2)}) collective-permute-start(f32[3,4,4,8,128]{4,3,2,1,0:T(8,128)S(1)} %get-tuple-element.17), channel_id=1, source_target_pairs={{0,17},{1,18},{2,19},{3,20},{4,21},{5,22},{6,23},{7,24},{8,25},{9,... | collective-permute-start | bytes 589832 | tf_op jit(solution)/shard_map/ppermute | solution.py:415
  44.6 1.7 %collective-permute-done.4.p1_ref = f32[3,4,4,8,128]{4,3,2,1,0:T(8,128)S(1)} collective-permute-done((f32[3,4,4,8,128]{4,3,2,1,0:T(8,128)S(1)}, f32[3,4,4,8,128]{4,3,2,1,0:T(8,128)S(1)}, u32[]{:S(2)}, u32[]{:S(2)}) %collective-permute-start.4) | collective-permute-done | bytes 196640 | tf_op jit(solution)/shard_map/ppermute | solution.py:415
  46.3 0.0 collective-permute-done.3.own_ref
  46.3 1.7 %collective-permute-done.2.m1_ref = f32[3,4,4,8,128]{4,3,2,1,0:T(8,128)S(1)} collective-permute-done((f32[3,4,4,8,128]{4,3,2,1,0:T(8,128)S(1)}, f32[3,4,4,8,128]{4,3,2,1,0:T(8,128)S(1)}, u32[]{:S(2)}, u32[]{:S(2)}) %collective-permute-start.2) | collective-permute-done | bytes 196640 | tf_op jit(solution)/shard_map/ppermute | solution.py:415
  48.0 0.0 copy-start.1
  48.0 1.1 copy-done.1
  49.0 0.0 copy-start.8
  49.0 0.8 copy-done.8
  49.8 2.8 %fine2.1 = (f32[3,4,4,8,128]{4,3,2,1,0:T(8,128)S(1)}, f32[2,3,8,128]{3,2,1,0:T(8,128)}) custom-call(s32[3]{0:T(128)S(1)} %pad_add_fusion.pos_ref, f32[12,4,15,8,128]{4,3,2,1,0:T(8,128)S(1)} %get-tuple-element.14.coefs, f32[4,3,8,128]{3,2,1,0:T(8,128)S(1)} %copy-done.8, f32[3,12,4,8,128]{4,3,2,1,0:T(8,128)S(1)} %copy-done.1, ...), custom_call_target="tpu_custom_call" | custom-call | flops 10000000 | bytes 6000000 | tf_op jit(solution)/shard_map/fine2/pallas_call | solution.py:236
  52.6 3.8 %collective-permute-start.5 = (f32[2,3,8,128]{3,2,1,0:T(8,128)}, f32[2,3,8,128]{3,2,1,0:T(8,128)S(1)}, u32[]{:S(2)}, u32[]{:S(2)}) collective-permute-start(f32[2,3,8,128]{3,2,1,0:T(8,128)} %get-tuple-element.20.own_ref), channel_id=1, source_target_pairs={{0,16},{1,17},{2,18},{3,19},{4,20},{5,21},{6,22},{7,23},{8,24},{9,... | collective-permute-start | bytes 73736 | tf_op jit(solution)/shard_map/ppermute | solution.py:415
  56.4 0.0 all-to-all-done
  56.4 1.4 coefs.1
  57.8 0.0 collective-permute-done.5.got_ref
  57.8 1.1 round1.1.own_ref
  58.9 9.3 %collective-permute-start.6 = (f32[4,3,8,128]{3,2,1,0:T(8,128)S(1)}, f32[4,3,8,128]{3,2,1,0:T(8,128)S(1)}, u32[]{:S(2)}, u32[]{:S(2)}) collective-permute-start(f32[4,3,8,128]{3,2,1,0:T(8,128)S(1)} %round1.1.own_ref), channel_id=1, source_target_pairs={{0,32},{1,33},{2,34},{3,35},{4,36},{5,37},{6,38},{7,39},{8,40},{9,... | collective-permute-start | bytes 147464 | tf_op jit(solution)/shard_map/ppermute | solution.py:415
  68.2 1.7 %collective-permute-done.6.got_ref = f32[4,3,8,128]{3,2,1,0:T(8,128)S(1)} collective-permute-done((f32[4,3,8,128]{3,2,1,0:T(8,128)S(1)}, f32[4,3,8,128]{3,2,1,0:T(8,128)S(1)}, u32[]{:S(2)}, u32[]{:S(2)}) %collective-permute-start.6) | collective-permute-done | bytes 49184 | tf_op jit(solution)/shard_map/ppermute | solution.py:415
  69.9 1.0 round2.1.own_ref
  71.0 8.1 %collective-permute-start.7 = (f32[8,3,8,128]{3,2,1,0:T(8,128)S(1)}, f32[8,3,8,128]{3,2,1,0:T(8,128)S(1)}, u32[]{:S(2)}, u32[]{:S(2)}) collective-permute-start(f32[8,3,8,128]{3,2,1,0:T(8,128)S(1)} %round2.1.own_ref), channel_id=1, source_target_pairs={{0,64},{1,65},{2,66},{3,67},{4,68},{5,69},{6,70},{7,71},{8,72},{9,... | collective-permute-start | bytes 294920 | tf_op jit(solution)/shard_map/ppermute | solution.py:415
  79.1 2.2 %collective-permute-done.7.got_ref = f32[8,3,8,128]{3,2,1,0:T(8,128)S(1)} collective-permute-done((f32[8,3,8,128]{3,2,1,0:T(8,128)S(1)}, f32[8,3,8,128]{3,2,1,0:T(8,128)S(1)}, u32[]{:S(2)}, u32[]{:S(2)}) %collective-permute-start.7) | collective-permute-done | bytes 98336 | tf_op jit(solution)/shard_map/ppermute | solution.py:415
  81.2 1.7 %round4.1.own_ref = f32[16,3,8,128]{3,2,1,0:T(8,128)S(1)} custom-call(s32[3]{0:T(128)S(1)} %pad_add_fusion.pos_ref, f32[32,15,8,128]{3,2,1,0:T(8,128)S(1)} %coefs.1, f32[8,3,8,128]{3,2,1,0:T(8,128)S(1)} %round2.1.own_ref, f32[8,3,8,128]{3,2,1,0:T(8,128)S(1)} %collective-permute-done.7.got_ref), custom_call_target="tpu_custom_call" | custom-call | flops 8000000 | bytes 3000000 | tf_op jit(solution)/shard_map/round4/pallas_call | solution.py:343
  83.0 6.1 %collective-permute-start.8 = (f32[16,3,8,128]{3,2,1,0:T(8,128)S(1)}, f32[16,3,8,128]{3,2,1,0:T(8,128)S(1)}, u32[]{:S(2)}, u32[]{:S(2)}) collective-permute-start(f32[16,3,8,128]{3,2,1,0:T(8,128)S(1)} %round4.1.own_ref), channel_id=1, source_target_pairs={{0,128},{1,129},{2,130},{3,131},{4,132},{5,133},{6,134},{7,135},{8... | collective-permute-start | bytes 589832 | tf_op jit(solution)/shard_map/ppermute | solution.py:415
  89.1 3.2 %collective-permute-done.8.got_ref = f32[16,3,8,128]{3,2,1,0:T(8,128)S(1)} collective-permute-done((f32[16,3,8,128]{3,2,1,0:T(8,128)S(1)}, f32[16,3,8,128]{3,2,1,0:T(8,128)S(1)}, u32[]{:S(2)}, u32[]{:S(2)}) %collective-permute-start.8) | collective-permute-done | bytes 196640 | tf_op jit(solution)/shard_map/ppermute | solution.py:415
  92.3 12.0 %round8.1 = f32[16,2,2,3,8,128]{5,4,3,2,1,0:T(8,128)S(1)} custom-call(s32[3]{0:T(128)S(1)} %pad_add_fusion.pos_ref, f32[32,15,8,128]{3,2,1,0:T(8,128)S(1)} %coefs.1, f32[16,3,8,128]{3,2,1,0:T(8,128)S(1)} %round4.1.own_ref, f32[16,3,8,128]{3,2,1,0:T(8,128)S(1)} %collective-permute-done.8.got_ref), custom_call_target="tpu_custom_call" | custom-call | flops 48000000 | bytes 3000000 | tf_op jit(solution)/shard_map/round8/pallas_call | solution.py:343
  104.3 28.2 %all_to_all.10.got_ref = f32[16,2,2,3,8,128]{5,4,3,2,1,0:T(8,128)S(1)} all-to-all(f32[16,2,2,3,8,128]{5,4,3,2,1,0:T(8,128)S(1)} %round8.1), channel_id=1, replica_groups=mesh['tm'=32,'gz'=16] {'gz'}, dimensions={0} | all-to-all | bytes 1572864 | tf_op jit(solution)/shard_map/all_to_all | solution.py:432
  132.5 1.3 collective-permute-start.9
  133.8 15.4 %collective-permute-start.10 = (f32[2,3,8,128]{3,2,1,0:T(8,128)S(1)}, f32[2,3,8,128]{3,2,1,0:T(8,128)S(1)}, u32[]{:S(2)}, u32[]{:S(2)}) collective-permute-start(f32[2,3,8,128]{3,2,1,0:T(8,128)S(1)} %get-tuple-element.22), channel_id=1, source_target_pairs={{0,272},{1,273},{2,274},{3,275},{4,276},{5,277},{6,278},{7,279},{8... | collective-permute-start | bytes 73736 | tf_op jit(solution)/shard_map/ppermute | solution.py:415
  149.2 0.0 collective-permute-done.9.near_ref
  149.2 1.5 collective-permute-done.10.far_ref
  150.7 1.6 %last.1 = f32[3,4,16,256]{3,2,1,0:T(8,128)} custom-call(s32[3]{0:T(128)S(1)} %pad_add_fusion.pos_ref, f32[3,4,4,8,128]{4,3,2,1,0:T(8,128)S(1)} %get-tuple-element.18.relaxed_ref, f32[2,3,8,128]{3,2,1,0:T(8,128)S(1)} %collective-permute-done.9.near_ref, f32[2,3,8,128]{3,2,1,0:T(8,128)S(1)} %collective-permute-done.10.far_ref), custom_call_target="tpu_custom_call" | custom-call | flops 2000000 | bytes 500000 | tf_op jit(solution)/shard_map/last/pallas_call | solution.py:396
  (1 shorter events, 0.0 us)
Async XLA Ops:
  1.1 13.0 %collective-permute-start.1 = (f32[6,4,16,256]{3,2,1,0:T(8,128)S(1)}, f32[6,4,16,256]{3,2,1,0:T(8,128)S(1)}, u32[]{:S(2)}, u32[]{:S(2)}) collective-permute-start(f32[6,4,16,256]{3,2,1,0:T(8,128)S(1)} %pad_maximum_fusion.own_ref), channel_id=1, source_target_pairs={{1,0},{2,1},{3,2},{4,3},{5,4},{6,5},{7,6},{8,7},{9,8},{10,9},{11,1... | collective-permute-start | bytes 1179656 | tf_op jit(solution)/shard_map/ppermute | solution.py:415
  8.8 9.7 %collective-permute-start = (f32[6,4,16,256]{3,2,1,0:T(8,128)S(1)}, f32[6,4,16,256]{3,2,1,0:T(8,128)S(1)}, u32[]{:S(2)}, u32[]{:S(2)}) collective-permute-start(f32[6,4,16,256]{3,2,1,0:T(8,128)S(1)} %pad_maximum_fusion.own_ref), channel_id=1, source_target_pairs={{0,1},{1,2},{2,3},{3,4},{4,5},{5,6},{6,7},{7,8},{8,9},{9,10},{10,1... | collective-permute-start | bytes 1179656 | tf_op jit(solution)/shard_map/ppermute | solution.py:415
  14.0 0.7 copy-start.3
  18.4 0.8 copy-start.5
  19.2 1.0 copy-start.4
  20.2 1.0 copy-start.6
  25.5 0.8 copy-start
  26.4 0.7 copy-start.2
  27.1 0.6 copy-start.7
  27.7 28.7 %all-to-all-start = ((f32[16,2,3,8,128]{4,3,2,1,0:T(8,128)}), f32[16,2,3,8,128]{4,3,2,1,0:T(8,128)S(1)}, u32[]{:S(2)}, u32[]{:S(2)}) async-start(f32[16,2,3,8,128]{4,3,2,1,0:T(8,128)} %copy-done.2), calls=%async_computation | async-start | bytes 786432 | tf_op jit(solution)/shard_map/all_to_all | solution.py:427
  34.9 11.4 %collective-permute-start.4 = (f32[3,4,4,8,128]{4,3,2,1,0:T(8,128)S(1)}, f32[3,4,4,8,128]{4,3,2,1,0:T(8,128)S(1)}, u32[]{:S(2)}, u32[]{:S(2)}) collective-permute-start(f32[3,4,4,8,128]{4,3,2,1,0:T(8,128)S(1)} %get-tuple-element.17), channel_id=1, source_target_pairs={{1,16},{2,17},{3,18},{4,19},{5,20},{6,21},{7,22},{8,23},{9,24},{10... | collective-permute-start | bytes 589832 | tf_op jit(solution)/shard_map/ppermute | solution.py:415
  36.2 10.1 %collective-permute-start.3 = (f32[3,4,4,8,128]{4,3,2,1,0:T(8,128)S(1)}, f32[3,4,4,8,128]{4,3,2,1,0:T(8,128)S(1)}, u32[]{:S(2)}, u32[]{:S(2)}) collective-permute-start(f32[3,4,4,8,128]{4,3,2,1,0:T(8,128)S(1)} %get-tuple-element.17), channel_id=1, source_target_pairs={{0,16},{1,17},{2,18},{3,19},{4,20},{5,21},{6,22},{7,23},{8,24},{9,... | collective-permute-start | bytes 589832 | tf_op jit(solution)/shard_map/ppermute | solution.py:415
  41.1 6.9 %collective-permute-start.2 = (f32[3,4,4,8,128]{4,3,2,1,0:T(8,128)S(1)}, f32[3,4,4,8,128]{4,3,2,1,0:T(8,128)S(1)}, u32[]{:S(2)}, u32[]{:S(2)}) collective-permute-start(f32[3,4,4,8,128]{4,3,2,1,0:T(8,128)S(1)} %get-tuple-element.17), channel_id=1, source_target_pairs={{0,17},{1,18},{2,19},{3,20},{4,21},{5,22},{6,23},{7,24},{8,25},{9,... | collective-permute-start | bytes 589832 | tf_op jit(solution)/shard_map/ppermute | solution.py:415
  48.0 1.1 copy-start.1
  49.0 0.8 copy-start.8
  52.6 5.2 %collective-permute-start.5 = (f32[2,3,8,128]{3,2,1,0:T(8,128)}, f32[2,3,8,128]{3,2,1,0:T(8,128)S(1)}, u32[]{:S(2)}, u32[]{:S(2)}) collective-permute-start(f32[2,3,8,128]{3,2,1,0:T(8,128)} %get-tuple-element.20.own_ref), channel_id=1, source_target_pairs={{0,16},{1,17},{2,18},{3,19},{4,20},{5,21},{6,22},{7,23},{8,24},{9,... | collective-permute-start | bytes 73736 | tf_op jit(solution)/shard_map/ppermute | solution.py:415
  58.9 11.1 %collective-permute-start.6 = (f32[4,3,8,128]{3,2,1,0:T(8,128)S(1)}, f32[4,3,8,128]{3,2,1,0:T(8,128)S(1)}, u32[]{:S(2)}, u32[]{:S(2)}) collective-permute-start(f32[4,3,8,128]{3,2,1,0:T(8,128)S(1)} %round1.1.own_ref), channel_id=1, source_target_pairs={{0,32},{1,33},{2,34},{3,35},{4,36},{5,37},{6,38},{7,39},{8,40},{9,... | collective-permute-start | bytes 147464 | tf_op jit(solution)/shard_map/ppermute | solution.py:415
  71.0 10.3 %collective-permute-start.7 = (f32[8,3,8,128]{3,2,1,0:T(8,128)S(1)}, f32[8,3,8,128]{3,2,1,0:T(8,128)S(1)}, u32[]{:S(2)}, u32[]{:S(2)}) collective-permute-start(f32[8,3,8,128]{3,2,1,0:T(8,128)S(1)} %round2.1.own_ref), channel_id=1, source_target_pairs={{0,64},{1,65},{2,66},{3,67},{4,68},{5,69},{6,70},{7,71},{8,72},{9,... | collective-permute-start | bytes 294920 | tf_op jit(solution)/shard_map/ppermute | solution.py:415
  83.0 9.3 %collective-permute-start.8 = (f32[16,3,8,128]{3,2,1,0:T(8,128)S(1)}, f32[16,3,8,128]{3,2,1,0:T(8,128)S(1)}, u32[]{:S(2)}, u32[]{:S(2)}) collective-permute-start(f32[16,3,8,128]{3,2,1,0:T(8,128)S(1)} %round4.1.own_ref), channel_id=1, source_target_pairs={{0,128},{1,129},{2,130},{3,131},{4,132},{5,133},{6,134},{7,135},{8... | collective-permute-start | bytes 589832 | tf_op jit(solution)/shard_map/ppermute | solution.py:415
  132.5 16.7 %collective-permute-start.9 = (f32[2,3,8,128]{3,2,1,0:T(8,128)S(1)}, f32[2,3,8,128]{3,2,1,0:T(8,128)S(1)}, u32[]{:S(2)}, u32[]{:S(2)}) collective-permute-start(f32[2,3,8,128]{3,2,1,0:T(8,128)S(1)} %get-tuple-element.21), channel_id=1, source_target_pairs={{0,16},{1,17},{2,18},{3,19},{4,20},{5,21},{6,22},{7,23},{8,24},{9,... | collective-permute-start | bytes 73736 | tf_op jit(solution)/shard_map/ppermute | solution.py:415
  133.8 16.9 %collective-permute-start.10 = (f32[2,3,8,128]{3,2,1,0:T(8,128)S(1)}, f32[2,3,8,128]{3,2,1,0:T(8,128)S(1)}, u32[]{:S(2)}, u32[]{:S(2)}) collective-permute-start(f32[2,3,8,128]{3,2,1,0:T(8,128)S(1)} %get-tuple-element.22), channel_id=1, source_target_pairs={{0,272},{1,273},{2,274},{3,275},{4,276},{5,277},{6,278},{7,279},{8... | collective-permute-start | bytes 73736 | tf_op jit(solution)/shard_map/ppermute | solution.py:415

commit v4 on v3

--- a/solution.py
+++ b/solution.py
@@ -5,6 +5,7 @@
 from jax.experimental import pallas as pl
 from jax.experimental.pallas import tpu as pltpu
 from jax.sharding import PartitionSpec as P
+
 
 STEPS = 4
 KAPPA = 0.04
@@ -88,7 +89,7 @@
     return pl.CostEstimate(flops=flops, bytes_accessed=moved, transcendentals=0)
 
 
-def march4(coefs, first, second, base):
+def march4(coefs, first, second):
     src, dst = first, second
     for k in range(1, STEPS + 1):
         def layer(l, carry, src=src, dst=dst):
@@ -123,24 +124,7 @@
     return out
 
 
-def fine1_kernel(pos_ref, m1_ref, own_ref, p1_ref, start_ref, after_ref, coefs, speed_c_ref, share_ref,
-                 state_a, state_b, begin, speed, share, ev, od, sems):
-    slab = pos_ref[0]
-    depth = pos_ref[2]
-    perm = lane_parity()
-    for i, ref in enumerate((m1_ref, own_ref, p1_ref)):
-        rows = ref[...].reshape(384, 256)
-        both = jnp.dot(rows, perm, precision=HI, preferred_element_type=F32)
-        ev[...] = both[:, :128]
-        od[...] = both[:, 128:]
-        for part, dest in ((0, state_a), (1, speed)):
-            for q in range(2):
-                for p, half in ((0, ev), (1, od)):
-                    got = half[pl.ds(192 * part + q, 96, stride=2), :]
-                    dest[:, 4 * i:4 * i + 4, 2 * q + p] = got.reshape(3, 4, 8, 128)
-    begin[...] = state_a[...]
-    keep = pltpu.make_async_copy(begin, start_ref, sems.at[0])
-    keep.start()
+def fine_coefs(slab, depth, speed, coefs):
     sub, lane = iotas()
 
     def build(l, carry):
@@ -173,15 +157,51 @@
         return carry
 
     lax.fori_loop(1, NL - 1, build, 0)
-    for j in range(1, 5):
+
+
+def split_kernel(c_ref, u_ref, out_ref, ev, od):
+    perm = lane_parity()
+    for part, ref in ((0, c_ref), (1, u_ref)):
+        both = jnp.dot(ref[...].reshape(192, 256), perm, precision=HI, preferred_element_type=F32)
+        ev[part] = both[:, :128]
+        od[part] = both[:, 128:]
+        for q in range(2):
+            for p, half in ((0, ev), (1, od)):
+                got = half[part, pl.ds(q, 96, stride=2), :]
+                out_ref[3 * part:3 * part + 3, :, 2 * q + p] = got.reshape(3, 4, 8, 128)
+
+
+def split_fields(c, u):
+    return pl.pallas_call(
+        split_kernel,
+        out_shape=shaped(6, 4, 4, 8, 128),
+        in_specs=[VSPEC] * 2,
+        out_specs=VSPEC,
+        scratch_shapes=[pltpu.VMEM((2, 192, 128), F32)] * 2,
+        compiler_params=pltpu.CompilerParams(vmem_limit_bytes=GRANT),
+        cost_estimate=cost(50_000_000, 800_000),
+        name="split",
+    )(c, u)
+
+
+def fine1_kernel(pos_ref, m1_ref, own_ref, p1_ref, start_ref, after_ref, speed, share_ref,
+                 state_a, state_b, begin, coefs, share, sems):
+    slab = pos_ref[0]
+    depth = pos_ref[2]
+    for i, ref in enumerate((m1_ref, own_ref, p1_ref)):
+        state_a[:, 4 * i:4 * i + 4] = ref[0:3]
+        begin[:, 4 * i:4 * i + 4] = ref[0:3]
+        speed[:, 4 * i:4 * i + 4] = ref[3:6]
+    keep = pltpu.make_async_copy(begin, start_ref, sems.at[0])
+    keep.start()
+    for j in (2, 3):
         for c, v in enumerate(restrict(speed, j)):
-            speed_c_ref[j - 1, c] = 2.0 * v
-            if j in (2, 3):
-                for to in range(share.shape[0]):
-                    share[to, j - 2, c] = 2.0 * v
+            for to in range(share.shape[0]):
+                share[to, j - 2, c] = 2.0 * v
     send = pltpu.make_async_copy(share, share_ref, sems.at[1])
     send.start()
-    march4(coefs, state_a, state_b, 0)
+    fine_coefs(slab, depth, speed, coefs)
+    march4(coefs, state_a, state_b)
     after_ref[...] = state_a[:, 4:8]
     keep.wait()
     send.wait()
@@ -190,19 +210,19 @@
 def fine1(pos, m1, own, p1, slabs):
     return pl.pallas_call(
         fine1_kernel,
-        out_shape=(shaped(3, NL, 4, 8, 128), shaped(3, 4, 4, 8, 128), shaped(NL, 4, 15, 8, 128),
-                   shaped(4, 3, 8, 128), shaped(slabs, 2, 3, 8, 128)),
+        out_shape=(shaped(3, NL, 4, 8, 128), shaped(3, 4, 4, 8, 128), shaped(3, NL, 4, 8, 128),
+                   shaped(slabs, 2, 3, 8, 128)),
         in_specs=[SSPEC] + [VSPEC] * 3,
-        out_specs=(HSPEC, VSPEC, VSPEC, VSPEC, HSPEC),
-        scratch_shapes=[pltpu.VMEM((3, NL, 4, 8, 128), F32)] * 4 + [pltpu.VMEM((slabs, 2, 3, 8, 128), F32)]
-        + [pltpu.VMEM((384, 128), F32)] * 2 + [pltpu.SemaphoreType.DMA((2,))],
+        out_specs=(HSPEC, VSPEC, VSPEC, HSPEC),
+        scratch_shapes=[pltpu.VMEM((3, NL, 4, 8, 128), F32)] * 3 + [pltpu.VMEM((NL, 4, 15, 8, 128), F32)]
+        + [pltpu.VMEM((slabs, 2, 3, 8, 128), F32), pltpu.SemaphoreType.DMA((2,))],
         compiler_params=pltpu.CompilerParams(vmem_limit_bytes=GRANT),
         cost_estimate=cost(10_000_000, 6_000_000),
         name="fine1",
     )(pos, m1, own, p1)
 
 
-def fine2_kernel(pos_ref, coefs, speed_c, start_ref, m1_ref, own_ref, p1_ref, relaxed_ref, forcing_ref, state_a, state_b, sem):
+def fine2_kernel(pos_ref, speed, start_ref, m1_ref, own_ref, p1_ref, relaxed_ref, forcing_ref, state_a, state_b, coefs, sem):
     slab = pos_ref[0]
     first = pos_ref[1] == 1
     depth = pos_ref[2]
@@ -217,13 +237,15 @@
         for i, ref in enumerate((m1_ref, own_ref, p1_ref)):
             state_a[:, 4 * i:4 * i + 4] = ref[...]
     relaxed_ref[...] = state_a[:, 4:8]
+    fine_coefs(slab, depth, speed, coefs)
     coarse = {j: restrict(state_a, j) for j in range(1, 5)}
+    speed_c = {j: [2.0 * v for v in restrict(speed, j)] for j in range(1, 5)}
     image = {}
     for j in (2, 3):
         cc = {}
-        coarse_coefs(*[[speed_c[i, c] for c in range(3)] for i in (j - 2, j - 1, j)], jnp.float32(1.0), cc.__setitem__)
+        coarse_coefs(*[speed_c[i] for i in (j - 1, j, j + 1)], jnp.float32(1.0), cc.__setitem__)
         image[j] = psi(cc.__getitem__, coarse[j - 1], coarse[j], coarse[j + 1])
-    march4(coefs, state_a, state_b, 0)
+    march4(coefs, state_a, state_b)
     for i, j in enumerate((2, 3)):
         again = restrict(state_a, j)
         for c in range(3):
@@ -232,17 +254,18 @@
             forcing_ref[i, c] = forcing
 
 
-def fine2(pos, coefs, speed_c, start, m1, own, p1):
+def fine2(pos, speed, start, m1, own, p1):
     return pl.pallas_call(
         fine2_kernel,
         out_shape=(shaped(3, 4, 4, 8, 128), shaped(2, 3, 8, 128)),
-        in_specs=[SSPEC, VSPEC, VSPEC, HSPEC] + [VSPEC] * 3,
+        in_specs=[SSPEC, VSPEC, HSPEC] + [VSPEC] * 3,
         out_specs=(VSPEC,) * 2,
-        scratch_shapes=[pltpu.VMEM((3, NL, 4, 8, 128), F32)] * 2 + [pltpu.SemaphoreType.DMA],
+        scratch_shapes=[pltpu.VMEM((3, NL, 4, 8, 128), F32)] * 2
+        + [pltpu.VMEM((NL, 4, 15, 8, 128), F32), pltpu.SemaphoreType.DMA],
         compiler_params=pltpu.CompilerParams(vmem_limit_bytes=GRANT),
         cost_estimate=cost(10_000_000, 6_000_000),
         name="fine2",
-    )(pos, coefs, speed_c, start, m1, own, p1)
+    )(pos, speed, start, m1, own, p1)
 
 
 def coefs_kernel(speed_ref, coefs):
@@ -348,7 +371,6 @@
         scratch_shapes=[pltpu.VMEM((layers + 2, 3, 8, 128), F32)] * 2,
         compiler_params=pltpu.CompilerParams(vmem_limit_bytes=GRANT),
         cost_estimate=cost((3 if final else 1) * distance * 2_000_000, 3_000_000),
-        name=f"round{distance}",
     )(pos, coefs, own, got)
 
 
@@ -421,11 +443,13 @@
     slabs = lax.axis_size("gz")
     depth = slabs * velocity.shape[1]
     pos = jnp.stack([slab, (t == 0).astype(jnp.int32), jnp.int32(depth)])
-    own = jnp.concatenate([c_states[0], velocity], axis=0)
-    start, after, coefs, speed_c, share = fine1(pos, moved(own, 0, 1), own, moved(own, 0, -1), slabs)
-    m1, same, p1 = [moved(after, 1, by) for by in (1, 0, -1)]
+    own = split_fields(c_states[0], velocity)
+    start, after, velocity_ext, share = fine1(pos, moved(own, 0, 1), own, moved(own, 0, -1), slabs)
+    around = []
+    for by in (1, 0, -1):
+        around.append(moved(after, 1, by))
     speed = lax.all_to_all(share, "gz", 0, 0, tiled=True)
-    relaxed, state = fine2(pos, coefs, speed_c, start, m1, same, p1)
+    relaxed, state = fine2(pos, velocity_ext, start, *around)
     coefs = sweep_coefs(speed.reshape(2 * slabs, 3, 8, 128))
     for distance in (1, 2, 4, 8):
         state = sweep_round(distance, distance - 1, distance == 8, pos, coefs, state, moved(state, distance, 0))

time: 153 us -> 146 us (0.954)
  local copies, waits for them, and re-layouts: 7.53 us -> 1.85 us
    unnamed x18 -> x4, local copies, waits for them, and re-layouts: 7.53 us -> 1.85 us
where the time goes in v4:
time: 146 us
  starting transfers between devices  70.3 us (48%)
  blocking collectives  28.4 us (19%)
  Pallas kernels  25.4 us (17%)
  waiting for transfers between devices  19.7 us (13%)
  local copies, waits for them, and re-layouts  1.85 us (1%)
    ppermute x11, starting transfers between devices, moved(): return lax.ppermute(block, ('tm', 'gz'), route)  63.2 us
    all_to_all x1, blocking collectives, local(): near, far = totals(lax.all_to_all(state, 'gz', 0, 0, tiled=True))  28.4 us
    ppermute x11, waiting for transfers between devices, moved(): return lax.ppermute(block, ('tm', 'gz'), route)  19.7 us
    pallas_call x4, Pallas kernels, sweep_round(): pl.pallas_call(functools.partial(final_kernel if final else round_kernel,...  15.8 us
    all_to_all x1, starting transfers between devices, local(): speed = lax.all_to_all(share, 'gz', 0, 0, tiled=True)  7.16 us
    pallas_call x1, Pallas kernels, fine1(): pl.pallas_call(fine1_kernel, out_shape=(shaped(3, NL, 4, 8, 128), shaped(...  3.03 us
    pallas_call x1, Pallas kernels, fine2(): pl.pallas_call(fine2_kernel, out_shape=(shaped(3, 4, 4, 8, 128), shaped(2...  3 us
  transfers between devices with their start and end apart: 12, of which 8 were waited for; matrix products, arithmetic and copies ran while one was open for 0% of the time, Pallas kernels for 3%

profile of v4, /device:TPU:8, one launch (start us, length us, event | category | flops | bytes accessed | tf_op | source)
XLA Modules:
  0.0 145.9 jit_solution(8424453264013738690)
XLA Ops:
  0.0 0.0 copy-start
  0.0 0.9 copy-done
  0.9 0.0 copy-start.1
  0.9 0.9 copy-done.1
  1.9 0.5 split.1.own_ref
  2.4 7.7 %collective-permute-start.1 = (f32[6,4,4,8,128]{4,3,2,1,0:T(8,128)S(1)}, f32[6,4,4,8,128]{4,3,2,1,0:T(8,128)S(1)}, u32[]{:S(2)}, u32[]{:S(2)}) collective-permute-start(f32[6,4,4,8,128]{4,3,2,1,0:T(8,128)S(1)} %split.1.own_ref), channel_id=1, source_target_pairs={{1,0},{2,1},{3,2},{4,3},{5,4},{6,5},{7,6},{8,7},{9,8},{10,9},{11,1... | collective-permute-start | bytes 1179656 | tf_op jit(solution)/shard_map/ppermute | solution.py:437
  10.1 1.9 %collective-permute-start = (f32[6,4,4,8,128]{4,3,2,1,0:T(8,128)S(1)}, f32[6,4,4,8,128]{4,3,2,1,0:T(8,128)S(1)}, u32[]{:S(2)}, u32[]{:S(2)}) collective-permute-start(f32[6,4,4,8,128]{4,3,2,1,0:T(8,128)S(1)} %split.1.own_ref), channel_id=1, source_target_pairs={{0,1},{1,2},{2,3},{3,4},{4,5},{5,6},{6,7},{7,8},{8,9},{9,10},{10,1... | collective-permute-start | bytes 1179656 | tf_op jit(solution)/shard_map/ppermute | solution.py:437
  12.0 0.1 pad_add_fusion.pos_ref
  12.1 3.3 %collective-permute-done.1.p1_ref = f32[6,4,4,8,128]{4,3,2,1,0:T(8,128)S(1)} collective-permute-done((f32[6,4,4,8,128]{4,3,2,1,0:T(8,128)S(1)}, f32[6,4,4,8,128]{4,3,2,1,0:T(8,128)S(1)}, u32[]{:S(2)}, u32[]{:S(2)}) %collective-permute-start.1) | collective-permute-done | bytes 393248 | tf_op jit(solution)/shard_map/ppermute | solution.py:437
  15.4 4.4 %collective-permute-done.m1_ref = f32[6,4,4,8,128]{4,3,2,1,0:T(8,128)S(1)} collective-permute-done((f32[6,4,4,8,128]{4,3,2,1,0:T(8,128)S(1)}, f32[6,4,4,8,128]{4,3,2,1,0:T(8,128)S(1)}, u32[]{:S(2)}, u32[]{:S(2)}) %collective-permute-start) | collective-permute-done | bytes 393248 | tf_op jit(solution)/shard_map/ppermute | solution.py:437
  19.8 3.0 %fine1.1 = (f32[3,12,4,8,128]{4,3,2,1,0:T(8,128)S(1)}, f32[3,4,4,8,128]{4,3,2,1,0:T(8,128)S(1)}, f32[3,12,4,8,128]{4,3,2,1,0:T(8,128)S(1)}, f32[16,2,3,8,128]{4,3,2,1,0:T(8,128)}) custom-call(s32[3]{0:T(128)S(1)} %pad_add_fusion.pos_ref, f32[6,4,4,8,128]{4,3,2,1,0:T(8,128)S(1)} %collective-permute-done.m1_ref, f32[6,4,4,8,128]{4,3,2,1,0:T(8,128)S(1)} %split.1.own_ref, ...), custom_call_target="tpu_custom_call" | custom-call | flops 10000000 | bytes 6000000 | tf_op jit(solution)/shard_map/fine1/pallas_call | solution.py:211
  22.8 7.2 %all-to-all-start = ((f32[16,2,3,8,128]{4,3,2,1,0:T(8,128)}), f32[16,2,3,8,128]{4,3,2,1,0:T(8,128)S(1)}, u32[]{:S(2)}, u32[]{:S(2)}) async-start(f32[16,2,3,8,128]{4,3,2,1,0:T(8,128)} %get-tuple-element.17), calls=%async_computation | async-start | bytes 786432 | tf_op jit(solution)/shard_map/all_to_all | solution.py:451
  30.0 1.3 collective-permute-start.4
  31.3 4.9 %collective-permute-start.3 = (f32[3,4,4,8,128]{4,3,2,1,0:T(8,128)S(1)}, f32[3,4,4,8,128]{4,3,2,1,0:T(8,128)S(1)}, u32[]{:S(2)}, u32[]{:S(2)}) collective-permute-start(f32[3,4,4,8,128]{4,3,2,1,0:T(8,128)S(1)} %get-tuple-element.15), channel_id=1, source_target_pairs={{0,16},{1,17},{2,18},{3,19},{4,20},{5,21},{6,22},{7,23},{8,24},{9,... | collective-permute-start | bytes 589832 | tf_op jit(solution)/shard_map/ppermute | solution.py:437
  36.2 3.4 %collective-permute-start.2 = (f32[3,4,4,8,128]{4,3,2,1,0:T(8,128)S(1)}, f32[3,4,4,8,128]{4,3,2,1,0:T(8,128)S(1)}, u32[]{:S(2)}, u32[]{:S(2)}) collective-permute-start(f32[3,4,4,8,128]{4,3,2,1,0:T(8,128)S(1)} %get-tuple-element.15), channel_id=1, source_target_pairs={{0,17},{1,18},{2,19},{3,20},{4,21},{5,22},{6,23},{7,24},{8,25},{9,... | collective-permute-start | bytes 589832 | tf_op jit(solution)/shard_map/ppermute | solution.py:437
  39.6 1.7 %collective-permute-done.4.p1_ref = f32[3,4,4,8,128]{4,3,2,1,0:T(8,128)S(1)} collective-permute-done((f32[3,4,4,8,128]{4,3,2,1,0:T(8,128)S(1)}, f32[3,4,4,8,128]{4,3,2,1,0:T(8,128)S(1)}, u32[]{:S(2)}, u32[]{:S(2)}) %collective-permute-start.4) | collective-permute-done | bytes 196640 | tf_op jit(solution)/shard_map/ppermute | solution.py:437
  41.4 0.0 collective-permute-done.3.own_ref
  41.4 1.7 %collective-permute-done.2.m1_ref = f32[3,4,4,8,128]{4,3,2,1,0:T(8,128)S(1)} collective-permute-done((f32[3,4,4,8,128]{4,3,2,1,0:T(8,128)S(1)}, f32[3,4,4,8,128]{4,3,2,1,0:T(8,128)S(1)}, u32[]{:S(2)}, u32[]{:S(2)}) %collective-permute-start.2) | collective-permute-done | bytes 196640 | tf_op jit(solution)/shard_map/ppermute | solution.py:437
  43.1 3.0 %fine2.1 = (f32[3,4,4,8,128]{4,3,2,1,0:T(8,128)S(1)}, f32[2,3,8,128]{3,2,1,0:T(8,128)S(1)}) custom-call(s32[3]{0:T(128)S(1)} %pad_add_fusion.pos_ref, f32[3,12,4,8,128]{4,3,2,1,0:T(8,128)S(1)} %get-tuple-element.13.speed, f32[3,12,4,8,128]{4,3,2,1,0:T(8,128)S(1)} %get-tuple-element.14.start_ref, f32[3,4,4,8,128]{4,3,2,1,0:T(8,128)S(1)} %collective-permute-done.2.m1_ref, ...), custom_call_target="tpu_custom_call" | custom-call | flops 10000000 | bytes 6000000 | tf_op jit(solution)/shard_map/fine2/pallas_call | solution.py:258
  46.1 3.8 %collective-permute-start.5 = (f32[2,3,8,128]{3,2,1,0:T(8,128)S(1)}, f32[2,3,8,128]{3,2,1,0:T(8,128)S(1)}, u32[]{:S(2)}, u32[]{:S(2)}) collective-permute-start(f32[2,3,8,128]{3,2,1,0:T(8,128)S(1)} %get-tuple-element.18.own_ref), channel_id=1, source_target_pairs={{0,16},{1,17},{2,18},{3,19},{4,20},{5,21},{6,22},{7,23},{8,24},{9,... | collective-permute-start | bytes 73736 | tf_op jit(solution)/shard_map/ppermute | solution.py:437
  49.9 0.0 all-to-all-done
  49.9 1.4 coefs.1
  51.3 0.0 collective-permute-done.5.got_ref
  51.3 0.9 shard_map.28.own_ref
  52.1 9.1 %collective-permute-start.6 = (f32[4,3,8,128]{3,2,1,0:T(8,128)S(1)}, f32[4,3,8,128]{3,2,1,0:T(8,128)S(1)}, u32[]{:S(2)}, u32[]{:S(2)}) collective-permute-start(f32[4,3,8,128]{3,2,1,0:T(8,128)S(1)} %shard_map.28.own_ref), channel_id=1, source_target_pairs={{0,32},{1,33},{2,34},{3,35},{4,36},{5,37},{6,38},{7,39},{8,40},{9,... | collective-permute-start | bytes 147464 | tf_op jit(solution)/shard_map/ppermute | solution.py:437
  61.2 1.7 %collective-permute-done.6.got_ref = f32[4,3,8,128]{3,2,1,0:T(8,128)S(1)} collective-permute-done((f32[4,3,8,128]{3,2,1,0:T(8,128)S(1)}, f32[4,3,8,128]{3,2,1,0:T(8,128)S(1)}, u32[]{:S(2)}, u32[]{:S(2)}) %collective-permute-start.6) | collective-permute-done | bytes 49184 | tf_op jit(solution)/shard_map/ppermute | solution.py:437
  63.0 1.0 shard_map.29.own_ref
  64.0 8.1 %collective-permute-start.7 = (f32[8,3,8,128]{3,2,1,0:T(8,128)S(1)}, f32[8,3,8,128]{3,2,1,0:T(8,128)S(1)}, u32[]{:S(2)}, u32[]{:S(2)}) collective-permute-start(f32[8,3,8,128]{3,2,1,0:T(8,128)S(1)} %shard_map.29.own_ref), channel_id=1, source_target_pairs={{0,64},{1,65},{2,66},{3,67},{4,68},{5,69},{6,70},{7,71},{8,72},{9,... | collective-permute-start | bytes 294920 | tf_op jit(solution)/shard_map/ppermute | solution.py:437
  72.1 2.2 %collective-permute-done.7.got_ref = f32[8,3,8,128]{3,2,1,0:T(8,128)S(1)} collective-permute-done((f32[8,3,8,128]{3,2,1,0:T(8,128)S(1)}, f32[8,3,8,128]{3,2,1,0:T(8,128)S(1)}, u32[]{:S(2)}, u32[]{:S(2)}) %collective-permute-start.7) | collective-permute-done | bytes 98336 | tf_op jit(solution)/shard_map/ppermute | solution.py:437
  74.3 1.7 %shard_map.30.own_ref = f32[16,3,8,128]{3,2,1,0:T(8,128)S(1)} custom-call(s32[3]{0:T(128)S(1)} %pad_add_fusion.pos_ref, f32[32,15,8,128]{3,2,1,0:T(8,128)S(1)} %coefs.1, f32[8,3,8,128]{3,2,1,0:T(8,128)S(1)} %shard_map.29.own_ref, f32[8,3,8,128]{3,2,1,0:T(8,128)S(1)} %collective-permute-done.7.got_ref), custom_call_target="tpu_custom_call" | custom-call | flops 8000000 | bytes 3000000 | tf_op jit(solution)/shard_map/pallas_call | solution.py:366
  76.0 6.1 %collective-permute-start.8 = (f32[16,3,8,128]{3,2,1,0:T(8,128)S(1)}, f32[16,3,8,128]{3,2,1,0:T(8,128)S(1)}, u32[]{:S(2)}, u32[]{:S(2)}) collective-permute-start(f32[16,3,8,128]{3,2,1,0:T(8,128)S(1)} %shard_map.30.own_ref), channel_id=1, source_target_pairs={{0,128},{1,129},{2,130},{3,131},{4,132},{5,133},{6,134},{7,135},{8... | collective-permute-start | bytes 589832 | tf_op jit(solution)/shard_map/ppermute | solution.py:437
  82.2 3.2 %collective-permute-done.8.got_ref = f32[16,3,8,128]{3,2,1,0:T(8,128)S(1)} collective-permute-done((f32[16,3,8,128]{3,2,1,0:T(8,128)S(1)}, f32[16,3,8,128]{3,2,1,0:T(8,128)S(1)}, u32[]{:S(2)}, u32[]{:S(2)}) %collective-permute-start.8) | collective-permute-done | bytes 196640 | tf_op jit(solution)/shard_map/ppermute | solution.py:437
  85.4 12.2 %shard_map.31 = f32[16,2,2,3,8,128]{5,4,3,2,1,0:T(8,128)S(1)} custom-call(s32[3]{0:T(128)S(1)} %pad_add_fusion.pos_ref, f32[32,15,8,128]{3,2,1,0:T(8,128)S(1)} %coefs.1, f32[16,3,8,128]{3,2,1,0:T(8,128)S(1)} %shard_map.30.own_ref, f32[16,3,8,128]{3,2,1,0:T(8,128)S(1)} %collective-permute-done.8.got_ref), custom_call_target="tpu_custom_call" | custom-call | flops 48000000 | bytes 3000000 | tf_op jit(solution)/shard_map/pallas_call | solution.py:366
  97.5 28.4 %all_to_all.10.got_ref = f32[16,2,2,3,8,128]{5,4,3,2,1,0:T(8,128)S(1)} all-to-all(f32[16,2,2,3,8,128]{5,4,3,2,1,0:T(8,128)S(1)} %shard_map.31), channel_id=1, replica_groups=mesh['tm'=32,'gz'=16] {'gz'}, dimensions={0} | all-to-all | bytes 1572864 | tf_op jit(solution)/shard_map/all_to_all | solution.py:456
  126.0 1.3 collective-permute-start.9
  127.3 15.5 %collective-permute-start.10 = (f32[2,3,8,128]{3,2,1,0:T(8,128)S(1)}, f32[2,3,8,128]{3,2,1,0:T(8,128)S(1)}, u32[]{:S(2)}, u32[]{:S(2)}) collective-permute-start(f32[2,3,8,128]{3,2,1,0:T(8,128)S(1)} %get-tuple-element.20), channel_id=1, source_target_pairs={{0,272},{1,273},{2,274},{3,275},{4,276},{5,277},{6,278},{7,279},{8... | collective-permute-start | bytes 73736 | tf_op jit(solution)/shard_map/ppermute | solution.py:437
  142.8 0.0 collective-permute-done.9.near_ref
  142.8 1.5 %collective-permute-done.10.far_ref = f32[2,3,8,128]{3,2,1,0:T(8,128)S(1)} collective-permute-done((f32[2,3,8,128]{3,2,1,0:T(8,128)S(1)}, f32[2,3,8,128]{3,2,1,0:T(8,128)S(1)}, u32[]{:S(2)}, u32[]{:S(2)}) %collective-permute-start.10) | collective-permute-done | bytes 24608 | tf_op jit(solution)/shard_map/ppermute | solution.py:437
  144.3 1.6 %last.1 = f32[3,4,16,256]{3,2,1,0:T(8,128)} custom-call(s32[3]{0:T(128)S(1)} %pad_add_fusion.pos_ref, f32[3,4,4,8,128]{4,3,2,1,0:T(8,128)S(1)} %get-tuple-element.16.relaxed_ref, f32[2,3,8,128]{3,2,1,0:T(8,128)S(1)} %collective-permute-done.9.near_ref, f32[2,3,8,128]{3,2,1,0:T(8,128)S(1)} %collective-permute-done.10.far_ref), custom_call_target="tpu_custom_call" | custom-call | flops 2000000 | bytes 500000 | tf_op jit(solution)/shard_map/last/pallas_call | solution.py:418
  (1 shorter events, 0.0 us)
Async XLA Ops:
  0.0 0.9 copy-start
  0.9 0.9 copy-start.1
  2.4 13.0 %collective-permute-start.1 = (f32[6,4,4,8,128]{4,3,2,1,0:T(8,128)S(1)}, f32[6,4,4,8,128]{4,3,2,1,0:T(8,128)S(1)}, u32[]{:S(2)}, u32[]{:S(2)}) collective-permute-start(f32[6,4,4,8,128]{4,3,2,1,0:T(8,128)S(1)} %split.1.own_ref), channel_id=1, source_target_pairs={{1,0},{2,1},{3,2},{4,3},{5,4},{6,5},{7,6},{8,7},{9,8},{10,9},{11,1... | collective-permute-start | bytes 1179656 | tf_op jit(solution)/shard_map/ppermute | solution.py:437
  10.1 9.7 %collective-permute-start = (f32[6,4,4,8,128]{4,3,2,1,0:T(8,128)S(1)}, f32[6,4,4,8,128]{4,3,2,1,0:T(8,128)S(1)}, u32[]{:S(2)}, u32[]{:S(2)}) collective-permute-start(f32[6,4,4,8,128]{4,3,2,1,0:T(8,128)S(1)} %split.1.own_ref), channel_id=1, source_target_pairs={{0,1},{1,2},{2,3},{3,4},{4,5},{5,6},{6,7},{7,8},{8,9},{9,10},{10,1... | collective-permute-start | bytes 1179656 | tf_op jit(solution)/shard_map/ppermute | solution.py:437
  22.8 27.1 %all-to-all-start = ((f32[16,2,3,8,128]{4,3,2,1,0:T(8,128)}), f32[16,2,3,8,128]{4,3,2,1,0:T(8,128)S(1)}, u32[]{:S(2)}, u32[]{:S(2)}) async-start(f32[16,2,3,8,128]{4,3,2,1,0:T(8,128)} %get-tuple-element.17), calls=%async_computation | async-start | bytes 786432 | tf_op jit(solution)/shard_map/all_to_all | solution.py:451
  30.0 11.4 %collective-permute-start.4 = (f32[3,4,4,8,128]{4,3,2,1,0:T(8,128)S(1)}, f32[3,4,4,8,128]{4,3,2,1,0:T(8,128)S(1)}, u32[]{:S(2)}, u32[]{:S(2)}) collective-permute-start(f32[3,4,4,8,128]{4,3,2,1,0:T(8,128)S(1)} %get-tuple-element.15), channel_id=1, source_target_pairs={{1,16},{2,17},{3,18},{4,19},{5,20},{6,21},{7,22},{8,23},{9,24},{10... | collective-permute-start | bytes 589832 | tf_op jit(solution)/shard_map/ppermute | solution.py:437
  31.3 10.1 %collective-permute-start.3 = (f32[3,4,4,8,128]{4,3,2,1,0:T(8,128)S(1)}, f32[3,4,4,8,128]{4,3,2,1,0:T(8,128)S(1)}, u32[]{:S(2)}, u32[]{:S(2)}) collective-permute-start(f32[3,4,4,8,128]{4,3,2,1,0:T(8,128)S(1)} %get-tuple-element.15), channel_id=1, source_target_pairs={{0,16},{1,17},{2,18},{3,19},{4,20},{5,21},{6,22},{7,23},{8,24},{9,... | collective-permute-start | bytes 589832 | tf_op jit(solution)/shard_map/ppermute | solution.py:437
  36.2 6.9 %collective-permute-start.2 = (f32[3,4,4,8,128]{4,3,2,1,0:T(8,128)S(1)}, f32[3,4,4,8,128]{4,3,2,1,0:T(8,128)S(1)}, u32[]{:S(2)}, u32[]{:S(2)}) collective-permute-start(f32[3,4,4,8,128]{4,3,2,1,0:T(8,128)S(1)} %get-tuple-element.15), channel_id=1, source_target_pairs={{0,17},{1,18},{2,19},{3,20},{4,21},{5,22},{6,23},{7,24},{8,25},{9,... | collective-permute-start | bytes 589832 | tf_op jit(solution)/shard_map/ppermute | solution.py:437
  46.1 5.2 %collective-permute-start.5 = (f32[2,3,8,128]{3,2,1,0:T(8,128)S(1)}, f32[2,3,8,128]{3,2,1,0:T(8,128)S(1)}, u32[]{:S(2)}, u32[]{:S(2)}) collective-permute-start(f32[2,3,8,128]{3,2,1,0:T(8,128)S(1)} %get-tuple-element.18.own_ref), channel_id=1, source_target_pairs={{0,16},{1,17},{2,18},{3,19},{4,20},{5,21},{6,22},{7,23},{8,24},{9,... | collective-permute-start | bytes 73736 | tf_op jit(solution)/shard_map/ppermute | solution.py:437
  52.1 10.9 %collective-permute-start.6 = (f32[4,3,8,128]{3,2,1,0:T(8,128)S(1)}, f32[4,3,8,128]{3,2,1,0:T(8,128)S(1)}, u32[]{:S(2)}, u32[]{:S(2)}) collective-permute-start(f32[4,3,8,128]{3,2,1,0:T(8,128)S(1)} %shard_map.28.own_ref), channel_id=1, source_target_pairs={{0,32},{1,33},{2,34},{3,35},{4,36},{5,37},{6,38},{7,39},{8,40},{9,... | collective-permute-start | bytes 147464 | tf_op jit(solution)/shard_map/ppermute | solution.py:437
  64.0 10.3 %collective-permute-start.7 = (f32[8,3,8,128]{3,2,1,0:T(8,128)S(1)}, f32[8,3,8,128]{3,2,1,0:T(8,128)S(1)}, u32[]{:S(2)}, u32[]{:S(2)}) collective-permute-start(f32[8,3,8,128]{3,2,1,0:T(8,128)S(1)} %shard_map.29.own_ref), channel_id=1, source_target_pairs={{0,64},{1,65},{2,66},{3,67},{4,68},{5,69},{6,70},{7,71},{8,72},{9,... | collective-permute-start | bytes 294920 | tf_op jit(solution)/shard_map/ppermute | solution.py:437
  76.0 9.3 %collective-permute-start.8 = (f32[16,3,8,128]{3,2,1,0:T(8,128)S(1)}, f32[16,3,8,128]{3,2,1,0:T(8,128)S(1)}, u32[]{:S(2)}, u32[]{:S(2)}) collective-permute-start(f32[16,3,8,128]{3,2,1,0:T(8,128)S(1)} %shard_map.30.own_ref), channel_id=1, source_target_pairs={{0,128},{1,129},{2,130},{3,131},{4,132},{5,133},{6,134},{7,135},{8... | collective-permute-start | bytes 589832 | tf_op jit(solution)/shard_map/ppermute | solution.py:437
  126.0 16.8 %collective-permute-start.9 = (f32[2,3,8,128]{3,2,1,0:T(8,128)S(1)}, f32[2,3,8,128]{3,2,1,0:T(8,128)S(1)}, u32[]{:S(2)}, u32[]{:S(2)}) collective-permute-start(f32[2,3,8,128]{3,2,1,0:T(8,128)S(1)} %get-tuple-element.19), channel_id=1, source_target_pairs={{0,16},{1,17},{2,18},{3,19},{4,20},{5,21},{6,22},{7,23},{8,24},{9,... | collective-permute-start | bytes 73736 | tf_op jit(solution)/shard_map/ppermute | solution.py:437
  127.3 17.0 %collective-permute-start.10 = (f32[2,3,8,128]{3,2,1,0:T(8,128)S(1)}, f32[2,3,8,128]{3,2,1,0:T(8,128)S(1)}, u32[]{:S(2)}, u32[]{:S(2)}) collective-permute-start(f32[2,3,8,128]{3,2,1,0:T(8,128)S(1)} %get-tuple-element.20), channel_id=1, source_target_pairs={{0,272},{1,273},{2,274},{3,275},{4,276},{5,277},{6,278},{7,279},{8... | collective-permute-start | bytes 73736 | tf_op jit(solution)/shard_map/ppermute | solution.py:437

commit v5 on v4

--- a/solution.py
+++ b/solution.py
@@ -78,7 +78,7 @@
 VSPEC = pl.BlockSpec(memory_space=VM)
 HSPEC = pl.BlockSpec(memory_space=pltpu.MemorySpace.HBM)
 SSPEC = pl.BlockSpec(memory_space=pltpu.MemorySpace.SMEM)
-GRANT = 16 << 20
+PARAMS = pltpu.CompilerParams(vmem_limit_bytes=16 << 20)
 
 
 def shaped(*dims):
@@ -178,7 +178,7 @@
         in_specs=[VSPEC] * 2,
         out_specs=VSPEC,
         scratch_shapes=[pltpu.VMEM((2, 192, 128), F32)] * 2,
-        compiler_params=pltpu.CompilerParams(vmem_limit_bytes=GRANT),
+        compiler_params=PARAMS,
         cost_estimate=cost(50_000_000, 800_000),
         name="split",
     )(c, u)
@@ -216,7 +216,7 @@
         out_specs=(HSPEC, VSPEC, VSPEC, HSPEC),
         scratch_shapes=[pltpu.VMEM((3, NL, 4, 8, 128), F32)] * 3 + [pltpu.VMEM((NL, 4, 15, 8, 128), F32)]
         + [pltpu.VMEM((slabs, 2, 3, 8, 128), F32), pltpu.SemaphoreType.DMA((2,))],
-        compiler_params=pltpu.CompilerParams(vmem_limit_bytes=GRANT),
+        compiler_params=PARAMS,
         cost_estimate=cost(10_000_000, 6_000_000),
         name="fine1",
     )(pos, m1, own, p1)
@@ -262,26 +262,29 @@
         out_specs=(VSPEC,) * 2,
         scratch_shapes=[pltpu.VMEM((3, NL, 4, 8, 128), F32)] * 2
         + [pltpu.VMEM((NL, 4, 15, 8, 128), F32), pltpu.SemaphoreType.DMA],
-        compiler_params=pltpu.CompilerParams(vmem_limit_bytes=GRANT),
+        compiler_params=PARAMS,
         cost_estimate=cost(10_000_000, 6_000_000),
         name="fine2",
     )(pos, speed, start, m1, own, p1)
 
 
+def layer_coefs(speed_ref, j, store):
+    layers = speed_ref.shape[0]
+
+    def at(i):
+        keep = jnp.where(jnp.logical_and(i >= 0, i < layers), 1.0, 0.0).astype(F32)
+        k = jnp.clip(i, 0, layers - 1)
+        return [speed_ref[k, c] * keep for c in range(3)]
+    coarse_coefs(at(j - 1), at(j), at(j + 1), jnp.float32(1.0), store)
+
+
 def coefs_kernel(speed_ref, coefs):
-    layers = speed_ref.shape[0]
-
     def one(j, carry):
-        def at(i):
-            keep = jnp.where(jnp.logical_and(i >= 0, i < layers), 1.0, 0.0).astype(F32)
-            k = jnp.clip(i, 0, layers - 1)
-            return [speed_ref[k, c] * keep for c in range(3)]
-
         def store(i, x):
             coefs[j, i] = x
-        coarse_coefs(at(j - 1), at(j), at(j + 1), jnp.float32(1.0), store)
+        layer_coefs(speed_ref, j, store)
         return carry
-    lax.fori_loop(0, layers, one, 0, unroll=2)
+    lax.fori_loop(0, speed_ref.shape[0], one, 0, unroll=2)
 
 
 def sweep_coefs(speed):
@@ -290,7 +293,7 @@
         out_shape=shaped(speed.shape[0], 15, 8, 128),
         in_specs=[VSPEC],
         out_specs=VSPEC,
-        compiler_params=pltpu.CompilerParams(vmem_limit_bytes=GRANT),
+        compiler_params=PARAMS,
         cost_estimate=cost(3_000_000, 2_400_000),
         name="coefs",
     )(speed)
@@ -313,6 +316,35 @@
                 dst[j + 1, c] = new[c]
         return carry
     lax.fori_loop(low, high, some, 0)
+
+
+def first_kernel(pos_ref, speed_ref, near_ref, far_ref, out_ref, state, coefs):
+    slab = pos_ref[0]
+    n_out, at_out = window(slab, 1, speed_ref.shape[0])
+    state[...] = jnp.zeros_like(state)
+    inner = 2 * slab - at_out
+    state[pl.ds(inner + 1, 2)] = far_ref[...]
+    for i in range(n_out):
+        def store(n, x, i=i):
+            coefs[i, n] = x
+        layer_coefs(speed_ref, at_out + i, store)
+        new = psi(lambda n, i=i: coefs[i, n], *[[state[i + d, c] for c in range(3)] for d in range(3)])
+        for c in range(3):
+            out_ref[i, c] = new[c]
+    out_ref[pl.ds(inner, 2)] = out_ref[pl.ds(inner, 2)] + near_ref[...]
+
+
+def first_round(pos, speed, near, far):
+    return pl.pallas_call(
+        first_kernel,
+        out_shape=shaped(4, 3, 8, 128),
+        in_specs=[SSPEC] + [VSPEC] * 3,
+        out_specs=VSPEC,
+        scratch_shapes=[pltpu.VMEM((6, 3, 8, 128), F32), pltpu.VMEM((4, 15, 8, 128), F32)],
+        compiler_params=PARAMS,
+        cost_estimate=cost(1_000_000, 500_000),
+        name="round1",
+    )(pos, speed, near, far)
 
 
 def spread(distance, halo, slab, coefs, got_ref, state_a, state_b):
@@ -369,7 +401,7 @@
         in_specs=[SSPEC] + [VSPEC] * 3,
         out_specs=VSPEC,
         scratch_shapes=[pltpu.VMEM((layers + 2, 3, 8, 128), F32)] * 2,
-        compiler_params=pltpu.CompilerParams(vmem_limit_bytes=GRANT),
+        compiler_params=PARAMS,
         cost_estimate=cost((3 if final else 1) * distance * 2_000_000, 3_000_000),
     )(pos, coefs, own, got)
 
@@ -390,41 +422,75 @@
         out_shape=(shaped(2, 3, 8, 128),) * 2,
         in_specs=[VSPEC],
         out_specs=(VSPEC,) * 2,
-        compiler_params=pltpu.CompilerParams(vmem_limit_bytes=GRANT),
+        compiler_params=PARAMS,
         cost_estimate=cost(200_000, 850_000),
         name="totals",
     )(got)
 
 
-def last_kernel(pos_ref, relaxed_ref, near_ref, far_ref, out_ref, ev, od):
-    first = pos_ref[1] == 1
+def base_kernel(relaxed_ref, base_ref, mean_ref, ev, od):
     for zc in range(2):
         for c in range(3):
             w = [[relaxed_ref[c, 2 * zc + dz, k] for k in range(4)] for dz in range(2)]
             lo, hi = [(v[0] + v[1]) + (v[2] + v[3]) for v in w]
             mean = (lo + hi) * 0.125
-            diff = jnp.where(first, mean, near_ref[zc, c] + far_ref[zc, c]) - mean
+            mean_ref[zc, c] = mean
             for dz in range(2):
                 row0 = (c * 4 + 2 * zc + dz) * 16
                 for q in range(2):
-                    ev[pl.ds(row0 + q, 8, stride=2), :] = w[dz][2 * q] + diff
-                    od[pl.ds(row0 + q, 8, stride=2), :] = w[dz][2 * q + 1] + diff
+                    ev[pl.ds(row0 + q, 8, stride=2), :] = w[dz][2 * q] - mean
+                    od[pl.ds(row0 + q, 8, stride=2), :] = w[dz][2 * q + 1] - mean
     both = jnp.concatenate([ev[...], od[...]], axis=1)
     out = jnp.dot(both, lane_parity(True), precision=HI, preferred_element_type=F32)
-    out_ref[...] = out.reshape(3, 4, 16, 256)
-
-
-def sweep_last(pos, relaxed, near, far):
+    base_ref[...] = out.reshape(3, 4, 16, 256)
+
+
+def output_base(relaxed):
+    return pl.pallas_call(
+        base_kernel,
+        out_shape=(shaped(3, 4, 16, 256), shaped(2, 3, 8, 128)),
+        in_specs=[VSPEC],
+        out_specs=(VSPEC,) * 2,
+        scratch_shapes=[pltpu.VMEM((192, 128), F32)] * 2,
+        compiler_params=PARAMS,
+        cost_estimate=cost(25_000_000, 400_000),
+        name="base",
+    )(relaxed)
+
+
+def last_kernel(pos_ref, base_ref, mean_ref, near_ref, far_ref, out_ref, half_a, half_b):
+    first = pos_ref[1] == 1
+    row = lax.broadcasted_iota(jnp.int32, (128, 256), 0)
+    col = lax.broadcasted_iota(jnp.int32, (128, 256), 1)
+    widen = (col // 2 == row).astype(F32)
+    coarse = jnp.where(first, mean_ref[...], near_ref[...] + far_ref[...]).reshape(48, 128)
+    wide = jnp.dot(coarse, widen, precision=HI, preferred_element_type=F32)
+    for n in range(6):
+        for h, half in ((0, half_a), (1, half_b)):
+            piece = wide[8 * n:8 * n + 8, 128 * h:128 * h + 128]
+            for q in range(2):
+                half[pl.ds(16 * n + q, 8, stride=2), :] = piece
+    for zc in range(2):
+        for c in range(3):
+            n = 3 * zc + c
+            for h, half in ((0, half_a), (1, half_b)):
+                piece = half[16 * n:16 * n + 16, :]
+                lanes = slice(128 * h, 128 * h + 128)
+                for dz in range(2):
+                    out_ref[c, 2 * zc + dz, :, lanes] = base_ref[c, 2 * zc + dz, :, lanes] + piece
+
+
+def sweep_last(pos, base, mean, near, far):
     return pl.pallas_call(
         last_kernel,
         out_shape=shaped(3, 4, 16, 256),
-        in_specs=[SSPEC] + [VSPEC] * 3,
+        in_specs=[SSPEC] + [VSPEC] * 4,
         out_specs=VSPEC,
-        scratch_shapes=[pltpu.VMEM((192, 128), F32)] * 2,
-        compiler_params=pltpu.CompilerParams(vmem_limit_bytes=GRANT),
+        scratch_shapes=[pltpu.VMEM((96, 128), F32)] * 2,
+        compiler_params=PARAMS,
         cost_estimate=cost(2_000_000, 500_000),
         name="last",
-    )(pos, relaxed, near, far)
+    )(pos, base, mean, near, far)
 
 
 def moved(block, by_t, by_z):
@@ -450,11 +516,14 @@
         around.append(moved(after, 1, by))
     speed = lax.all_to_all(share, "gz", 0, 0, tiled=True)
     relaxed, state = fine2(pos, velocity_ext, start, *around)
-    coefs = sweep_coefs(speed.reshape(2 * slabs, 3, 8, 128))
-    for distance in (1, 2, 4, 8):
+    base, mean = output_base(relaxed)
+    speed = speed.reshape(2 * slabs, 3, 8, 128)
+    coefs = sweep_coefs(speed)
+    state = first_round(pos, speed, moved(state, 1, 0), moved(state, 2, 0))
+    for distance in (2, 4, 8):
         state = sweep_round(distance, distance - 1, distance == 8, pos, coefs, state, moved(state, distance, 0))
     near, far = totals(lax.all_to_all(state, "gz", 0, 0, tiled=True))
-    out = sweep_last(pos, relaxed, moved(near, 1, 0), moved(far, 17, 0))
+    out = sweep_last(pos, base, mean, near, moved(far, 16, 0))
     return out[None]
 
 

time: 146 us -> 154 us (1.055)
  starting transfers between devices: 70.3 us -> 74.7 us
  blocking collectives: 28.4 us -> 31.1 us
    ppermute x11, starting transfers between devices: 63.2 us -> 66 us  [moved(): return lax.ppermute(block, ('tm', 'gz'), route)]
    all_to_all x1, blocking collectives: 28.4 us -> 31.1 us  [local(): near, far = totals(lax.all_to_all(state, 'gz', 0, 0, tiled=True))]
    pallas_call x4 -> x3, Pallas kernels: 15.8 us -> 14.9 us  [sweep_round(): pl.pallas_call(functools.partial(final_kernel if final else round_kernel,...]
  transfers between devices with their start and end apart: 12 -> 12, of which waited for: 8 -> 9; matrix products, arithmetic and copies ran while one was open for 0% -> 0% of each run, Pallas kernels for 3% -> 3%
where the time goes in v5:
time: 154 us; the launch traced here: 153 us
  starting transfers between devices  74.7 us (49%)
  blocking collectives  31.1 us (20%)
  Pallas kernels  25.4 us (16%)
  waiting for transfers between devices  20 us (13%)
  local copies, waits for them, and re-layouts  1.85 us (1%)
    ppermute x11, starting transfers between devices, moved(): return lax.ppermute(block, ('tm', 'gz'), route)  66 us
    all_to_all x1, blocking collectives, local(): near, far = totals(lax.all_to_all(state, 'gz', 0, 0, tiled=True))  31.1 us
    ppermute x11, waiting for transfers between devices, moved(): return lax.ppermute(block, ('tm', 'gz'), route)  20 us
    pallas_call x3, Pallas kernels, sweep_round(): pl.pallas_call(functools.partial(final_kernel if final else round_kernel,...  14.9 us
    all_to_all x1, starting transfers between devices, local(): speed = lax.all_to_all(share, 'gz', 0, 0, tiled=True)  8.7 us
  transfers between devices with their start and end apart: 12, of which 9 were waited for; matrix products, arithmetic and copies ran while one was open for 0% of the time, Pallas kernels for 3%

profile of v5, /device:TPU:8, one launch (start us, length us, event | category | flops | bytes accessed | tf_op | source)
XLA Modules:
  0.0 153.3 jit_solution(12656181470334826614)
XLA Ops:
  0.0 0.0 copy-start
  0.0 0.9 copy-done
  0.9 0.0 copy-start.1
  0.9 0.9 copy-done.1
  1.9 0.5 split.1.own_ref
  2.4 3.5 %collective-permute-start = (f32[6,4,4,8,128]{4,3,2,1,0:T(8,128)S(1)}, f32[6,4,4,8,128]{4,3,2,1,0:T(8,128)S(1)}, u32[]{:S(2)}, u32[]{:S(2)}) collective-permute-start(f32[6,4,4,8,128]{4,3,2,1,0:T(8,128)S(1)} %split.1.own_ref), channel_id=1, source_target_pairs={{0,1},{1,2},{2,3},{3,4},{4,5},{5,6},{6,7},{7,8},{8,9},{9,10},{10,1... | collective-permute-start | bytes 1179656 | tf_op jit(solution)/shard_map/ppermute | solution.py:503
  5.9 5.5 %collective-permute-start.1 = (f32[6,4,4,8,128]{4,3,2,1,0:T(8,128)S(1)}, f32[6,4,4,8,128]{4,3,2,1,0:T(8,128)S(1)}, u32[]{:S(2)}, u32[]{:S(2)}) collective-permute-start(f32[6,4,4,8,128]{4,3,2,1,0:T(8,128)S(1)} %split.1.own_ref), channel_id=1, source_target_pairs={{1,0},{2,1},{3,2},{4,3},{5,4},{6,5},{7,6},{8,7},{9,8},{10,9},{11,1... | collective-permute-start | bytes 1179656 | tf_op jit(solution)/shard_map/ppermute | solution.py:503
  11.4 0.1 pad_add_fusion.pos_ref
  11.5 3.7 %collective-permute-done.m1_ref = f32[6,4,4,8,128]{4,3,2,1,0:T(8,128)S(1)} collective-permute-done((f32[6,4,4,8,128]{4,3,2,1,0:T(8,128)S(1)}, f32[6,4,4,8,128]{4,3,2,1,0:T(8,128)S(1)}, u32[]{:S(2)}, u32[]{:S(2)}) %collective-permute-start) | collective-permute-done | bytes 393248 | tf_op jit(solution)/shard_map/ppermute | solution.py:503
  15.2 3.1 %collective-permute-done.1.p1_ref = f32[6,4,4,8,128]{4,3,2,1,0:T(8,128)S(1)} collective-permute-done((f32[6,4,4,8,128]{4,3,2,1,0:T(8,128)S(1)}, f32[6,4,4,8,128]{4,3,2,1,0:T(8,128)S(1)}, u32[]{:S(2)}, u32[]{:S(2)}) %collective-permute-start.1) | collective-permute-done | bytes 393248 | tf_op jit(solution)/shard_map/ppermute | solution.py:503
  18.4 3.0 %fine1.1 = (f32[3,12,4,8,128]{4,3,2,1,0:T(8,128)S(1)}, f32[3,4,4,8,128]{4,3,2,1,0:T(8,128)S(1)}, f32[3,12,4,8,128]{4,3,2,1,0:T(8,128)S(1)}, f32[16,2,3,8,128]{4,3,2,1,0:T(8,128)}) custom-call(s32[3]{0:T(128)S(1)} %pad_add_fusion.pos_ref, f32[6,4,4,8,128]{4,3,2,1,0:T(8,128)S(1)} %collective-permute-done.m1_ref, f32[6,4,4,8,128]{4,3,2,1,0:T(8,128)S(1)} %split.1.own_ref, ...), custom_call_target="tpu_custom_call" | custom-call | flops 10000000 | bytes 6000000 | tf_op jit(solution)/shard_map/fine1/pallas_call | solution.py:211
  21.4 8.7 %all-to-all-start = ((f32[16,2,3,8,128]{4,3,2,1,0:T(8,128)}), f32[16,2,3,8,128]{4,3,2,1,0:T(8,128)S(1)}, u32[]{:S(2)}, u32[]{:S(2)}) async-start(f32[16,2,3,8,128]{4,3,2,1,0:T(8,128)} %get-tuple-element.21), calls=%async_computation | async-start | bytes 786432 | tf_op jit(solution)/shard_map/all_to_all | solution.py:517
  30.1 1.3 collective-permute-start.2
  31.4 6.3 %collective-permute-start.3 = (f32[3,4,4,8,128]{4,3,2,1,0:T(8,128)S(1)}, f32[3,4,4,8,128]{4,3,2,1,0:T(8,128)S(1)}, u32[]{:S(2)}, u32[]{:S(2)}) collective-permute-start(f32[3,4,4,8,128]{4,3,2,1,0:T(8,128)S(1)} %get-tuple-element.17), channel_id=1, source_target_pairs={{0,16},{1,17},{2,18},{3,19},{4,20},{5,21},{6,22},{7,23},{8,24},{9,... | collective-permute-start | bytes 589832 | tf_op jit(solution)/shard_map/ppermute | solution.py:503
  37.7 2.1 %collective-permute-start.4 = (f32[3,4,4,8,128]{4,3,2,1,0:T(8,128)S(1)}, f32[3,4,4,8,128]{4,3,2,1,0:T(8,128)S(1)}, u32[]{:S(2)}, u32[]{:S(2)}) collective-permute-start(f32[3,4,4,8,128]{4,3,2,1,0:T(8,128)S(1)} %get-tuple-element.17), channel_id=1, source_target_pairs={{1,16},{2,17},{3,18},{4,19},{5,20},{6,21},{7,22},{8,23},{9,24},{10... | collective-permute-start | bytes 589832 | tf_op jit(solution)/shard_map/ppermute | solution.py:503
  39.8 1.4 collective-permute-done.2.m1_ref
  41.2 0.0 collective-permute-done.3.own_ref
  41.2 2.0 %collective-permute-done.4.p1_ref = f32[3,4,4,8,128]{4,3,2,1,0:T(8,128)S(1)} collective-permute-done((f32[3,4,4,8,128]{4,3,2,1,0:T(8,128)S(1)}, f32[3,4,4,8,128]{4,3,2,1,0:T(8,128)S(1)}, u32[]{:S(2)}, u32[]{:S(2)}) %collective-permute-start.4) | collective-permute-done | bytes 196640 | tf_op jit(solution)/shard_map/ppermute | solution.py:503
  43.2 3.0 %fine2.1 = (f32[3,4,4,8,128]{4,3,2,1,0:T(8,128)S(1)}, f32[2,3,8,128]{3,2,1,0:T(8,128)S(1)}) custom-call(s32[3]{0:T(128)S(1)} %pad_add_fusion.pos_ref, f32[3,12,4,8,128]{4,3,2,1,0:T(8,128)S(1)} %get-tuple-element.15.speed, f32[3,12,4,8,128]{4,3,2,1,0:T(8,128)S(1)} %get-tuple-element.16.start_ref, f32[3,4,4,8,128]{4,3,2,1,0:T(8,128)S(1)} %collective-permute-done.2.m1_ref, ...), custom_call_target="tpu_custom_call" | custom-call | flops 10000000 | bytes 6000000 | tf_op jit(solution)/shard_map/fine2/pallas_call | solution.py:258
  46.2 3.8 %collective-permute-start.5 = (f32[2,3,8,128]{3,2,1,0:T(8,128)S(1)}, f32[2,3,8,128]{3,2,1,0:T(8,128)S(1)}, u32[]{:S(2)}, u32[]{:S(2)}) collective-permute-start(f32[2,3,8,128]{3,2,1,0:T(8,128)S(1)} %get-tuple-element.22), channel_id=1, source_target_pairs={{0,16},{1,17},{2,18},{3,19},{4,20},{5,21},{6,22},{7,23},{8,24},{9,... | collective-permute-start | bytes 73736 | tf_op jit(solution)/shard_map/ppermute | solution.py:503
  50.0 6.7 %collective-permute-start.6 = (f32[2,3,8,128]{3,2,1,0:T(8,128)S(1)}, f32[2,3,8,128]{3,2,1,0:T(8,128)S(1)}, u32[]{:S(2)}, u32[]{:S(2)}) collective-permute-start(f32[2,3,8,128]{3,2,1,0:T(8,128)S(1)} %get-tuple-element.22), channel_id=1, source_target_pairs={{0,32},{1,33},{2,34},{3,35},{4,36},{5,37},{6,38},{7,39},{8,40},{9,... | collective-permute-start | bytes 73736 | tf_op jit(solution)/shard_map/ppermute | solution.py:503
  56.7 0.0 collective-permute-done.5.near_ref
  56.7 1.5 collective-permute-done.6.far_ref
  58.2 0.0 all-to-all-done
  58.2 0.7 round1.1.own_ref
  58.9 5.7 %collective-permute-start.7 = (f32[4,3,8,128]{3,2,1,0:T(8,128)S(1)}, f32[4,3,8,128]{3,2,1,0:T(8,128)S(1)}, u32[]{:S(2)}, u32[]{:S(2)}) collective-permute-start(f32[4,3,8,128]{3,2,1,0:T(8,128)S(1)} %round1.1.own_ref), channel_id=1, source_target_pairs={{0,32},{1,33},{2,34},{3,35},{4,36},{5,37},{6,38},{7,39},{8,40},{9,... | collective-permute-start | bytes 147464 | tf_op jit(solution)/shard_map/ppermute | solution.py:503
  64.6 1.4 coefs.1
  66.0 0.4 collective-permute-done.7.got_ref
  66.3 1.0 shard_map.28.own_ref
  67.3 8.4 %collective-permute-start.8 = (f32[8,3,8,128]{3,2,1,0:T(8,128)S(1)}, f32[8,3,8,128]{3,2,1,0:T(8,128)S(1)}, u32[]{:S(2)}, u32[]{:S(2)}) collective-permute-start(f32[8,3,8,128]{3,2,1,0:T(8,128)S(1)} %shard_map.28.own_ref), channel_id=1, source_target_pairs={{0,64},{1,65},{2,66},{3,67},{4,68},{5,69},{6,70},{7,71},{8,72},{9,... | collective-permute-start | bytes 294920 | tf_op jit(solution)/shard_map/ppermute | solution.py:503
  75.8 2.2 %collective-permute-done.8.got_ref = f32[8,3,8,128]{3,2,1,0:T(8,128)S(1)} collective-permute-done((f32[8,3,8,128]{3,2,1,0:T(8,128)S(1)}, f32[8,3,8,128]{3,2,1,0:T(8,128)S(1)}, u32[]{:S(2)}, u32[]{:S(2)}) %collective-permute-start.8) | collective-permute-done | bytes 98336 | tf_op jit(solution)/shard_map/ppermute | solution.py:503
  78.0 1.7 %shard_map.29.own_ref = f32[16,3,8,128]{3,2,1,0:T(8,128)S(1)} custom-call(s32[3]{0:T(128)S(1)} %pad_add_fusion.pos_ref, f32[32,15,8,128]{3,2,1,0:T(8,128)S(1)} %coefs.1, f32[8,3,8,128]{3,2,1,0:T(8,128)S(1)} %shard_map.28.own_ref, f32[8,3,8,128]{3,2,1,0:T(8,128)S(1)} %collective-permute-done.8.got_ref), custom_call_target="tpu_custom_call" | custom-call | flops 8000000 | bytes 3000000 | tf_op jit(solution)/shard_map/pallas_call | solution.py:398
  79.7 6.5 %collective-permute-start.9 = (f32[16,3,8,128]{3,2,1,0:T(8,128)S(1)}, f32[16,3,8,128]{3,2,1,0:T(8,128)S(1)}, u32[]{:S(2)}, u32[]{:S(2)}) collective-permute-start(f32[16,3,8,128]{3,2,1,0:T(8,128)S(1)} %shard_map.29.own_ref), channel_id=1, source_target_pairs={{0,128},{1,129},{2,130},{3,131},{4,132},{5,133},{6,134},{7,135},{8... | collective-permute-start | bytes 589832 | tf_op jit(solution)/shard_map/ppermute | solution.py:503
  86.3 4.6 %collective-permute-done.9.got_ref = f32[16,3,8,128]{3,2,1,0:T(8,128)S(1)} collective-permute-done((f32[16,3,8,128]{3,2,1,0:T(8,128)S(1)}, f32[16,3,8,128]{3,2,1,0:T(8,128)S(1)}, u32[]{:S(2)}, u32[]{:S(2)}) %collective-permute-start.9) | collective-permute-done | bytes 196640 | tf_op jit(solution)/shard_map/ppermute | solution.py:503
  90.9 12.2 %shard_map.30 = f32[16,2,2,3,8,128]{5,4,3,2,1,0:T(8,128)S(1)} custom-call(s32[3]{0:T(128)S(1)} %pad_add_fusion.pos_ref, f32[32,15,8,128]{3,2,1,0:T(8,128)S(1)} %coefs.1, f32[16,3,8,128]{3,2,1,0:T(8,128)S(1)} %shard_map.29.own_ref, f32[16,3,8,128]{3,2,1,0:T(8,128)S(1)} %collective-permute-done.9.got_ref), custom_call_target="tpu_custom_call" | custom-call | flops 48000000 | bytes 3000000 | tf_op jit(solution)/shard_map/pallas_call | solution.py:398
  103.0 31.1 %all_to_all.10.got_ref = f32[16,2,2,3,8,128]{5,4,3,2,1,0:T(8,128)S(1)} all-to-all(f32[16,2,2,3,8,128]{5,4,3,2,1,0:T(8,128)S(1)} %shard_map.30), channel_id=1, replica_groups=mesh['tm'=32,'gz'=16] {'gz'}, dimensions={0} | all-to-all | bytes 1572864 | tf_op jit(solution)/shard_map/all_to_all | solution.py:525
  134.2 16.2 %collective-permute-start.10 = (f32[2,3,8,128]{3,2,1,0:T(8,128)S(1)}, f32[2,3,8,128]{3,2,1,0:T(8,128)S(1)}, u32[]{:S(2)}, u32[]{:S(2)}) collective-permute-start(f32[2,3,8,128]{3,2,1,0:T(8,128)S(1)} %get-tuple-element.24), channel_id=1, source_target_pairs={{0,256},{1,257},{2,258},{3,259},{4,260},{5,261},{6,262},{7,263},{8... | collective-permute-start | bytes 73736 | tf_op jit(solution)/shard_map/ppermute | solution.py:503
  150.4 0.4 base.1
  150.8 1.1 collective-permute-done.10.far_ref
  151.9 1.4 last.1
  (1 shorter events, 0.0 us)
Async XLA Ops:
  0.0 0.9 copy-start
  0.9 0.9 copy-start.1
  2.4 12.8 %collective-permute-start = (f32[6,4,4,8,128]{4,3,2,1,0:T(8,128)S(1)}, f32[6,4,4,8,128]{4,3,2,1,0:T(8,128)S(1)}, u32[]{:S(2)}, u32[]{:S(2)}) collective-permute-start(f32[6,4,4,8,128]{4,3,2,1,0:T(8,128)S(1)} %split.1.own_ref), channel_id=1, source_target_pairs={{0,1},{1,2},{2,3},{3,4},{4,5},{5,6},{6,7},{7,8},{8,9},{9,10},{10,1... | collective-permute-start | bytes 1179656 | tf_op jit(solution)/shard_map/ppermute | solution.py:503
  5.9 12.5 %collective-permute-start.1 = (f32[6,4,4,8,128]{4,3,2,1,0:T(8,128)S(1)}, f32[6,4,4,8,128]{4,3,2,1,0:T(8,128)S(1)}, u32[]{:S(2)}, u32[]{:S(2)}) collective-permute-start(f32[6,4,4,8,128]{4,3,2,1,0:T(8,128)S(1)} %split.1.own_ref), channel_id=1, source_target_pairs={{1,0},{2,1},{3,2},{4,3},{5,4},{6,5},{7,6},{8,7},{9,8},{10,9},{11,1... | collective-permute-start | bytes 1179656 | tf_op jit(solution)/shard_map/ppermute | solution.py:503
  21.4 36.8 %all-to-all-start = ((f32[16,2,3,8,128]{4,3,2,1,0:T(8,128)}), f32[16,2,3,8,128]{4,3,2,1,0:T(8,128)S(1)}, u32[]{:S(2)}, u32[]{:S(2)}) async-start(f32[16,2,3,8,128]{4,3,2,1,0:T(8,128)} %get-tuple-element.21), calls=%async_computation | async-start | bytes 786432 | tf_op jit(solution)/shard_map/all_to_all | solution.py:517
  30.1 11.1 %collective-permute-start.2 = (f32[3,4,4,8,128]{4,3,2,1,0:T(8,128)S(1)}, f32[3,4,4,8,128]{4,3,2,1,0:T(8,128)S(1)}, u32[]{:S(2)}, u32[]{:S(2)}) collective-permute-start(f32[3,4,4,8,128]{4,3,2,1,0:T(8,128)S(1)} %get-tuple-element.17), channel_id=1, source_target_pairs={{0,17},{1,18},{2,19},{3,20},{4,21},{5,22},{6,23},{7,24},{8,25},{9,... | collective-permute-start | bytes 589832 | tf_op jit(solution)/shard_map/ppermute | solution.py:503
  31.4 9.8 %collective-permute-start.3 = (f32[3,4,4,8,128]{4,3,2,1,0:T(8,128)S(1)}, f32[3,4,4,8,128]{4,3,2,1,0:T(8,128)S(1)}, u32[]{:S(2)}, u32[]{:S(2)}) collective-permute-start(f32[3,4,4,8,128]{4,3,2,1,0:T(8,128)S(1)} %get-tuple-element.17), channel_id=1, source_target_pairs={{0,16},{1,17},{2,18},{3,19},{4,20},{5,21},{6,22},{7,23},{8,24},{9,... | collective-permute-start | bytes 589832 | tf_op jit(solution)/shard_map/ppermute | solution.py:503
  37.7 5.5 %collective-permute-start.4 = (f32[3,4,4,8,128]{4,3,2,1,0:T(8,128)S(1)}, f32[3,4,4,8,128]{4,3,2,1,0:T(8,128)S(1)}, u32[]{:S(2)}, u32[]{:S(2)}) collective-permute-start(f32[3,4,4,8,128]{4,3,2,1,0:T(8,128)S(1)} %get-tuple-element.17), channel_id=1, source_target_pairs={{1,16},{2,17},{3,18},{4,19},{5,20},{6,21},{7,22},{8,23},{9,24},{10... | collective-permute-start | bytes 589832 | tf_op jit(solution)/shard_map/ppermute | solution.py:503
  46.2 10.5 %collective-permute-start.5 = (f32[2,3,8,128]{3,2,1,0:T(8,128)S(1)}, f32[2,3,8,128]{3,2,1,0:T(8,128)S(1)}, u32[]{:S(2)}, u32[]{:S(2)}) collective-permute-start(f32[2,3,8,128]{3,2,1,0:T(8,128)S(1)} %get-tuple-element.22), channel_id=1, source_target_pairs={{0,16},{1,17},{2,18},{3,19},{4,20},{5,21},{6,22},{7,23},{8,24},{9,... | collective-permute-start | bytes 73736 | tf_op jit(solution)/shard_map/ppermute | solution.py:503
  50.0 8.2 %collective-permute-start.6 = (f32[2,3,8,128]{3,2,1,0:T(8,128)S(1)}, f32[2,3,8,128]{3,2,1,0:T(8,128)S(1)}, u32[]{:S(2)}, u32[]{:S(2)}) collective-permute-start(f32[2,3,8,128]{3,2,1,0:T(8,128)S(1)} %get-tuple-element.22), channel_id=1, source_target_pairs={{0,32},{1,33},{2,34},{3,35},{4,36},{5,37},{6,38},{7,39},{8,40},{9,... | collective-permute-start | bytes 73736 | tf_op jit(solution)/shard_map/ppermute | solution.py:503
  58.9 7.5 %collective-permute-start.7 = (f32[4,3,8,128]{3,2,1,0:T(8,128)S(1)}, f32[4,3,8,128]{3,2,1,0:T(8,128)S(1)}, u32[]{:S(2)}, u32[]{:S(2)}) collective-permute-start(f32[4,3,8,128]{3,2,1,0:T(8,128)S(1)} %round1.1.own_ref), channel_id=1, source_target_pairs={{0,32},{1,33},{2,34},{3,35},{4,36},{5,37},{6,38},{7,39},{8,40},{9,... | collective-permute-start | bytes 147464 | tf_op jit(solution)/shard_map/ppermute | solution.py:503
  67.3 10.6 %collective-permute-start.8 = (f32[8,3,8,128]{3,2,1,0:T(8,128)S(1)}, f32[8,3,8,128]{3,2,1,0:T(8,128)S(1)}, u32[]{:S(2)}, u32[]{:S(2)}) collective-permute-start(f32[8,3,8,128]{3,2,1,0:T(8,128)S(1)} %shard_map.28.own_ref), channel_id=1, source_target_pairs={{0,64},{1,65},{2,66},{3,67},{4,68},{5,69},{6,70},{7,71},{8,72},{9,... | collective-permute-start | bytes 294920 | tf_op jit(solution)/shard_map/ppermute | solution.py:503
  79.7 11.2 %collective-permute-start.9 = (f32[16,3,8,128]{3,2,1,0:T(8,128)S(1)}, f32[16,3,8,128]{3,2,1,0:T(8,128)S(1)}, u32[]{:S(2)}, u32[]{:S(2)}) collective-permute-start(f32[16,3,8,128]{3,2,1,0:T(8,128)S(1)} %shard_map.29.own_ref), channel_id=1, source_target_pairs={{0,128},{1,129},{2,130},{3,131},{4,132},{5,133},{6,134},{7,135},{8... | collective-permute-start | bytes 589832 | tf_op jit(solution)/shard_map/ppermute | solution.py:503
  134.2 17.7 %collective-permute-start.10 = (f32[2,3,8,128]{3,2,1,0:T(8,128)S(1)}, f32[2,3,8,128]{3,2,1,0:T(8,128)S(1)}, u32[]{:S(2)}, u32[]{:S(2)}) collective-permute-start(f32[2,3,8,128]{3,2,1,0:T(8,128)S(1)} %get-tuple-element.24), channel_id=1, source_target_pairs={{0,256},{1,257},{2,258},{3,259},{4,260},{5,261},{6,262},{7,263},{8... | collective-permute-start | bytes 73736 | tf_op jit(solution)/shard_map/ppermute | solution.py:503

commit v6 on v5

--- a/solution.py
+++ b/solution.py
@@ -10,7 +10,7 @@
 STEPS = 4
 KAPPA = 0.04
 FINE_UNROLL = 2
-FULL_CHUNK = 8
+FULL_CHUNK = 32
 F32 = jnp.float32
 HI = lax.Precision.HIGHEST
 VM = pltpu.MemorySpace.VMEM
@@ -375,56 +375,68 @@
     out_ref[inner] = out_ref[inner] + own_ref[...]
 
 
-def final_kernel(distance, halo, pos_ref, coefs, own_ref, got_ref, share_ref, state_a, state_b):
-    slab = pos_ref[0]
+def power_kernel(steps, coefs, got_ref, out_ref, state_a, state_b):
     layers = coefs.shape[0]
-    n_in, at_in = window(slab, halo, layers)
-    last, other = spread(distance, halo, slab, coefs, got_ref, state_a, state_b)
-    inner = pl.ds(at_in + 1, n_in)
-    last[inner] = last[inner] + own_ref[...]
-    share_ref[:, 0] = last[1:layers + 1].reshape(layers // 2, 2, 3, 8, 128)
+    for ref in (state_a, state_b):
+        ref[0] = jnp.zeros((3, 8, 128), F32)
+        ref[layers + 1] = jnp.zeros((3, 8, 128), F32)
+    state_a[1:layers + 1] = got_ref[...]
 
     def pair(i, carry):
-        psi_step(coefs, last, other, FULL_CHUNK, 0, layers // FULL_CHUNK)
-        psi_step(coefs, other, last, FULL_CHUNK, 0, layers // FULL_CHUNK)
+        psi_step(coefs, state_a, state_b, FULL_CHUNK, 0, layers // FULL_CHUNK)
+        psi_step(coefs, state_b, state_a, FULL_CHUNK, 0, layers // FULL_CHUNK)
         return carry
-    lax.fori_loop(0, distance, pair, 0)
-    share_ref[:, 1] = last[1:layers + 1].reshape(layers // 2, 2, 3, 8, 128)
-
-
-def sweep_round(distance, halo, final, pos, coefs, own, got):
+    lax.fori_loop(0, steps // 2, pair, 0)
+    out_ref[...] = state_a[1:layers + 1]
+
+
+def power(steps, coefs, got):
     layers = coefs.shape[0]
-    out = shaped(layers // 2, 2, 2, 3, 8, 128) if final else shaped(min(layers, 2 + 2 * (halo + distance)), 3, 8, 128)
-    return pl.pallas_call(
-        functools.partial(final_kernel if final else round_kernel, distance, halo),
-        out_shape=out,
+    return pl.pallas_call(
+        functools.partial(power_kernel, steps),
+        out_shape=shaped(layers, 3, 8, 128),
+        in_specs=[VSPEC] * 2,
+        out_specs=VSPEC,
+        scratch_shapes=[pltpu.VMEM((layers + 2, 3, 8, 128), F32)] * 2,
+        compiler_params=PARAMS,
+        cost_estimate=cost(steps * 2_000_000, 3_000_000),
+        name="power",
+    )(coefs, got)
+
+
+def sweep_round(distance, halo, pos, coefs, own, got):
+    layers = coefs.shape[0]
+    return pl.pallas_call(
+        functools.partial(round_kernel, distance, halo),
+        out_shape=shaped(min(layers, 2 + 2 * (halo + distance)), 3, 8, 128),
         in_specs=[SSPEC] + [VSPEC] * 3,
         out_specs=VSPEC,
         scratch_shapes=[pltpu.VMEM((layers + 2, 3, 8, 128), F32)] * 2,
         compiler_params=PARAMS,
-        cost_estimate=cost((3 if final else 1) * distance * 2_000_000, 3_000_000),
+        cost_estimate=cost(distance * 2_000_000, 3_000_000),
     )(pos, coefs, own, got)
 
 
-def total_kernel(got_ref, near_ref, far_ref):
+def total_kernel(got_ref, out_ref):
     for i in range(2):
         for c in range(3):
-            for part, ref in ((0, near_ref), (1, far_ref)):
-                terms = [got_ref[s, part, i, c] for s in range(got_ref.shape[0])]
-                while len(terms) > 1:
-                    terms = [a + b for a, b in zip(terms[::2], terms[1::2])] + terms[len(terms) // 2 * 2:]
-                ref[i, c] = terms[0]
-
-
-def totals(got):
+            terms = [got_ref[s, i, c] for s in range(got_ref.shape[0])]
+            while len(terms) > 1:
+                terms = [a + b for a, b in zip(terms[::2], terms[1::2])] + terms[len(terms) // 2 * 2:]
+            out_ref[i, c] = terms[0]
+
+
+def slab_total(field):
+    layers = field.shape[0]
+    got = lax.all_to_all(field.reshape(layers // 2, 2, 3, 8, 128), "gz", 0, 0, tiled=True)
     return pl.pallas_call(
         total_kernel,
-        out_shape=(shaped(2, 3, 8, 128),) * 2,
+        out_shape=shaped(2, 3, 8, 128),
         in_specs=[VSPEC],
-        out_specs=(VSPEC,) * 2,
-        compiler_params=PARAMS,
-        cost_estimate=cost(200_000, 850_000),
-        name="totals",
+        out_specs=VSPEC,
+        compiler_params=PARAMS,
+        cost_estimate=cost(100_000, 430_000),
+        name="total",
     )(got)
 
 
@@ -521,9 +533,13 @@
     coefs = sweep_coefs(speed)
     state = first_round(pos, speed, moved(state, 1, 0), moved(state, 2, 0))
     for distance in (2, 4, 8):
-        state = sweep_round(distance, distance - 1, distance == 8, pos, coefs, state, moved(state, distance, 0))
-    near, far = totals(lax.all_to_all(state, "gz", 0, 0, tiled=True))
-    out = sweep_last(pos, base, mean, near, moved(far, 16, 0))
+        state = sweep_round(distance, distance - 1, pos, coefs, state, moved(state, distance, 0))
+    near = slab_total(state)
+    state = power(16, coefs, state)
+    near, state = lax.optimization_barrier((near, state))
+    far = slab_total(state)
+    far = moved(far, 16, 0)
+    out = sweep_last(pos, base, mean, near, far)
     return out[None]
 
 

time: 154 us -> 154 us (level)
  the two profiles are of different devices: /device:TPU:8 before, /device:TPU:10 now
where the time goes in v6:
time: 154 us
  starting transfers between devices  79.4 us (52%)
  waiting for transfers between devices  29.9 us (19%)
  Pallas kernels  25.5 us (17%)
  blocking collectives  16.5 us (11%)
  local copies, waits for them, and re-layouts  1.85 us (1%)
    ppermute x11, starting transfers between devices, moved(): return lax.ppermute(block, ('tm', 'gz'), route)  63 us
    ppermute x11, waiting for transfers between devices, moved(): return lax.ppermute(block, ('tm', 'gz'), route)  23 us
    all_to_all x1, blocking collectives, slab_total(): lax.all_to_all(field.reshape(layers // 2, 2, 3, 8, 128), 'gz', 0, 0, tile...  16.5 us
    pallas_call x3, Pallas kernels, sweep_round(): pl.pallas_call(functools.partial(round_kernel, distance, halo), out_shape...  9.89 us
    all_to_all x1, starting transfers between devices, local(): speed = lax.all_to_all(share, 'gz', 0, 0, tiled=True)  8.68 us
    all_to_all x1, starting transfers between devices, slab_total(): lax.all_to_all(field.reshape(layers // 2, 2, 3, 8, 128), 'gz', 0, 0, tile...  7.76 us
    all_to_all x1, waiting for transfers between devices, slab_total(): lax.all_to_all(field.reshape(layers // 2, 2, 3, 8, 128), 'gz', 0, 0, tile...  6.95 us
    pallas_call x1, Pallas kernels, power(): pl.pallas_call(functools.partial(power_kernel, steps), out_shape=shaped(l...  5.17 us
  transfers between devices with their start and end apart: 13, of which 10 were waited for; matrix products, arithmetic and copies ran while one was open for 0% of the time, Pallas kernels for 6%

profile of v6, /device:TPU:10, one launch (start us, length us, event | category | flops | bytes accessed | tf_op | source)
XLA Modules:
  0.0 153.5 jit_solution(8778871350129496806)
XLA Ops:
  0.0 0.0 copy-start
  0.0 0.9 copy-done
  0.9 0.0 copy-start.1
  0.9 0.9 copy-done.1
  1.9 0.5 split.1.own_ref
  2.4 3.5 %collective-permute-start = (f32[6,4,4,8,128]{4,3,2,1,0:T(8,128)S(1)}, f32[6,4,4,8,128]{4,3,2,1,0:T(8,128)S(1)}, u32[]{:S(2)}, u32[]{:S(2)}) collective-permute-start(f32[6,4,4,8,128]{4,3,2,1,0:T(8,128)S(1)} %split.1.own_ref), channel_id=1, source_target_pairs={{0,1},{1,2},{2,3},{3,4},{4,5},{5,6},{6,7},{7,8},{8,9},{9,10},{10,1... | collective-permute-start | bytes 1179656 | tf_op jit(solution)/shard_map/ppermute | solution.py:515
  5.9 2.4 %collective-permute-start.1 = (f32[6,4,4,8,128]{4,3,2,1,0:T(8,128)S(1)}, f32[6,4,4,8,128]{4,3,2,1,0:T(8,128)S(1)}, u32[]{:S(2)}, u32[]{:S(2)}) collective-permute-start(f32[6,4,4,8,128]{4,3,2,1,0:T(8,128)S(1)} %split.1.own_ref), channel_id=1, source_target_pairs={{1,0},{2,1},{3,2},{4,3},{5,4},{6,5},{7,6},{8,7},{9,8},{10,9},{11,1... | collective-permute-start | bytes 1179656 | tf_op jit(solution)/shard_map/ppermute | solution.py:515
  8.3 0.1 pad_add_fusion.pos_ref
  8.3 6.8 %collective-permute-done.m1_ref = f32[6,4,4,8,128]{4,3,2,1,0:T(8,128)S(1)} collective-permute-done((f32[6,4,4,8,128]{4,3,2,1,0:T(8,128)S(1)}, f32[6,4,4,8,128]{4,3,2,1,0:T(8,128)S(1)}, u32[]{:S(2)}, u32[]{:S(2)}) %collective-permute-start) | collective-permute-done | bytes 393248 | tf_op jit(solution)/shard_map/ppermute | solution.py:515
  15.1 3.2 %collective-permute-done.1.p1_ref = f32[6,4,4,8,128]{4,3,2,1,0:T(8,128)S(1)} collective-permute-done((f32[6,4,4,8,128]{4,3,2,1,0:T(8,128)S(1)}, f32[6,4,4,8,128]{4,3,2,1,0:T(8,128)S(1)}, u32[]{:S(2)}, u32[]{:S(2)}) %collective-permute-start.1) | collective-permute-done | bytes 393248 | tf_op jit(solution)/shard_map/ppermute | solution.py:515
  18.4 3.0 %fine1.1 = (f32[3,12,4,8,128]{4,3,2,1,0:T(8,128)S(1)}, f32[3,4,4,8,128]{4,3,2,1,0:T(8,128)S(1)}, f32[3,12,4,8,128]{4,3,2,1,0:T(8,128)S(1)}, f32[16,2,3,8,128]{4,3,2,1,0:T(8,128)}) custom-call(s32[3]{0:T(128)S(1)} %pad_add_fusion.pos_ref, f32[6,4,4,8,128]{4,3,2,1,0:T(8,128)S(1)} %collective-permute-done.m1_ref, f32[6,4,4,8,128]{4,3,2,1,0:T(8,128)S(1)} %split.1.own_ref, ...), custom_call_target="tpu_custom_call" | custom-call | flops 10000000 | bytes 6000000 | tf_op jit(solution)/shard_map/fine1/pallas_call | solution.py:211
  21.4 8.7 %all-to-all-start = ((f32[16,2,3,8,128]{4,3,2,1,0:T(8,128)}), f32[16,2,3,8,128]{4,3,2,1,0:T(8,128)S(1)}, u32[]{:S(2)}, u32[]{:S(2)}) async-start(f32[16,2,3,8,128]{4,3,2,1,0:T(8,128)} %get-tuple-element.21), calls=%async_computation | async-start | bytes 786432 | tf_op jit(solution)/shard_map/all_to_all | solution.py:529
  30.1 1.3 collective-permute-start.2
  31.4 5.7 %collective-permute-start.3 = (f32[3,4,4,8,128]{4,3,2,1,0:T(8,128)S(1)}, f32[3,4,4,8,128]{4,3,2,1,0:T(8,128)S(1)}, u32[]{:S(2)}, u32[]{:S(2)}) collective-permute-start(f32[3,4,4,8,128]{4,3,2,1,0:T(8,128)S(1)} %get-tuple-element.17), channel_id=1, source_target_pairs={{0,16},{1,17},{2,18},{3,19},{4,20},{5,21},{6,22},{7,23},{8,24},{9,... | collective-permute-start | bytes 589832 | tf_op jit(solution)/shard_map/ppermute | solution.py:515
  37.0 2.1 %collective-permute-start.4 = (f32[3,4,4,8,128]{4,3,2,1,0:T(8,128)S(1)}, f32[3,4,4,8,128]{4,3,2,1,0:T(8,128)S(1)}, u32[]{:S(2)}, u32[]{:S(2)}) collective-permute-start(f32[3,4,4,8,128]{4,3,2,1,0:T(8,128)S(1)} %get-tuple-element.17), channel_id=1, source_target_pairs={{1,16},{2,17},{3,18},{4,19},{5,20},{6,21},{7,22},{8,23},{9,24},{10... | collective-permute-start | bytes 589832 | tf_op jit(solution)/shard_map/ppermute | solution.py:515
  39.1 2.3 %collective-permute-done.2.m1_ref = f32[3,4,4,8,128]{4,3,2,1,0:T(8,128)S(1)} collective-permute-done((f32[3,4,4,8,128]{4,3,2,1,0:T(8,128)S(1)}, f32[3,4,4,8,128]{4,3,2,1,0:T(8,128)S(1)}, u32[]{:S(2)}, u32[]{:S(2)}) %collective-permute-start.2) | collective-permute-done | bytes 196640 | tf_op jit(solution)/shard_map/ppermute | solution.py:515
  41.4 0.0 collective-permute-done.3.own_ref
  41.4 0.8 collective-permute-done.4.p1_ref
  42.3 3.0 %fine2.1 = (f32[3,4,4,8,128]{4,3,2,1,0:T(8,128)S(1)}, f32[2,3,8,128]{3,2,1,0:T(8,128)S(1)}) custom-call(s32[3]{0:T(128)S(1)} %pad_add_fusion.pos_ref, f32[3,12,4,8,128]{4,3,2,1,0:T(8,128)S(1)} %get-tuple-element.15.speed, f32[3,12,4,8,128]{4,3,2,1,0:T(8,128)S(1)} %get-tuple-element.16.start_ref, f32[3,4,4,8,128]{4,3,2,1,0:T(8,128)S(1)} %collective-permute-done.2.m1_ref, ...), custom_call_target="tpu_custom_call" | custom-call | flops 10000000 | bytes 6000000 | tf_op jit(solution)/shard_map/fine2/pallas_call | solution.py:258
  45.3 4.4 %collective-permute-start.5 = (f32[2,3,8,128]{3,2,1,0:T(8,128)S(1)}, f32[2,3,8,128]{3,2,1,0:T(8,128)S(1)}, u32[]{:S(2)}, u32[]{:S(2)}) collective-permute-start(f32[2,3,8,128]{3,2,1,0:T(8,128)S(1)} %get-tuple-element.22), channel_id=1, source_target_pairs={{0,16},{1,17},{2,18},{3,19},{4,20},{5,21},{6,22},{7,23},{8,24},{9,... | collective-permute-start | bytes 73736 | tf_op jit(solution)/shard_map/ppermute | solution.py:515
  49.7 6.7 %collective-permute-start.6 = (f32[2,3,8,128]{3,2,1,0:T(8,128)S(1)}, f32[2,3,8,128]{3,2,1,0:T(8,128)S(1)}, u32[]{:S(2)}, u32[]{:S(2)}) collective-permute-start(f32[2,3,8,128]{3,2,1,0:T(8,128)S(1)} %get-tuple-element.22), channel_id=1, source_target_pairs={{0,32},{1,33},{2,34},{3,35},{4,36},{5,37},{6,38},{7,39},{8,40},{9,... | collective-permute-start | bytes 73736 | tf_op jit(solution)/shard_map/ppermute | solution.py:515
  56.4 0.0 collective-permute-done.5.near_ref
  56.4 1.5 collective-permute-done.6.far_ref
  57.9 0.0 all-to-all-done
  57.9 0.7 round1.1.own_ref
  58.6 5.7 %collective-permute-start.7 = (f32[4,3,8,128]{3,2,1,0:T(8,128)S(1)}, f32[4,3,8,128]{3,2,1,0:T(8,128)S(1)}, u32[]{:S(2)}, u32[]{:S(2)}) collective-permute-start(f32[4,3,8,128]{3,2,1,0:T(8,128)S(1)} %round1.1.own_ref), channel_id=1, source_target_pairs={{0,32},{1,33},{2,34},{3,35},{4,36},{5,37},{6,38},{7,39},{8,40},{9,... | collective-permute-start | bytes 147464 | tf_op jit(solution)/shard_map/ppermute | solution.py:515
  64.3 1.4 coefs.1
  65.7 0.4 collective-permute-done.7.got_ref
  66.0 1.1 shard_map.28.own_ref
  67.2 8.4 %collective-permute-start.8 = (f32[8,3,8,128]{3,2,1,0:T(8,128)S(1)}, f32[8,3,8,128]{3,2,1,0:T(8,128)S(1)}, u32[]{:S(2)}, u32[]{:S(2)}) collective-permute-start(f32[8,3,8,128]{3,2,1,0:T(8,128)S(1)} %shard_map.28.own_ref), channel_id=1, source_target_pairs={{0,64},{1,65},{2,66},{3,67},{4,68},{5,69},{6,70},{7,71},{8,72},{9,... | collective-permute-start | bytes 294920 | tf_op jit(solution)/shard_map/ppermute | solution.py:515
  75.6 2.2 %collective-permute-done.8.got_ref = f32[8,3,8,128]{3,2,1,0:T(8,128)S(1)} collective-permute-done((f32[8,3,8,128]{3,2,1,0:T(8,128)S(1)}, f32[8,3,8,128]{3,2,1,0:T(8,128)S(1)}, u32[]{:S(2)}, u32[]{:S(2)}) %collective-permute-start.8) | collective-permute-done | bytes 98336 | tf_op jit(solution)/shard_map/ppermute | solution.py:515
  77.8 2.2 %shard_map.29.own_ref = f32[16,3,8,128]{3,2,1,0:T(8,128)S(1)} custom-call(s32[3]{0:T(128)S(1)} %pad_add_fusion.pos_ref, f32[32,15,8,128]{3,2,1,0:T(8,128)S(1)} %coefs.1, f32[8,3,8,128]{3,2,1,0:T(8,128)S(1)} %shard_map.28.own_ref, f32[8,3,8,128]{3,2,1,0:T(8,128)S(1)} %collective-permute-done.8.got_ref), custom_call_target="tpu_custom_call" | custom-call | flops 8000000 | bytes 3000000 | tf_op jit(solution)/shard_map/pallas_call | solution.py:409
  80.0 6.8 %collective-permute-start.9 = (f32[16,3,8,128]{3,2,1,0:T(8,128)S(1)}, f32[16,3,8,128]{3,2,1,0:T(8,128)S(1)}, u32[]{:S(2)}, u32[]{:S(2)}) collective-permute-start(f32[16,3,8,128]{3,2,1,0:T(8,128)S(1)} %shard_map.29.own_ref), channel_id=1, source_target_pairs={{0,128},{1,129},{2,130},{3,131},{4,132},{5,133},{6,134},{7,135},{8... | collective-permute-start | bytes 589832 | tf_op jit(solution)/shard_map/ppermute | solution.py:515
  86.8 4.6 %collective-permute-done.9.got_ref = f32[16,3,8,128]{3,2,1,0:T(8,128)S(1)} collective-permute-done((f32[16,3,8,128]{3,2,1,0:T(8,128)S(1)}, f32[16,3,8,128]{3,2,1,0:T(8,128)S(1)}, u32[]{:S(2)}, u32[]{:S(2)}) %collective-permute-start.9) | collective-permute-done | bytes 196640 | tf_op jit(solution)/shard_map/ppermute | solution.py:515
  91.4 6.6 %shard_map.30.got_ref = f32[32,3,8,128]{3,2,1,0:T(8,128)} custom-call(s32[3]{0:T(128)S(1)} %pad_add_fusion.pos_ref, f32[32,15,8,128]{3,2,1,0:T(8,128)S(1)} %coefs.1, f32[16,3,8,128]{3,2,1,0:T(8,128)S(1)} %shard_map.29.own_ref, f32[16,3,8,128]{3,2,1,0:T(8,128)S(1)} %collective-permute-done.9.got_ref), custom_call_target="tpu_custom_call" | custom-call | flops 16000000 | bytes 3000000 | tf_op jit(solution)/shard_map/pallas_call | solution.py:409
  98.0 7.8 %all-to-all-start.1 = ((f32[16,2,3,8,128]{4,3,2,1,0:T(8,128)}), f32[16,2,3,8,128]{4,3,2,1,0:T(8,128)S(1)}, u32[]{:S(2)}, u32[]{:S(2)}) async-start(f32[16,2,3,8,128]{4,3,2,1,0:T(8,128)} %bitcast.4), calls=%async_computation.1 | async-start | bytes 786432 | tf_op jit(solution)/shard_map/all_to_all | solution.py:431
  105.8 5.2 %power.1 = f32[32,3,8,128]{3,2,1,0:T(8,128)S(1)} custom-call(f32[32,15,8,128]{3,2,1,0:T(8,128)S(1)} %coefs.1, f32[32,3,8,128]{3,2,1,0:T(8,128)} %shard_map.30.got_ref), custom_call_target="tpu_custom_call" | custom-call | flops 32000000 | bytes 3000000 | tf_op jit(solution)/shard_map/power/pallas_call | solution.py:395
  111.0 7.0 %all-to-all-done.1.got_ref = f32[16,2,3,8,128]{4,3,2,1,0:T(8,128)S(1)} async-done(((f32[16,2,3,8,128]{4,3,2,1,0:T(8,128)}), f32[16,2,3,8,128]{4,3,2,1,0:T(8,128)S(1)}, u32[]{:S(2)}, u32[]{:S(2)}) %all-to-all-start.1) | async-done | bytes 393248 | tf_op jit(solution)/shard_map/all_to_all | solution.py:431
  117.9 16.5 %all_to_all.15.got_ref = f32[16,2,3,8,128]{4,3,2,1,0:T(8,128)S(1)} all-to-all(f32[16,2,3,8,128]{4,3,2,1,0:T(8,128)S(1)} %bitcast.9), channel_id=1, replica_groups=mesh['tm'=32,'gz'=16] {'gz'}, dimensions={0} | all-to-all | bytes 786432 | tf_op jit(solution)/shard_map/all_to_all | solution.py:431
  134.5 16.1 %collective-permute-start.10 = (f32[2,3,8,128]{3,2,1,0:T(8,128)S(1)}, f32[2,3,8,128]{3,2,1,0:T(8,128)S(1)}, u32[]{:S(2)}, u32[]{:S(2)}) collective-permute-start(f32[2,3,8,128]{3,2,1,0:T(8,128)S(1)} %total.3), channel_id=1, source_target_pairs={{0,256},{1,257},{2,258},{3,259},{4,260},{5,261},{6,262},{7,263},{8... | collective-permute-start | bytes 73736 | tf_op jit(solution)/shard_map/ppermute | solution.py:515
  150.6 0.4 base.1
  151.0 1.1 collective-permute-done.10.far_ref
  152.1 1.4 last.1
  (2 shorter events, 0.0 us)
Async XLA Ops:
  0.0 0.9 copy-start
  0.9 0.9 copy-start.1
  2.4 12.7 %collective-permute-start = (f32[6,4,4,8,128]{4,3,2,1,0:T(8,128)S(1)}, f32[6,4,4,8,128]{4,3,2,1,0:T(8,128)S(1)}, u32[]{:S(2)}, u32[]{:S(2)}) collective-permute-start(f32[6,4,4,8,128]{4,3,2,1,0:T(8,128)S(1)} %split.1.own_ref), channel_id=1, source_target_pairs={{0,1},{1,2},{2,3},{3,4},{4,5},{5,6},{6,7},{7,8},{8,9},{9,10},{10,1... | collective-permute-start | bytes 1179656 | tf_op jit(solution)/shard_map/ppermute | solution.py:515
  5.9 12.5 %collective-permute-start.1 = (f32[6,4,4,8,128]{4,3,2,1,0:T(8,128)S(1)}, f32[6,4,4,8,128]{4,3,2,1,0:T(8,128)S(1)}, u32[]{:S(2)}, u32[]{:S(2)}) collective-permute-start(f32[6,4,4,8,128]{4,3,2,1,0:T(8,128)S(1)} %split.1.own_ref), channel_id=1, source_target_pairs={{1,0},{2,1},{3,2},{4,3},{5,4},{6,5},{7,6},{8,7},{9,8},{10,9},{11,1... | collective-permute-start | bytes 1179656 | tf_op jit(solution)/shard_map/ppermute | solution.py:515
  21.4 36.5 %all-to-all-start = ((f32[16,2,3,8,128]{4,3,2,1,0:T(8,128)}), f32[16,2,3,8,128]{4,3,2,1,0:T(8,128)S(1)}, u32[]{:S(2)}, u32[]{:S(2)}) async-start(f32[16,2,3,8,128]{4,3,2,1,0:T(8,128)} %get-tuple-element.21), calls=%async_computation | async-start | bytes 786432 | tf_op jit(solution)/shard_map/all_to_all | solution.py:529
  30.1 11.4 %collective-permute-start.2 = (f32[3,4,4,8,128]{4,3,2,1,0:T(8,128)S(1)}, f32[3,4,4,8,128]{4,3,2,1,0:T(8,128)S(1)}, u32[]{:S(2)}, u32[]{:S(2)}) collective-permute-start(f32[3,4,4,8,128]{4,3,2,1,0:T(8,128)S(1)} %get-tuple-element.17), channel_id=1, source_target_pairs={{0,17},{1,18},{2,19},{3,20},{4,21},{5,22},{6,23},{7,24},{8,25},{9,... | collective-permute-start | bytes 589832 | tf_op jit(solution)/shard_map/ppermute | solution.py:515
  31.4 10.1 %collective-permute-start.3 = (f32[3,4,4,8,128]{4,3,2,1,0:T(8,128)S(1)}, f32[3,4,4,8,128]{4,3,2,1,0:T(8,128)S(1)}, u32[]{:S(2)}, u32[]{:S(2)}) collective-permute-start(f32[3,4,4,8,128]{4,3,2,1,0:T(8,128)S(1)} %get-tuple-element.17), channel_id=1, source_target_pairs={{0,16},{1,17},{2,18},{3,19},{4,20},{5,21},{6,22},{7,23},{8,24},{9,... | collective-permute-start | bytes 589832 | tf_op jit(solution)/shard_map/ppermute | solution.py:515
  37.0 5.3 %collective-permute-start.4 = (f32[3,4,4,8,128]{4,3,2,1,0:T(8,128)S(1)}, f32[3,4,4,8,128]{4,3,2,1,0:T(8,128)S(1)}, u32[]{:S(2)}, u32[]{:S(2)}) collective-permute-start(f32[3,4,4,8,128]{4,3,2,1,0:T(8,128)S(1)} %get-tuple-element.17), channel_id=1, source_target_pairs={{1,16},{2,17},{3,18},{4,19},{5,20},{6,21},{7,22},{8,23},{9,24},{10... | collective-permute-start | bytes 589832 | tf_op jit(solution)/shard_map/ppermute | solution.py:515
  45.3 11.1 %collective-permute-start.5 = (f32[2,3,8,128]{3,2,1,0:T(8,128)S(1)}, f32[2,3,8,128]{3,2,1,0:T(8,128)S(1)}, u32[]{:S(2)}, u32[]{:S(2)}) collective-permute-start(f32[2,3,8,128]{3,2,1,0:T(8,128)S(1)} %get-tuple-element.22), channel_id=1, source_target_pairs={{0,16},{1,17},{2,18},{3,19},{4,20},{5,21},{6,22},{7,23},{8,24},{9,... | collective-permute-start | bytes 73736 | tf_op jit(solution)/shard_map/ppermute | solution.py:515
  49.7 8.2 %collective-permute-start.6 = (f32[2,3,8,128]{3,2,1,0:T(8,128)S(1)}, f32[2,3,8,128]{3,2,1,0:T(8,128)S(1)}, u32[]{:S(2)}, u32[]{:S(2)}) collective-permute-start(f32[2,3,8,128]{3,2,1,0:T(8,128)S(1)} %get-tuple-element.22), channel_id=1, source_target_pairs={{0,32},{1,33},{2,34},{3,35},{4,36},{5,37},{6,38},{7,39},{8,40},{9,... | collective-permute-start | bytes 73736 | tf_op jit(solution)/shard_map/ppermute | solution.py:515
  58.6 7.5 %collective-permute-start.7 = (f32[4,3,8,128]{3,2,1,0:T(8,128)S(1)}, f32[4,3,8,128]{3,2,1,0:T(8,128)S(1)}, u32[]{:S(2)}, u32[]{:S(2)}) collective-permute-start(f32[4,3,8,128]{3,2,1,0:T(8,128)S(1)} %round1.1.own_ref), channel_id=1, source_target_pairs={{0,32},{1,33},{2,34},{3,35},{4,36},{5,37},{6,38},{7,39},{8,40},{9,... | collective-permute-start | bytes 147464 | tf_op jit(solution)/shard_map/ppermute | solution.py:515
  67.2 10.6 %collective-permute-start.8 = (f32[8,3,8,128]{3,2,1,0:T(8,128)S(1)}, f32[8,3,8,128]{3,2,1,0:T(8,128)S(1)}, u32[]{:S(2)}, u32[]{:S(2)}) collective-permute-start(f32[8,3,8,128]{3,2,1,0:T(8,128)S(1)} %shard_map.28.own_ref), channel_id=1, source_target_pairs={{0,64},{1,65},{2,66},{3,67},{4,68},{5,69},{6,70},{7,71},{8,72},{9,... | collective-permute-start | bytes 294920 | tf_op jit(solution)/shard_map/ppermute | solution.py:515
  80.0 11.4 %collective-permute-start.9 = (f32[16,3,8,128]{3,2,1,0:T(8,128)S(1)}, f32[16,3,8,128]{3,2,1,0:T(8,128)S(1)}, u32[]{:S(2)}, u32[]{:S(2)}) collective-permute-start(f32[16,3,8,128]{3,2,1,0:T(8,128)S(1)} %shard_map.29.own_ref), channel_id=1, source_target_pairs={{0,128},{1,129},{2,130},{3,131},{4,132},{5,133},{6,134},{7,135},{8... | collective-permute-start | bytes 589832 | tf_op jit(solution)/shard_map/ppermute | solution.py:515
  98.0 19.9 %all-to-all-start.1 = ((f32[16,2,3,8,128]{4,3,2,1,0:T(8,128)}), f32[16,2,3,8,128]{4,3,2,1,0:T(8,128)S(1)}, u32[]{:S(2)}, u32[]{:S(2)}) async-start(f32[16,2,3,8,128]{4,3,2,1,0:T(8,128)} %bitcast.4), calls=%async_computation.1 | async-start | bytes 786432 | tf_op jit(solution)/shard_map/all_to_all | solution.py:431
  134.5 17.6 %collective-permute-start.10 = (f32[2,3,8,128]{3,2,1,0:T(8,128)S(1)}, f32[2,3,8,128]{3,2,1,0:T(8,128)S(1)}, u32[]{:S(2)}, u32[]{:S(2)}) collective-permute-start(f32[2,3,8,128]{3,2,1,0:T(8,128)S(1)} %total.3), channel_id=1, source_target_pairs={{0,256},{1,257},{2,258},{3,259},{4,260},{5,261},{6,262},{7,263},{8... | collective-permute-start | bytes 73736 | tf_op jit(solution)/shard_map/ppermute | solution.py:515
